TPU v7x, 32 devices: a whole 2x2x4 slice. The times are simulated.
32 devices in a mesh: dp: 16 (over z, y, x), mp: 2 (over core).
Axes of the slice: x: 2, y: 2, z: 4, core: 2. Of those that a mesh axis runs over, the one named last changes fastest.
Arguments:
- layer_entries: bfloat16 [2, 2048, 1024], P(None, 'dp'), may hold values from -6 to 6
- loss_sensitivity: bfloat16 [2, 2048, 1024], P(None, 'dp'), may hold values from -6 to 6
- occupied_counts: int32 [2, 16], P(None, 'dp'), may hold values from 32 to 128, as said below
- earlier_normalizer_gain: float32 [1024], replicated, may hold values from 0.5 to 1.5
- inflow_logits: float32 [1024, 16], replicated, may hold values from -6 to 0
- decay_logits: float32 [1024, 16], replicated, may hold values from -4 to 2
- channel_lifting: float32 [1024, 16], replicated, may hold values from -6 to 6
- channel_collapse: float32 [1024, 16], replicated, may hold values from -3 to 3
- direct_term_weight: float32 [1024], replicated, may hold values from 0.5 to 1.5
- content_projector: bfloat16 [1024, 2048], P('dp', 'mp'), may hold values from -0.1875 to 0.1875
- content_offset: float32 [2048], P('mp'), may hold values from -1.2 to 1.2
- common_projector: bfloat16 [1024, 128], P('dp'), may hold values from -0.1875 to 0.1875
- common_offset: float32 [128], replicated, may hold values from -1.2 to 1.2
- asking_gain: float32 [128], replicated, may hold values from -12 to 12
- asking_offset: float32 [128], replicated, may hold values from -6 to 6
- lookup_gain: float32 [128], replicated, may hold values from -12 to 12
- forget_gate_matrix: bfloat16 [1024, 2048], P('dp', 'mp'), may hold values from -0.1875 to 0.1875
- forget_gate_offset: float32 [2048], P('mp'), may hold values from -1.2 to 1.2
- renewal_gate_matrix: bfloat16 [1024, 1024], P('dp'), may hold values from -0.1875 to 0.1875
- renewal_gate_offset: float32 [1024], replicated, may hold values from -1.2 to 1.2
- candidate_matrix: bfloat16 [1024, 1024], P('dp'), may hold values from -0.1875 to 0.1875
- candidate_offset: float32 [1024], replicated, may hold values from -1.2 to 1.2
- attended_projector: bfloat16 [2048, 1024], P('mp', 'dp'), may hold values from -0.5 to 0.5
- later_normalizer_gain: float32 [1024], replicated, may hold values from 0.5 to 1.5
- hidden_layer_matrix: bfloat16 [1024, 4096], P('dp', 'mp'), may hold values from -0.1875 to 0.1875
- hidden_layer_offset: float32 [4096], P('mp'), may hold values from -1.2 to 1.2
- outward_layer_matrix: bfloat16 [4096, 1024], P('mp', 'dp'), may hold values from -0.09375 to 0.09375
- outward_layer_offset: float32 [1024], replicated, may hold values from -1.2 to 1.2
Outputs:
- outputs: bfloat16 [2, 2048, 1024], P(None, 'dp')
- grad_tokens: bfloat16 [2, 2048, 1024], P(None, 'dp')
- grad_prenorm: float32 [1024], replicated
- grad_alphas: float32 [1024, 16], replicated
- grad_deltas: float32 [1024, 16], replicated
- grad_expand: float32 [1024, 16], replicated
- grad_readout: float32 [1024, 16], replicated
- grad_omegas: float32 [1024], replicated
- grad_wvalue: float32 [1024, 2048], P('dp', 'mp')
- grad_bvalue: float32 [2048], P('mp')
- grad_wshared: float32 [1024, 128], P('dp')
- grad_bshared: float32 [128], replicated
- grad_qscale: float32 [128], replicated
- grad_qshift: float32 [128], replicated
- key_scale_gradient: float32 [128], replicated
- grad_wreset: float32 [1024, 2048], P('dp', 'mp')
- grad_breset: float32 [2048], P('mp')
- grad_wupdate: float32 [1024, 1024], P('dp')
- grad_bupdate: float32 [1024], replicated
- grad_whidden: float32 [1024, 1024], P('dp')
- grad_bhidden: float32 [1024], replicated
- grad_woutput: float32 [2048, 1024], P('mp', 'dp')
- grad_postnorm: float32 [1024], replicated
- grad_wffnin: float32 [1024, 4096], P('dp', 'mp')
- grad_bffnin: float32 [4096], P('mp')
- grad_wffnout: float32 [4096, 1024], P('mp', 'dp')
- grad_bffnout: float32 [1024], replicated
Inputs may be any that keep to these rules, and one draw needn't show every extreme that they name: `occupied_counts`: a row's live tokens come first and the rest of its 128 slots are padding; some row is full.
All inputs are finite; a program needn't handle non-finite values.
Results may differ from a plain program's by a relative error of at most 0.04.
Values may be sent and summed in bfloat16 or wider, within the bound.
No kernel may reach another device: no remote copies, remote signals or barrier semaphores. Data moves between devices by JAX's collectives and lax.ppermute only.
A program may use at most 256 MiB of HBM per device.

v0:
```python
import jax
import jax.numpy as jnp
from jax import lax
from jax.sharding import PartitionSpec as P

COMMON_SPAN_DIM = 128
SPAN = 128


epsilon = 1e-05
highest = lax.Precision.HIGHEST
piece_length = 16


def product(left, right):
    return jnp.dot(left, right, preferred_element_type=jnp.float32)


def left_inner(left, right):
    return lax.dot_general(
        left, right, (((0,), (0,)), ((), ())), preferred_element_type=jnp.float32
    )


def right_inner(left, right):
    return lax.dot_general(
        left, right, (((1,), (1,)), ((), ())), preferred_element_type=jnp.float32
    )


def sigmoid_linear_slope(values):
    sigma = jax.nn.sigmoid(values)
    return sigma * (1.0 + values * (1.0 - sigma))


def layer_norm(values, gain):
    center = values - jnp.mean(values, axis=-1, keepdims=True)
    spread = jnp.mean(center * center, axis=-1, keepdims=True)
    return center * lax.rsqrt(spread + epsilon) * gain


def combine_pieces(former, latter):
    return (former[0] * latter[0], former[1] * latter[0] + latter[1])


def ema_apply(normed, inflow_logits, decay_logits, channel_lifting, channel_collapse):
    steps = normed.shape[0]
    width = normed.shape[1]
    piece_count = steps // piece_length
    rate_in = jax.nn.sigmoid(inflow_logits)
    log_keep = jnp.log(1.0 - rate_in * jax.nn.sigmoid(decay_logits))
    inflow = rate_in * channel_lifting
    lag_index = jnp.arange(piece_length).astype(jnp.float32)
    powers = jnp.exp(log_keep[None] * lag_index[:, None, None])
    kernel = jnp.sum(channel_collapse[None] * inflow[None] * powers, axis=-1)
    offsets = jnp.arange(piece_length)
    offset_gap = offsets[:, None] - offsets[None, :]
    toeplitz = jnp.where(
        (offset_gap >= 0)[:, :, None], kernel[jnp.clip(offset_gap, 0, piece_length - 1)], 0.0
    )
    pieces = normed.reshape(piece_count, piece_length, width)
    inside = jnp.einsum("tsd,bsd->btd", toeplitz, pieces, precision=highest)
    tail_power = powers[::-1] * inflow[None]
    piece_state = jnp.einsum("sdh,bsd->bdh", tail_power, pieces, precision=highest)
    full_keep = jnp.broadcast_to(jnp.exp(log_keep * piece_length)[None], piece_state.shape)
    unused, block_ends = lax.associative_scan(combine_pieces, (full_keep, piece_state))
    earlier = jnp.concatenate([jnp.zeros_like(block_ends[:1]), block_ends[:-1]], axis=0)
    carry_weight = channel_collapse[None] * powers * jnp.exp(log_keep)[None]
    carried = jnp.einsum("bdh,tdh->btd", earlier, carry_weight, precision=highest)
    return (inside + carried).reshape(steps, width)


def norm_mix(
    input_full,
    earlier_normalizer_gain,
    inflow_logits,
    decay_logits,
    channel_lifting,
    channel_collapse,
    direct_term_weight,
):
    normed = layer_norm(input_full, earlier_normalizer_gain)
    smooth = jax.nn.silu(
        ema_apply(normed, inflow_logits, decay_logits, channel_lifting, channel_collapse)
        + direct_term_weight * normed
    )
    return (normed, smooth)


def micro_step(weights, smalls, token_row, seed_row, length):
    (
        content_projector,
        common_projector,
        forget_gate_matrix,
        renewal_gate_matrix,
        candidate_matrix,
        attended_projector,
        hidden_layer_matrix,
        outward_layer_matrix,
    ) = weights
    (
        earlier_normalizer_gain,
        inflow_logits,
        decay_logits,
        channel_lifting,
        channel_collapse,
        direct_term_weight,
        content_offset,
        common_offset,
        asking_gain,
        asking_offset,
        lookup_gain,
        forget_gate_offset,
        renewal_gate_offset,
        candidate_offset,
        later_normalizer_gain,
        hidden_layer_offset,
        outward_layer_offset,
    ) = smalls
    steps = token_row.shape[0]
    live_flag = jnp.arange(steps) < length
    live = live_flag.astype(jnp.float32)
    input_full = token_row.astype(jnp.float32)
    (normed, smooth), mix_back = jax.vjp(
        norm_mix,
        input_full,
        earlier_normalizer_gain,
        inflow_logits,
        decay_logits,
        channel_lifting,
        channel_collapse,
        direct_term_weight,
    )
    norm_low = normed.astype(jnp.bfloat16)
    smooth_low = smooth.astype(jnp.bfloat16)
    value_pre = product(norm_low, content_projector) + content_offset
    value_low = jax.nn.silu(value_pre).astype(jnp.bfloat16)
    common_linear_sum = product(smooth_low, common_projector) + common_offset
    common_embedding = jax.nn.silu(common_linear_sum)
    query_low = (common_embedding * asking_gain + asking_offset).astype(jnp.bfloat16)
    lookup_lowbit = (common_embedding * lookup_gain).astype(jnp.bfloat16)
    reset_pre = product(smooth_low, forget_gate_matrix) + forget_gate_offset
    reset = jax.nn.silu(reset_pre)
    update = jax.nn.sigmoid(product(smooth_low, renewal_gate_matrix) + renewal_gate_offset)
    hidden_in = product(smooth_low, candidate_matrix) + candidate_offset
    blocks = steps // SPAN
    query_blocks = query_low.reshape(blocks, SPAN, -1)
    key_blocks = lookup_lowbit.reshape(blocks, SPAN, -1)
    value_blocks = value_low.reshape(blocks, SPAN, -1)
    position = jnp.arange(SPAN)
    causal = position[None, :] <= position[:, None]
    diagonal = position[None, :] == position[:, None]
    live_blocks = live_flag.reshape(blocks, SPAN)
    allowed = causal[None] & (live_blocks[:, None, :] | diagonal[None])
    raw_scores = jnp.einsum(
        "ctz,csz->cts", query_blocks, key_blocks, preferred_element_type=jnp.float32
    ) * COMMON_SPAN_DIM ** (-0.5)
    scores = jnp.where(allowed, raw_scores, -1e30)
    probs = jax.nn.softmax(scores, axis=-1)
    probs_low = probs.astype(jnp.bfloat16)
    attended = jnp.einsum(
        "cts,csv->ctv", probs_low, value_blocks, preferred_element_type=jnp.float32
    ).reshape(steps, -1)
    mixed = (reset * attended).astype(jnp.bfloat16)
    hidden_pre = hidden_in + lax.psum(product(mixed, attended_projector), "mp")
    hidden = jax.nn.silu(hidden_pre)
    blended = input_full + update * (hidden - input_full)
    ffn_norm, post_back = jax.vjp(layer_norm, blended, later_normalizer_gain)
    ffn_low = ffn_norm.astype(jnp.bfloat16)
    ffn_pre = product(ffn_low, hidden_layer_matrix) + hidden_layer_offset
    ffn_act = jax.nn.silu(ffn_pre).astype(jnp.bfloat16)
    down_part = product(ffn_act, outward_layer_matrix)
    down_full = lax.psum(down_part.astype(jnp.bfloat16), "mp").astype(jnp.float32)
    out_row = (live[:, None] * (blended + down_full + outward_layer_offset)).astype(jnp.bfloat16)
    seed = live[:, None] * seed_row.astype(jnp.float32)
    seed_low = seed.astype(jnp.bfloat16)
    grad_bffnout = jnp.sum(seed, axis=0)
    grad_wffnout = left_inner(ffn_act, seed_low)
    grad_ffn_pre = (
        right_inner(seed_low, outward_layer_matrix) * sigmoid_linear_slope(ffn_pre)
    ).astype(jnp.bfloat16)
    grad_bffnin = jnp.sum(grad_ffn_pre.astype(jnp.float32), axis=0)
    grad_wffnin = left_inner(ffn_low, grad_ffn_pre)
    grad_ffn_norm = lax.psum(right_inner(grad_ffn_pre, hidden_layer_matrix), "mp")
    grad_blend_norm, grad_postnorm = post_back(grad_ffn_norm)
    grad_blended = seed + grad_blend_norm
    grad_update = grad_blended * (hidden - input_full)
    grad_input = grad_blended * (1.0 - update)
    grad_hidden_pre = (grad_blended * update * sigmoid_linear_slope(hidden_pre)).astype(
        jnp.bfloat16
    )
    grad_update_pre = (grad_update * update * (1.0 - update)).astype(jnp.bfloat16)
    grad_bhidden = jnp.sum(grad_hidden_pre.astype(jnp.float32), axis=0)
    grad_whidden = left_inner(smooth_low, grad_hidden_pre)
    grad_woutput = left_inner(mixed, grad_hidden_pre)
    grad_bupdate = jnp.sum(grad_update_pre.astype(jnp.float32), axis=0)
    grad_wupdate = left_inner(smooth_low, grad_update_pre)
    grad_mixed = right_inner(grad_hidden_pre, attended_projector)
    grad_attended = (grad_mixed * reset).astype(jnp.bfloat16)
    grad_reset_pre = (grad_mixed * attended * sigmoid_linear_slope(reset_pre)).astype(jnp.bfloat16)
    grad_att_blocks = grad_attended.reshape(blocks, SPAN, -1)
    probs_part = jnp.einsum(
        "ctv,csv->cts", grad_att_blocks, value_blocks, preferred_element_type=jnp.float32
    )
    grad_probs = lax.psum(probs_part, "mp")
    grad_value = jnp.einsum(
        "cts,ctv->csv", probs_low, grad_att_blocks, preferred_element_type=jnp.float32
    ).reshape(steps, -1)
    grad_scores = (
        probs * (grad_probs - jnp.sum(grad_probs * probs, axis=-1, keepdims=True))
    ).astype(jnp.bfloat16)
    asking_sensitivity = (
        jnp.einsum("cts,csz->ctz", grad_scores, key_blocks, preferred_element_type=jnp.float32)
        * COMMON_SPAN_DIM ** (-0.5)
    ).reshape(steps, -1)
    lookup_sensitivity = (
        jnp.einsum("cts,ctz->csz", grad_scores, query_blocks, preferred_element_type=jnp.float32)
        * COMMON_SPAN_DIM ** (-0.5)
    ).reshape(steps, -1)
    grad_qscale = jnp.sum(asking_sensitivity * common_embedding, axis=0)
    grad_qshift = jnp.sum(asking_sensitivity, axis=0)
    key_scale_gradient = jnp.sum(lookup_sensitivity * common_embedding, axis=0)
    shared_input_gradient = (
        (asking_sensitivity * asking_gain + lookup_sensitivity * lookup_gain)
        * sigmoid_linear_slope(common_linear_sum)
    ).astype(jnp.bfloat16)
    grad_value_pre = (grad_value * sigmoid_linear_slope(value_pre)).astype(jnp.bfloat16)
    grad_bshared = jnp.sum(shared_input_gradient.astype(jnp.float32), axis=0)
    grad_breset = jnp.sum(grad_reset_pre.astype(jnp.float32), axis=0)
    grad_bvalue = jnp.sum(grad_value_pre.astype(jnp.float32), axis=0)
    grad_wshared = left_inner(smooth_low, shared_input_gradient)
    grad_wreset = left_inner(smooth_low, grad_reset_pre)
    grad_wvalue = left_inner(norm_low, grad_value_pre)
    reset_part = right_inner(grad_reset_pre, forget_gate_matrix)
    value_part = right_inner(grad_value_pre, content_projector)
    smooth_sum, norm_sum = (
        lax.psum(reset_part.astype(jnp.bfloat16), "mp").astype(jnp.float32),
        lax.psum(value_part.astype(jnp.bfloat16), "mp").astype(jnp.float32),
    )
    grad_smooth = (
        smooth_sum
        + right_inner(shared_input_gradient, common_projector)
        + right_inner(grad_update_pre, renewal_gate_matrix)
        + right_inner(grad_hidden_pre, candidate_matrix)
    )
    grad_in_norm, grad_prenorm, grad_alphas, grad_deltas, grad_expand, grad_readout, grad_omegas = (
        mix_back((norm_sum, grad_smooth))
    )
    grad_row = (grad_input + grad_in_norm).astype(jnp.bfloat16)
    big_grads = (
        grad_wvalue,
        grad_wshared,
        grad_wreset,
        grad_wupdate,
        grad_whidden,
        grad_woutput,
        grad_wffnin,
        grad_wffnout,
    )
    small_grads = (
        grad_prenorm,
        grad_alphas,
        grad_deltas,
        grad_expand,
        grad_readout,
        grad_omegas,
        grad_bvalue,
        grad_bshared,
        grad_qscale,
        grad_qshift,
        key_scale_gradient,
        grad_breset,
        grad_bupdate,
        grad_bhidden,
        grad_postnorm,
        grad_bffnin,
        grad_bffnout,
    )
    return (out_row, grad_row, big_grads, small_grads)


def per_device(
    layer_entries,
    loss_sensitivity,
    occupied_counts,
    earlier_normalizer_gain,
    inflow_logits,
    decay_logits,
    channel_lifting,
    channel_collapse,
    direct_term_weight,
    content_projector,
    content_offset,
    common_projector,
    common_offset,
    asking_gain,
    asking_offset,
    lookup_gain,
    forget_gate_matrix,
    forget_gate_offset,
    renewal_gate_matrix,
    renewal_gate_offset,
    candidate_matrix,
    candidate_offset,
    attended_projector,
    later_normalizer_gain,
    hidden_layer_matrix,
    hidden_layer_offset,
    outward_layer_matrix,
    outward_layer_offset,
):
    smalls = (
        earlier_normalizer_gain,
        inflow_logits,
        decay_logits,
        channel_lifting,
        channel_collapse,
        direct_term_weight,
        content_offset,
        common_offset,
        asking_gain,
        asking_offset,
        lookup_gain,
        forget_gate_offset,
        renewal_gate_offset,
        candidate_offset,
        later_normalizer_gain,
        hidden_layer_offset,
        outward_layer_offset,
    )
    out_list = []
    grad_list = []
    big_total = None
    small_total = None
    for micro_index in range(layer_entries.shape[0]):
        gathered = (
            lax.all_gather(content_projector, "dp", axis=0, tiled=True),
            lax.all_gather(common_projector, "dp", axis=0, tiled=True),
            lax.all_gather(forget_gate_matrix, "dp", axis=0, tiled=True),
            lax.all_gather(renewal_gate_matrix, "dp", axis=0, tiled=True),
            lax.all_gather(candidate_matrix, "dp", axis=0, tiled=True),
            lax.all_gather(attended_projector, "dp", axis=1, tiled=True),
            lax.all_gather(hidden_layer_matrix, "dp", axis=0, tiled=True),
            lax.all_gather(outward_layer_matrix, "dp", axis=1, tiled=True),
        )
        out_row, grad_row, big_grads, small_grads = micro_step(
            gathered,
            smalls,
            layer_entries[micro_index],
            loss_sensitivity[micro_index],
            occupied_counts[micro_index, 0],
        )
        out_list.append(out_row)
        grad_list.append(grad_row)
        if big_total is None:
            big_total = big_grads
            small_total = small_grads
        else:
            big_total = jax.tree.map(jnp.add, big_total, big_grads)
            small_total = jax.tree.map(jnp.add, small_total, small_grads)
    (
        sum_prenorm,
        sum_alphas,
        sum_deltas,
        sum_expand,
        sum_readout,
        sum_omegas,
        sum_bvalue,
        sum_bshared,
        sum_qscale,
        sum_qshift,
        key_scale_total,
        sum_breset,
        sum_bupdate,
        sum_bhidden,
        sum_postnorm,
        sum_bffnin,
        sum_bffnout,
    ) = small_total
    big_out = (
        lax.psum_scatter(big_total[0], "dp", scatter_dimension=0, tiled=True),
        lax.psum_scatter(big_total[1], "dp", scatter_dimension=0, tiled=True),
        lax.psum_scatter(big_total[2], "dp", scatter_dimension=0, tiled=True),
        lax.psum_scatter(big_total[3], "dp", scatter_dimension=0, tiled=True),
        lax.psum_scatter(big_total[4], "dp", scatter_dimension=0, tiled=True),
        lax.psum_scatter(big_total[5], "dp", scatter_dimension=1, tiled=True),
        lax.psum_scatter(big_total[6], "dp", scatter_dimension=0, tiled=True),
        lax.psum_scatter(big_total[7], "dp", scatter_dimension=1, tiled=True),
    )
    small_out = lax.psum(
        (
            sum_prenorm,
            sum_alphas,
            sum_deltas,
            sum_expand,
            sum_readout,
            sum_omegas,
            sum_bvalue,
            sum_bshared,
            sum_qscale,
            sum_qshift,
            key_scale_total,
            sum_breset,
            sum_bupdate,
            sum_bhidden,
            sum_postnorm,
            sum_bffnin,
            sum_bffnout,
        ),
        "dp",
    )
    outputs = jnp.stack(out_list)
    grad_tokens = jnp.stack(grad_list)
    return (
        outputs,
        grad_tokens,
        small_out[0],
        small_out[1],
        small_out[2],
        small_out[3],
        small_out[4],
        small_out[5],
        big_out[0],
        small_out[6],
        big_out[1],
        small_out[7],
        small_out[8],
        small_out[9],
        small_out[10],
        big_out[2],
        small_out[11],
        big_out[3],
        small_out[12],
        big_out[4],
        small_out[13],
        big_out[5],
        small_out[14],
        big_out[6],
        small_out[15],
        big_out[7],
        small_out[16],
    )


def solution(mesh):
    return jax.shard_map(
        per_device,
        mesh=mesh,
        in_specs=(
            P(None, "dp", None),
            P(None, "dp", None),
            P(None, "dp"),
            P(),
            P(),
            P(),
            P(),
            P(),
            P(),
            P("dp", "mp"),
            P("mp"),
            P("dp", None),
            P(),
            P(),
            P(),
            P(),
            P("dp", "mp"),
            P("mp"),
            P("dp", None),
            P(),
            P("dp", None),
            P(),
            P("mp", "dp"),
            P(),
            P("dp", "mp"),
            P("mp"),
            P("mp", "dp"),
            P(),
        ),
        out_specs=(
            P(None, "dp", None),
            P(None, "dp", None),
            P(),
            P(),
            P(),
            P(),
            P(),
            P(),
            P("dp", "mp"),
            P("mp"),
            P("dp", None),
            P(),
            P(),
            P(),
            P(),
            P("dp", "mp"),
            P("mp"),
            P("dp", None),
            P(),
            P("dp", None),
            P(),
            P("mp", "dp"),
            P(),
            P("dp", "mp"),
            P("mp"),
            P("mp", "dp"),
            P(),
        ),
        check_vma=False,
    )
```

profile of v0, /device:TPU:1, one launch (start us, length us, event | category | flops | bytes accessed | tf_op | source)
XLA Modules:
  0.0 2081.9 jit_solution(16799249894392131303)
XLA Ops:
  21.5 5.5 multiply_reduce_fusion.6
  26.9 11.9 rev.10
  38.9 12.9 fusion.18
  59.3 6.1 copy.226
  71.4 17.5 fusion.10
  88.9 17.9 bitcast_add_fusion
  111.1 36.6 %all_gather.35 = bf16[1024,128]{1,0:T(8,128)(2,1)S(1)} all-gather(bf16[64,128]{1,0:T(8,128)(2,1)S(1)} %copy-done.168), channel_id=1, replica_groups=mesh['dp'=16,'mp'=2] {'dp'}, dimensions={0}, use_global_device_ids=true | all-gather | bytes 278528 | tf_op jit(solution)/shard_map/all_gather | solution.py:338
  157.1 43.0 %all-gather.16.cloned.1.call-done = bf16[1024,1024]{0,1:T(8,128)(2,1)} async-done(((bf16[1024,64]{0,1:T(8,128)(2,1)}), bf16[1024,1024]{0,1:T(8,128)(2,1)}) %all-gather.16.cloned.1.call-update) | async-done | bytes 2097168 | tf_op jit(solution)/shard_map/all_gather | solution.py:342
  211.4 50.6 %all-gather.10.cloned.1.call-done = bf16[1024,1024]{1,0:T(8,128)(2,1)} async-done(((bf16[64,1024]{1,0:T(8,128)(2,1)}), bf16[1024,1024]{1,0:T(8,128)(2,1)}) %all-gather.10.cloned.1.call-update) | async-done | bytes 2097168 | tf_op jit(solution)/shard_map/all_gather | solution.py:341
  262.1 20.5 all-reduce.70.cloned.1.call-done
  284.7 61.9 %all-gather.8.cloned.1.call-done = bf16[1024,1024]{1,0:T(8,128)(2,1)} async-done(((bf16[64,1024]{1,0:T(8,128)(2,1)}), bf16[1024,1024]{1,0:T(8,128)(2,1)}) %all-gather.8.cloned.1.call-update) | async-done | bytes 2097168 | tf_op jit(solution)/shard_map/all_gather | solution.py:340
  350.4 73.4 %all-gather.18.cloned.1.call-done = bf16[1024,2048]{1,0:T(8,128)(2,1)} async-done(((bf16[64,2048]{1,0:T(8,128)(2,1)}), bf16[1024,2048]{1,0:T(8,128)(2,1)}) %all-gather.18.cloned.1.call-update) | async-done | bytes 4194320 | tf_op jit(solution)/shard_map/all_gather | solution.py:343
  426.8 74.9 %all-gather.20.cloned.1.call-done = bf16[2048,1024]{0,1:T(8,128)(2,1)} async-done(((bf16[2048,64]{0,1:T(8,128)(2,1)}), bf16[2048,1024]{0,1:T(8,128)(2,1)}) %all-gather.20.cloned.1.call-update) | async-done | bytes 4194320 | tf_op jit(solution)/shard_map/all_gather | solution.py:344
  514.5 13.4 all-reduce.76.cloned.1.call-done
  547.5 13.2 all-reduce.78.cloned.1.call-done
  566.1 17.0 all-reduce.84.cloned.1.call-done
  592.5 11.9 fusion.6
  638.2 16.8 fusion.14
  655.1 10.7 add_bitcast_fusion
  672.8 13.3 fusion.20
  724.7 17.4 fusion.12
  742.1 17.8 bitcast_add_fusion.1
  772.5 20.7 select_bitcast_fusion
  808.0 6.5 copy.258
  820.2 4.8 convolution_convert_fusion.5
  847.1 12.0 all-reduce.74.cloned.1.call-done
  865.4 17.8 all-reduce.82.cloned.1.call-done
  891.9 17.3 fusion.39
  909.2 10.1 fusion.8
  931.4 20.6 select_bitcast_fusion.1
  960.1 6.0 copy.250
  966.2 18.9 fusion.212
  985.1 27.0 %fusion.1 = (f32[1024,16]{1,0:T(8,128)}, f32[1024,16]{1,0:T(8,128)S(1)}, f32[16,1024,16]{2,0,1:T(8,128)}, f32[16,1024,16]{2,0,1:T(8,128)}) fusion(f32[16,1024,16]{2,0,1:T(8,128)} %rev.10, f32[1024,16,16]{1,2,0:T(8,128)S(1)} %fusion.212, f32[1024,16]{1,0:T(8,128)S(1)} %copy-done.13, f32[1024,8,16]{2,1,0:T(8,128)S(1)} %copy-done.9, ...), kind=kOutput, calls=%fused_computation.8 | convolution fusion | flops 27099136 | bytes 5444608 | tf_op jit(solution)/shard_map/transpose(jvp(sdh,bsd->bdh))/dot_general | solution.py:64
  1016.5 12.0 rev.11
  1028.5 11.9 rev.12
  1040.4 38.9 %multiply_reduce_fusion = (f32[1024,16]{1,0:T(8,128)}, f32[1024,16]{1,0:T(8,128)}, f32[1024,16]{1,0:T(8,128)}, f32[1024,16]{1,0:T(8,128)}, f32[1024,16]{1,0:T(8,...) fusion(f32[1024,16]{1,0:T(8,128)} %copy.228, f32[16]{0:T(128)S(1)} %copy-done.203, ...), kind=kOutput, calls=%fused_computation.15 | convolution fusion | flops 32899072 | bytes 5046336 | tf_op jit(solution)/shard_map/transpose(jvp(bdh,tdh->btd))/dot_general | solution.py:69
  1108.1 5.0 convolution_add_fusion.6
  1132.5 4.7 convolution_add_fusion.1
  1146.6 16.9 fusion.16
  1163.5 10.7 add_bitcast_fusion.1
  1182.8 65.3 %all-reduce.54 = (f32[1024]{0:T(1024)}, f32[1024]{0:T(1024)}, f32[1024]{0:T(1024)}, f32[128]{0:T(128)}, f32[128]{0:T(128)}, /*index=5*/f32[128]{0:T(128)}, f32[1...) all-reduce(f32[1024]{0:T(1024)S(1)} %add.733, ...), channel_id=1, replica_groups=mesh['dp'=16,'mp'=2] {'dp'}, use_global_device_ids=true, to_apply=%region_37.38 | all-reduce | flops 10752 | bytes 86016 | tf_op jit(solution)/shard_map/psum | solution.py:390
  1251.7 62.5 %reduce-scatter.15.cloned.1.call-done = f32[64,1024]{1,0:T(8,128)} async-done(((f32[1024,1024]{1,0:T(8,128)}), f32[64,1024]{1,0:T(8,128)}) %reduce-scatter.15.cloned.1.call-update) | async-done | bytes 262160 | tf_op jit(solution)/shard_map/reduce_scatter | solution.py:384
  1314.2 97.9 %reduce-scatter.19.cloned.1.call-done = f32[1024,64]{0,1:T(8,128)} async-done(((f32[1024,1024]{0,1:T(8,128)}), f32[1024,64]{0,1:T(8,128)}) %reduce-scatter.19.cloned.1.call-update) | async-done | bytes 262160 | tf_op jit(solution)/shard_map/reduce_scatter | solution.py:386
  1412.1 97.4 %reduce-scatter.17.cloned.1.call-done = f32[64,1024]{1,0:T(8,128)} async-done(((f32[1024,1024]{1,0:T(8,128)}), f32[64,1024]{1,0:T(8,128)}) %reduce-scatter.17.cloned.1.call-update) | async-done | bytes 262160 | tf_op jit(solution)/shard_map/reduce_scatter | solution.py:385
  1509.6 97.6 %reduce-scatter.13.cloned.1.call-done = f32[64,1024]{1,0:T(8,128)} async-done(((f32[1024,1024]{1,0:T(8,128)}), f32[64,1024]{1,0:T(8,128)}) %reduce-scatter.13.cloned.1.call-update) | async-done | bytes 262160 | tf_op jit(solution)/shard_map/reduce_scatter | solution.py:383
  1607.2 97.6 %reduce-scatter.9.cloned.1.call-done = f32[64,1024]{1,0:T(8,128)} async-done(((f32[1024,1024]{1,0:T(8,128)}), f32[64,1024]{1,0:T(8,128)}) %reduce-scatter.9.cloned.1.call-update) | async-done | bytes 262160 | tf_op jit(solution)/shard_map/reduce_scatter | solution.py:381
  1704.8 181.0 %reduce-scatter.21.cloned.1.call-done = f32[64,2048]{1,0:T(8,128)} async-done(((f32[1024,2048]{1,0:T(8,128)}), f32[64,2048]{1,0:T(8,128)}) %reduce-scatter.21.cloned.1.call-update) | async-done | bytes 524304 | tf_op jit(solution)/shard_map/reduce_scatter | solution.py:387
  1885.8 183.0 %reduce-scatter.23.cloned.1.call-done = f32[2048,64]{0,1:T(8,128)} async-done(((f32[2048,1024]{0,1:T(8,128)}), f32[2048,64]{0,1:T(8,128)}) %reduce-scatter.23.cloned.1.call-update) | async-done | bytes 524304 | tf_op jit(solution)/shard_map/reduce_scatter | solution.py:388
  (769 shorter events, 356.0 us)
Async XLA Ops:
  7.2 142.5 %all-gather.12.cloned.1.call-start = ((), (), s32[]{:S(2)}) async-start(), calls=%async_computation.10 | async-start | bytes 2228224 | tf_op jit(solution)/shard_map/all_gather | solution.py:339
  7.9 144.6 %all-gather.14.cloned.1.call-start = ((), (), s32[]{:S(2)}) async-start(), calls=%async_computation.11 | async-start | bytes 2228224 | tf_op jit(solution)/shard_map/all_gather | solution.py:337
  8.7 191.4 %all-gather.16.cloned.1.call-start = ((), (), s32[]{:S(2)}) async-start(), calls=%async_computation.12 | async-start | bytes 2228224 | tf_op jit(solution)/shard_map/all_gather | solution.py:342
  9.4 252.6 %all-gather.10.cloned.1.call-start = ((), (), s32[]{:S(2)}) async-start(), calls=%async_computation.9 | async-start | bytes 2228224 | tf_op jit(solution)/shard_map/all_gather | solution.py:341
  10.0 272.5 %all-reduce.70.cloned.1.call-start = ((), (), s32[]{:S(2)}) async-start(), calls=%async_computation.16 | async-start | bytes 1048576 | tf_op jit(solution)/shard_map/psum | solution.py:165
  18.6 654.3 %copy-start.12 = (f32[1024,16]{1,0:T(8,128)}, f32[1024,16]{1,0:T(8,128)S(1)}, u32[]{:S(2)}) copy-start(f32[1024,16]{1,0:T(8,128)S(1)} %copy.229) | copy-start | bytes 196612
  106.9 42.0 %copy-start.195 = (f32[128]{0:T(128)S(1)}, f32[128]{0:T(128)}, u32[]{:S(2)}) copy-start(f32[128]{0:T(128)} %param.40) | copy-start | bytes 1540
  106.9 42.2 %copy-start.204 = (f32[128]{0:T(128)S(1)}, f32[128]{0:T(128)}, u32[]{:S(2)}) copy-start(f32[128]{0:T(128)} %param.43) | copy-start | bytes 1540
  106.9 42.2 %copy-start.206 = (f32[128]{0:T(128)S(1)}, f32[128]{0:T(128)}, u32[]{:S(2)}) copy-start(f32[128]{0:T(128)} %param.41) | copy-start | bytes 1540
  106.9 42.2 %copy-start.216 = (f32[128]{0:T(128)S(1)}, f32[128]{0:T(128)}, u32[]{:S(2)}) copy-start(f32[128]{0:T(128)} %param.42) | copy-start | bytes 1540
  106.9 42.7 %copy-start.156 = (f32[1024]{0:T(1024)S(1)}, f32[1024]{0:T(1024)}, u32[]{:S(2)}) copy-start(f32[1024]{0:T(1024)} %param.45) | copy-start | bytes 12292
  109.8 42.7 %copy-start.154 = (f32[1024]{0:T(1024)S(1)}, f32[1024]{0:T(1024)}, u32[]{:S(2)}) copy-start(f32[1024]{0:T(1024)} %param.38) | copy-start | bytes 12292
  147.8 435.4 %copy-start.23 = (bf16[1024,128]{1,0:T(8,128)(2,1)}, bf16[1024,128]{1,0:T(8,128)(2,1)S(1)}, u32[]{:S(2)}) copy-start(bf16[1024,128]{1,0:T(8,128)(2,1)S(1)} %all_gather.35) | copy-start | bytes 786436
  148.9 197.7 %copy-start.16 = (bf16[128,1024]{1,0:T(8,128)(2,1)}, bf16[128,1024]{1,0:T(8,128)(2,1)S(1)}, u32[]{:S(2)}) copy-start(bf16[128,1024]{1,0:T(8,128)(2,1)S(1)} %get-tuple-element.232) | copy-start | bytes 786436
  154.6 49.2 %copy-start.106 = (f32[128,1024]{1,0:T(8,128)}, f32[128,1024]{1,0:T(8,128)S(1)}, u32[]{:S(2)}) copy-start(f32[128,1024]{1,0:T(8,128)S(1)} %convolution_add_fusion.16) | copy-start | bytes 1572868
  154.7 50.8 %copy-start.208 = (f32[128]{0:T(128)S(1)}, f32[128]{0:T(128)}, u32[]{:S(2)}) copy-start(f32[128]{0:T(128)} %get-tuple-element.163) | copy-start | bytes 1540
  157.0 51.9 %copy-start.88 = (bf16[128,1024]{1,0:T(8,128)(2,1)}, bf16[128,1024]{1,0:T(8,128)(2,1)S(1)}, u32[]{:S(2)}) copy-start(bf16[128,1024]{1,0:T(8,128)(2,1)S(1)} %get-tuple-element.308) | copy-start | bytes 786436
  200.1 82.5 %copy-start.158 = (f32[1024]{0:T(1024)S(1)}, f32[1024]{0:T(1024)}, u32[]{:S(2)}) copy-start(f32[1024]{0:T(1024)} %param.49) | copy-start | bytes 12292
  203.3 143.3 %all-gather.8.cloned.1.call-start = ((), (), s32[]{:S(2)}) async-start(), calls=%async_computation.8 | async-start | bytes 2228224 | tf_op jit(solution)/shard_map/all_gather | solution.py:340
  203.9 219.9 %all-gather.18.cloned.1.call-start = ((), (), s32[]{:S(2)}) async-start(), calls=%async_computation.14 | async-start | bytes 4456448 | tf_op jit(solution)/shard_map/all_gather | solution.py:343
  204.6 142.0 %copy-start.215 = (f32[1024]{0:T(1024)S(1)}, f32[1024]{0:T(1024)}, u32[]{:S(2)}) copy-start(f32[1024]{0:T(1024)} %param.47) | copy-start | bytes 12292
  204.7 297.0 %all-gather.20.cloned.1.call-start = ((), (), s32[]{:S(2)}) async-start(), calls=%async_computation.15 | async-start | bytes 4456448 | tf_op jit(solution)/shard_map/all_gather | solution.py:344
  205.4 322.5 %all-reduce.76.cloned.1.call-start = ((), (), s32[]{:S(2)}) async-start(), calls=%async_computation.19 | async-start | bytes 1048576 | tf_op jit(solution)/shard_map/psum | solution.py:184
  205.5 77.1 %copy-start.142 = (f32[128]{0:T(128)}, f32[128]{0:T(128)S(1)}, u32[]{:S(2)}) copy-start(f32[128]{0:T(128)S(1)} %broadcast_multiply_fusion.11) | copy-start | bytes 1540
  284.7 61.9 %copy-start.68 = (f32[128,1024]{1,0:T(8,128)}, f32[128,1024]{1,0:T(8,128)S(1)}, u32[]{:S(2)}) copy-start(f32[128,1024]{1,0:T(8,128)S(1)} %fusion.92) | copy-start | bytes 1572868
  284.7 139.1 %copy-start.113 = (f32[1024]{0:T(1024)S(1)}, f32[1024]{0:T(1024)}, u32[]{:S(2)}) copy-start(f32[1024]{0:T(1024)} %param.51) | copy-start | bytes 12292
  349.5 181.1 %copy-start.14 = (f32[128,1024]{1,0:T(8,128)}, f32[128,1024]{1,0:T(8,128)S(1)}, u32[]{:S(2)}) copy-start(f32[128,1024]{1,0:T(8,128)S(1)} %get-tuple-element.231) | copy-start | bytes 1572868
  349.5 152.1 %copy-start.26 = (bf16[2,128,1024]{2,1,0:T(8,128)(2,1)S(1)}, bf16[2,128,1024]{2,1,0:T(8,128)(2,1)}, u32[]{:S(2)}) copy-start(bf16[2,128,1024]{2,1,0:T(8,128)(2,1)} %param.29) | copy-start | bytes 1572868
  426.8 83.3 %copy-start.39 = (f32[128,2048]{1,0:T(8,128)}, f32[128,2048]{1,0:T(8,128)S(1)}, u32[]{:S(2)}) copy-start(f32[128,2048]{1,0:T(8,128)S(1)} %convolution_add_fusion.2) | copy-start | bytes 3145732
  508.8 51.9 %all-reduce.78.cloned.1.call-start = ((), (), s32[]{:S(2)}) async-start(), calls=%async_computation.20 | async-start | bytes 131072 | tf_op jit(solution)/shard_map/psum | solution.py:205
  541.6 41.5 %all-reduce.84.cloned.1.call-start = ((), (), s32[]{:S(2)}) async-start(), calls=%async_computation.31 | async-start | bytes 1048576 | tf_op jit(solution)/shard_map/psum | solution.py:237
  547.5 245.7 %all-reduce.68.cloned.1.call-start = ((), (), s32[]{:S(2)}) async-start(), calls=%async_computation.13 | async-start | bytes 1048576 | tf_op jit(solution)/shard_map/psum | solution.py:165
  772.4 53.5 %all-reduce.72.cloned.1.call-start = ((), (), s32[]{:S(2)}) async-start(), calls=%async_computation.17 | async-start | bytes 1048576 | tf_op jit(solution)/shard_map/psum | solution.py:184
  805.9 53.2 %all-reduce.74.cloned.1.call-start = ((), (), s32[]{:S(2)}) async-start(), calls=%async_computation.18 | async-start | bytes 131072 | tf_op jit(solution)/shard_map/psum | solution.py:205
  840.0 43.2 %all-reduce.82.cloned.1.call-start = ((), (), s32[]{:S(2)}) async-start(), calls=%async_computation.30 | async-start | bytes 2097152 | tf_op jit(solution)/shard_map/psum | solution.py:173
  847.1 404.7 %reduce-scatter.11.cloned.1.call-start = ((), (), s32[]{:S(2)}) async-start(), calls=%async_computation.22 | async-start | bytes 557056 | tf_op jit(solution)/shard_map/reduce_scatter | solution.py:382
  865.3 386.4 %all-reduce.80.cloned.1.call-start = ((), (), s32[]{:S(2)}) async-start(), calls=%async_computation.29 | async-start | bytes 524288 | tf_op jit(solution)/shard_map/psum | solution.py:390
  1040.4 44.7 %copy-start.86 = (f32[4,1024,16]{1,2,0:T(8,128)S(1)}, f32[4,1024,16]{1,2,0:T(8,128)}, u32[]{:S(2)}) copy-start(f32[4,1024,16]{1,2,0:T(8,128)} %get-tuple-element.200) | copy-start | bytes 786436
  1108.0 206.2 %reduce-scatter.15.cloned.1.call-start = ((), (), s32[]{:S(2)}) async-start(), calls=%async_computation.24 | async-start | bytes 4456448 | tf_op jit(solution)/shard_map/reduce_scatter | solution.py:384
  1113.1 299.0 %reduce-scatter.19.cloned.1.call-start = ((), (), s32[]{:S(2)}) async-start(), calls=%async_computation.26 | async-start | bytes 4456448 | tf_op jit(solution)/shard_map/reduce_scatter | solution.py:386
  1117.5 392.0 %reduce-scatter.17.cloned.1.call-start = ((), (), s32[]{:S(2)}) async-start(), calls=%async_computation.25 | async-start | bytes 4456448 | tf_op jit(solution)/shard_map/reduce_scatter | solution.py:385
  1121.0 486.2 %reduce-scatter.13.cloned.1.call-start = ((), (), s32[]{:S(2)}) async-start(), calls=%async_computation.23 | async-start | bytes 4456448 | tf_op jit(solution)/shard_map/reduce_scatter | solution.py:383
  1125.5 579.3 %reduce-scatter.9.cloned.1.call-start = ((), (), s32[]{:S(2)}) async-start(), calls=%async_computation.21 | async-start | bytes 4456448 | tf_op jit(solution)/shard_map/reduce_scatter | solution.py:381
  1130.1 755.7 %reduce-scatter.21.cloned.1.call-start = ((), (), s32[]{:S(2)}) async-start(), calls=%async_computation.27 | async-start | bytes 8912896 | tf_op jit(solution)/shard_map/reduce_scatter | solution.py:387
  1137.2 931.5 %reduce-scatter.23.cloned.1.call-start = ((), (), s32[]{:S(2)}) async-start(), calls=%async_computation.28 | async-start | bytes 8912896 | tf_op jit(solution)/shard_map/reduce_scatter | solution.py:388
  1177.8 70.3 %copy-start.33 = (f32[128,1024]{1,0:T(8,128)S(1)}, f32[128,1024]{1,0:T(8,128)}, u32[]{:S(2)}) copy-start(f32[128,1024]{1,0:T(8,128)} %copy-done.32) | copy-start | bytes 1572868
  1177.8 70.3 %copy-start.182 = (f32[1024]{0:T(1024)S(1)}, f32[1024]{0:T(1024)}, u32[]{:S(2)}) copy-start(f32[1024]{0:T(1024)} %param.55) | copy-start | bytes 12292
  1177.8 70.3 %copy-start.193 = (f32[128]{0:T(128)S(1)}, f32[128]{0:T(128)}, u32[]{:S(2)}) copy-start(f32[128]{0:T(128)} %copy-done.192) | copy-start | bytes 1540
  (208 other events, 1550.7 us)
Sparse Core Ops, SparseCore 0:
  10.8 62.3 all-gather.11
  75.9 61.5 all-gather.13
  140.3 59.6 all-gather.15
  202.7 59.3 all-gather.9
  264.3 18.2 all-reduce.69
  285.5 61.0 all-gather.7
  349.7 73.9 all-gather.17
  426.9 74.6 all-gather.19
  508.9 18.8 all-reduce.75
  541.8 18.8 all-reduce.77
  563.1 20.0 all-reduce.83
  772.5 19.9 all-reduce.67
  806.0 19.8 all-reduce.71
  840.1 18.9 all-reduce.73
  862.2 20.8 all-reduce.81
  885.8 66.3 reduce-scatter.10
  1108.1 107.3 all-reduce.79
  1218.3 95.8 reduce-scatter.14
  1317.1 95.0 reduce-scatter.18
  1414.8 94.6 reduce-scatter.16
  1512.4 94.7 reduce-scatter.12
  1610.0 94.7 reduce-scatter.8
  1707.7 178.0 reduce-scatter.20
  1888.5 180.2 reduce-scatter.22
where the time goes:
time: 2100 us; the launch traced here: 2080 us
  waiting for transfers between devices  1220 us (58%)
  matrix products  443 us (21%)
  local copies, waits for them, and re-layouts  209 us (10%)
  blocking collectives  102 us (5%)
  other arithmetic  88.9 us (4%)
    reduce_scatter x1, waiting for transfers between devices, per_device(): lax.psum_scatter(big_total[7], 'dp', scatter_dimension=1, tiled=True)  183 us
    reduce_scatter x1, waiting for transfers between devices, per_device(): lax.psum_scatter(big_total[6], 'dp', scatter_dimension=0, tiled=True)  181 us
    dot_general x6, matrix products, ema_apply(): jnp.einsum('bdh,tdh->btd', earlier, carry_weight, precision=highest)  113 us
    dot_general x6, matrix products, ema_apply(): jnp.einsum('sdh,bsd->bdh', tail_power, pieces, precision=highest)  106 us
    dot_general x6, matrix products, ema_apply(): inside = jnp.einsum('tsd,bsd->btd', toeplitz, pieces, precision=highest)  98.4 us
    reduce_scatter x1, waiting for transfers between devices, per_device(): lax.psum_scatter(big_total[5], 'dp', scatter_dimension=1, tiled=True)  97.9 us
    reduce_scatter x1, waiting for transfers between devices, per_device(): lax.psum_scatter(big_total[2], 'dp', scatter_dimension=0, tiled=True)  97.6 us
    reduce_scatter x1, waiting for transfers between devices, per_device(): lax.psum_scatter(big_total[0], 'dp', scatter_dimension=0, tiled=True)  97.6 us
  transfers between devices with their start and end apart: 24, of which 19 were waited for; matrix products, arithmetic and copies ran while one was open for 24% of the time, Pallas kernels for 0%

commit v1 on v0

v1 whole, which is shorter than its diff:
```python
import functools

import jax
import jax.numpy as jnp
from jax import lax
from jax.experimental import pallas as pl
from jax.experimental.pallas import tpu as pltpu
from jax.sharding import PartitionSpec as P

COMMON_SPAN_DIM = 128
SPAN = 128
LANES = 128
SUBLANES = 8

epsilon = 1e-05
bf16 = jnp.bfloat16
f32 = jnp.float32


def product(left, right):
    return jnp.dot(left, right, preferred_element_type=f32)


def left_inner(left, right):
    return lax.dot_general(left, right, (((0,), (0,)), ((), ())), preferred_element_type=f32)


def right_inner(left, right):
    return lax.dot_general(left, right, (((1,), (1,)), ((), ())), preferred_element_type=f32)


def silu_slope(values):
    sigma = jax.nn.sigmoid(values)
    return sigma * (1.0 + values * (1.0 - sigma))


def radices_of(n):
    found = []
    while n > 1:
        r = 4 if n % 4 == 0 and (n > 4 or not found) else 2
        if n % r:
            r = n
        found.append(r)
        n //= r
    while len(found) < 3:
        found.append(1)
    return tuple(found)


class Grid:
    def __init__(self, n):
        self.n = n
        self.radix = radices_of(n)
        strides, left = [], n
        for r in self.radix:
            left //= r
            strides.append(left)
        self.stride = tuple(strides)

    def coords(self, index):
        return [(index // s) % r for s, r in zip(self.stride, self.radix)]

    def shift(self, dim, k):
        pairs = []
        for source in range(self.n):
            at = (source // self.stride[dim]) % self.radix[dim]
            to = (at + k) % self.radix[dim]
            pairs.append((source, source + (to - at) * self.stride[dim]))
        return pairs

    def gather_dim(self, array, dim):
        r = self.radix[dim]
        if r == 1:
            return array
        got = [array]
        for k in range(1, r):
            got.append(lax.ppermute(array, "dp", self.shift(dim, -k)))
        return jnp.concatenate(got, axis=dim)

    def scatter_dim(self, array, dim, last):
        r = self.radix[dim]
        if r == 1:
            return array.astype(f32) if last else array
        parts = [lax.slice_in_dim(array, k, k + 1, axis=dim) for k in range(r)]
        got = [parts[0]]
        for k in range(1, r):
            got.append(lax.ppermute(parts[k], "dp", self.shift(dim, k)))
        total = got[0].astype(f32)
        for g in got[1:]:
            total = total + g.astype(f32)
        return total if last else total.astype(bf16)

    def sum_all(self, value):
        for dim, r in reversed(list(enumerate(self.radix))):
            got = [value] + [
                lax.ppermute(value, "dp", self.shift(dim, -k)) for k in range(1, r)
            ]
            if r == 4:
                value = (got[0] + got[2]) + (got[1] + got[3])
            elif r == 2:
                value = got[0] + got[1]
            elif r > 2:
                value = lax.psum(value, "dp", axis_index_groups=self.groups(dim))
        return value

    def groups(self, dim):
        lines = {}
        for i in range(self.n):
            c = self.coords(i)
            c[dim] = 0
            lines.setdefault(tuple(c), []).append(i)
        return list(lines.values())

    def blocks(self, rows):
        return tuple(self.radix) + (rows,)

    def permutation(self, width):
        rows = width // self.n
        me = lax.axis_index("dp")
        place = jnp.arange(width)
        block = place // rows
        absolute = place % rows
        for s, r in zip(self.stride, self.radix):
            absolute = absolute + (((block // s) % r + (me // s) % r) % r) * (s * rows)
        return (jnp.arange(width)[:, None] == absolute[None, :]).astype(bf16)


def gather_all(grid, units, orders):
    done = []
    before = None
    for unit, order in zip(units, orders):
        rows, columns = unit.shape
        array = unit.reshape((1,) * len(grid.radix) + (rows, columns))
        if before is not None:
            array, before = lax.optimization_barrier((array, before))
            done[-1] = before
        array = grid.gather_dim(array, order[0])
        before = array
        done.append(array)
    full = []
    for array, order in zip(done, orders):
        for dim in order[1:]:
            array = grid.gather_dim(array, dim)
        full.append(array.reshape(grid.n * array.shape[-2], array.shape[-1]))
    return full


def scatter_one(grid, array, order):
    total, columns = array.shape
    rows = total // grid.n
    array = array.astype(bf16).reshape(grid.blocks(rows) + (columns,))
    for at, dim in enumerate(order):
        array = grid.scatter_dim(array, dim, at == len(order) - 1)
    return array.reshape(rows, columns)


def tiles_of(array):
    return [array[i * SUBLANES : (i + 1) * SUBLANES] for i in range(array.shape[0] // SUBLANES)]


def row_tile(table_ref, lag, c):
    row = table_ref[lag, pl.ds(c, 1), :]
    return jnp.broadcast_to(row, (SUBLANES, LANES))


def norm_parts(x_ref):
    values = x_ref[...].astype(f32)
    center = values - jnp.mean(values, axis=-1, keepdims=True)
    scale = lax.rsqrt(jnp.mean(center * center, axis=-1, keepdims=True) + epsilon)
    return center * scale, scale


def ema_forward_kernel(
    x_ref, gain_ref, direct_ref, inflow_ref, decay_ref, lift_ref, collapse_ref,
    normed_ref, pre_ref, norm_low_ref, smooth_low_ref, table_ref,
):
    steps = x_ref.shape[0]
    hat, unused = norm_parts(x_ref)
    normed = hat * gain_ref[...]
    normed_ref[...] = normed
    norm_low_ref[...] = normed.astype(bf16)
    rate = jax.nn.sigmoid(inflow_ref[...])
    keep = 1.0 - rate * jax.nn.sigmoid(decay_ref[...])
    weight = collapse_ref[...] * (rate * lift_ref[...])

    def lag_step(lag, power):
        table_ref[lag] = jnp.sum(weight * power, axis=0)
        return power * keep

    lax.fori_loop(0, steps, lag_step, jnp.ones_like(keep))
    count = steps // SUBLANES
    sub = lax.broadcasted_iota(jnp.int32, (steps, LANES), 0)

    def block(c, carry):
        columns = pl.ds(pl.multiple_of(c * LANES, LANES), LANES)
        base = normed_ref[:, columns]
        total = [jnp.zeros((SUBLANES, LANES), f32)] * count
        for r in range(SUBLANES):
            moved = base if r == 0 else jnp.where(sub >= r, pltpu.roll(base, r, 0), 0.0)
            moved = tiles_of(moved)
            for q in range(count):
                w = row_tile(table_ref, q * SUBLANES + r, c)
                for i in range(q, count):
                    total[i] = total[i] + w * moved[i - q]
        pre = jnp.concatenate(total, axis=0) + direct_ref[:, columns] * base
        pre_ref[:, columns] = pre
        smooth_low_ref[:, columns] = (pre * jax.nn.sigmoid(pre)).astype(bf16)
        return carry

    lax.fori_loop(0, x_ref.shape[1] // LANES, block, 0)


def ema_backward_kernel(
    x_ref, gain_ref, direct_ref, inflow_ref, decay_ref, table_ref, normed_ref, pre_ref,
    grad_smooth_ref, grad_normed_ref, grad_input_ref,
    grad_row_ref, vectors_ref, zero_ref, first_ref,
    inner_ref, lag_ref,
):
    steps = x_ref.shape[0]
    count = steps // SUBLANES
    sub = lax.broadcasted_iota(jnp.int32, (steps, LANES), 0)

    def block(c, carry):
        columns = pl.ds(pl.multiple_of(c * LANES, LANES), LANES)
        pre = pre_ref[:, columns]
        grad_pre = grad_smooth_ref[:, columns] * silu_slope(pre)
        normed = normed_ref[:, columns]
        vectors_ref[1:2, columns] = jnp.sum(grad_pre * normed, axis=0, keepdims=True)
        own = tiles_of(normed)
        total = tiles_of(grad_normed_ref[:, columns] + direct_ref[:, columns] * grad_pre)
        for r in range(SUBLANES):
            moved = grad_pre
            if r:
                moved = jnp.where(sub < steps - r, pltpu.roll(grad_pre, steps - r, 0), 0.0)
            moved = tiles_of(moved)
            for q in range(count):
                w = row_tile(table_ref, q * SUBLANES + r, c)
                lag_sum = jnp.zeros((SUBLANES, LANES), f32)
                for i in range(count - q):
                    g = moved[i + q]
                    total[i] = total[i] + w * g
                    lag_sum = lag_sum + g * own[i]
                lag_ref[q * SUBLANES + r, pl.ds(c, 1), :] = jnp.sum(lag_sum, axis=0, keepdims=True)
        inner_ref[:, columns] = jnp.concatenate(total, axis=0)
        return carry

    lax.fori_loop(0, x_ref.shape[1] // LANES, block, 0)

    keep_all = 1.0 - jax.nn.sigmoid(inflow_ref[...]) * jax.nn.sigmoid(decay_ref[...])
    half = keep_all.shape[0] // 2
    for h in range(2):
        keep = keep_all[h * half : (h + 1) * half]

        def lag_step(lag, carry):
            power, zero, first = carry
            g = lag_ref[lag]
            first = first + (g * lag.astype(f32))[None] * power
            power = power * keep
            return (power, zero + g[None] * power, first)

        blank = jnp.zeros_like(keep)
        start = (jnp.ones_like(keep), blank + lag_ref[0][None], blank)
        unused, zero, first = lax.fori_loop(1, steps, lag_step, start)
        zero_ref[h * half : (h + 1) * half] = zero
        first_ref[h * half : (h + 1) * half] = first

    hat, scale = norm_parts(x_ref)
    grad = inner_ref[...]
    vectors_ref[0:1] = jnp.sum(grad * hat, axis=0, keepdims=True)
    grad = grad * gain_ref[...]
    grad = grad - jnp.mean(grad, axis=-1, keepdims=True) - hat * jnp.mean(
        grad * hat, axis=-1, keepdims=True
    )
    grad_row_ref[...] = (grad_input_ref[...] + scale * grad).astype(bf16)


def ema_forward(x, gain, direct, folded):
    steps, width = x.shape
    like = jax.ShapeDtypeStruct
    return pl.pallas_call(
        ema_forward_kernel,
        name="average_forward",
        out_shape=(
            like((steps, width), f32),
            like((steps, width), f32),
            like((steps, width), bf16),
            like((steps, width), bf16),
            like((steps, width // LANES, LANES), f32),
        ),
        cost_estimate=pl.CostEstimate(flops=20_000_000, bytes_accessed=3_000_000, transcendentals=0),
    )(x, gain[None], direct[None], *folded)


def ema_backward(x, gain, direct, folded, table, normed, pre, grad_smooth, grad_normed, grad_input):
    steps, width = x.shape
    like = jax.ShapeDtypeStruct
    inflow, decay = folded[0], folded[1]
    return pl.pallas_call(
        ema_backward_kernel,
        name="average_backward",
        out_shape=(
            like((steps, width), bf16),
            like((2, width), f32),
            like(inflow.shape, f32),
            like(inflow.shape, f32),
        ),
        scratch_shapes=[
            pltpu.VMEM((steps, width), f32),
            pltpu.VMEM((steps, width // LANES, LANES), f32),
        ],
        cost_estimate=pl.CostEstimate(flops=40_000_000, bytes_accessed=4_000_000, transcendentals=0),
    )(x, gain[None], direct[None], inflow, decay, table, normed, pre, grad_smooth, grad_normed, grad_input)


def per_device(
    grid,
    layer_entries,
    loss_sensitivity,
    occupied_counts,
    earlier_normalizer_gain,
    inflow_logits,
    decay_logits,
    channel_lifting,
    channel_collapse,
    direct_term_weight,
    content_projector,
    content_offset,
    common_projector,
    common_offset,
    asking_gain,
    asking_offset,
    lookup_gain,
    forget_gate_matrix,
    forget_gate_offset,
    renewal_gate_matrix,
    renewal_gate_offset,
    candidate_matrix,
    candidate_offset,
    attended_projector,
    later_normalizer_gain,
    hidden_layer_matrix,
    hidden_layer_offset,
    outward_layer_matrix,
    outward_layer_offset,
):
    core = lax.axis_index("mp")
    micro, steps, width = layer_entries.shape
    half = width // 2
    swap_pairs = [(0, 1), (1, 0)]

    def swap(value):
        return lax.ppermute(value, "mp", swap_pairs)

    def both(own):
        return jnp.concatenate([own, swap(own)], axis=0)

    def reduce_rows(part, send=f32):
        return part[:steps] + swap(part[steps:].astype(send)).astype(f32)

    def in_order(own, other, axis):
        first = jnp.where(core == 0, own, other)
        second = jnp.where(core == 0, other, own)
        return jnp.concatenate([first, second], axis=axis)

    def half_of(value, which, axis):
        return lax.dynamic_slice_in_dim(value, which * half, half, axis=axis)

    ff = hidden_layer_matrix.shape[1] // 2
    misc = jnp.concatenate(
        [
            half_of(renewal_gate_matrix, core, 1),
            half_of(candidate_matrix, core, 1),
            common_projector,
        ],
        axis=1,
    )
    outward_t = outward_layer_matrix.T
    units = [
        content_projector,
        misc,
        forget_gate_matrix,
        attended_projector.T,
        hidden_layer_matrix[:, :ff],
        outward_t[:, :ff],
        hidden_layer_matrix[:, ff:],
        outward_t[:, ff:],
    ]
    dims = list(range(len(grid.radix)))
    alpha = [0] + dims[:0:-1]
    beta = dims
    orders = [alpha, beta] * 4
    (w_value, w_misc, w_reset, w_out, w_in_a, w_down_a, w_in_b, w_down_b) = gather_all(
        grid, units, orders
    )
    w_gates, w_shared = w_misc[:, : 2 * half], w_misc[:, 2 * half :]

    row_in = lax.dynamic_index_in_dim(layer_entries, core, 0, keepdims=False)
    row_seed = lax.dynamic_index_in_dim(loss_sensitivity, core, 0, keepdims=False)
    lengths = jnp.stack(
        [
            lax.dynamic_index_in_dim(occupied_counts[:, 0], core, 0, keepdims=False),
            lax.dynamic_index_in_dim(occupied_counts[:, 0], 1 - core, 0, keepdims=False),
        ]
    )
    position = jnp.arange(steps)
    live_rows = position[None, :] < lengths[:, None]
    live = live_rows[0].astype(f32)[:, None]
    spread = grid.permutation(width)

    def relative(value):
        return product(value, spread).astype(bf16)

    def absolute(value):
        return lax.dot_general(
            value,
            spread.astype(f32),
            (((1,), (1,)), ((), ())),
            precision=lax.Precision.HIGHEST,
            preferred_element_type=f32,
        )

    def fold(value):
        return value.T.reshape(value.shape[1], width // LANES, LANES)

    folded = [fold(v) for v in (inflow_logits, decay_logits, channel_lifting, channel_collapse)]
    seed = live * row_seed.astype(f32)
    seed2 = both(relative(seed.astype(bf16)))
    normed, pre, norm_low, smooth_low, table = ema_forward(
        row_in, earlier_normalizer_gain, direct_term_weight, folded
    )
    norm2 = both(relative(norm_low))
    smooth2 = both(relative(smooth_low))
    input_full = row_in.astype(f32)

    value_pre = product(norm2, w_value) + content_offset
    value_low = jax.nn.silu(value_pre).astype(bf16)
    shared_pre = product(smooth2, w_shared) + common_offset
    shared = jax.nn.silu(shared_pre)
    query_low = (shared * asking_gain + asking_offset).astype(bf16)
    key_low = (shared * lookup_gain).astype(bf16)
    reset_pre = product(smooth2, w_reset) + forget_gate_offset
    reset = jax.nn.silu(reset_pre)
    gates = product(smooth2, w_gates)
    gates_other = swap(gates[steps:])
    update = jax.nn.sigmoid(
        in_order(gates[:steps, :half], gates_other[:, :half], 1) + renewal_gate_offset
    )
    hidden_in = in_order(gates[:steps, half:], gates_other[:, half:], 1) + candidate_offset
    query_rows = query_low.reshape(micro, SPAN, -1)
    key_rows = key_low.reshape(micro, SPAN, -1)
    value_rows = value_low.reshape(micro, SPAN, -1)
    causal = position[None, :] <= position[:, None]
    diagonal = position[None, :] == position[:, None]
    allowed = causal[None] & (live_rows[:, None, :] | diagonal[None])
    scale = COMMON_SPAN_DIM ** (-0.5)
    raw_scores = jnp.einsum("ctz,csz->cts", query_rows, key_rows, preferred_element_type=f32)
    probs = jax.nn.softmax(jnp.where(allowed, raw_scores * scale, -1e30), axis=-1)
    probs_low = probs.astype(bf16)
    attended = jnp.einsum(
        "cts,csv->ctv", probs_low, value_rows, preferred_element_type=f32
    ).reshape(micro * steps, -1)
    mixed = (reset * attended).astype(bf16)
    hidden_pre = hidden_in + absolute(reduce_rows(right_inner(mixed, w_out)))
    hidden = jax.nn.silu(hidden_pre)
    blended = input_full + update * (hidden - input_full)
    center = blended - jnp.mean(blended, axis=-1, keepdims=True)
    post_scale = lax.rsqrt(jnp.mean(center * center, axis=-1, keepdims=True) + epsilon)
    hat = center * post_scale
    ffn2 = both(relative((hat * later_normalizer_gain).astype(bf16)))

    down_part = None
    ffn_norm_part = None
    ffn_grads = []
    bffnin = []
    for at, (w_in, w_down) in enumerate(((w_in_a, w_down_a), (w_in_b, w_down_b))):
        ffn_pre = product(ffn2, w_in) + hidden_layer_offset[at * ff : (at + 1) * ff]
        act = jax.nn.silu(ffn_pre).astype(bf16)
        grad_pre = (product(seed2, w_down) * silu_slope(ffn_pre)).astype(bf16)
        bffnin.append(jnp.sum(grad_pre.astype(f32), axis=0))
        down = right_inner(act, w_down)
        back = right_inner(grad_pre, w_in)
        down_part = down if down_part is None else down_part + down
        ffn_norm_part = back if ffn_norm_part is None else ffn_norm_part + back
        ffn_grads.append(left_inner(ffn2, grad_pre))
        ffn_grads.append(left_inner(seed2, act))
    scatter_orders = [alpha[::-1], beta[::-1]]
    ffn_out = [scatter_one(grid, g, scatter_orders[i % 2]) for i, g in enumerate(ffn_grads)]

    down_full = absolute(reduce_rows(down_part, bf16))
    out_row = (live * (blended + down_full + outward_layer_offset)).astype(bf16)

    grad_ffn_norm = absolute(reduce_rows(ffn_norm_part))
    grad_postnorm = jnp.sum(grad_ffn_norm * hat, axis=0)
    grad_hat = grad_ffn_norm * later_normalizer_gain
    grad_blended = seed + post_scale * (
        grad_hat
        - jnp.mean(grad_hat, axis=-1, keepdims=True)
        - hat * jnp.mean(grad_hat * hat, axis=-1, keepdims=True)
    )
    grad_input = grad_blended * (1.0 - update)
    grad_hidden = (grad_blended * update * silu_slope(hidden_pre)).astype(bf16)
    grad_update = (grad_blended * (hidden - input_full) * update * (1.0 - update)).astype(bf16)
    grad_hidden2 = both(relative(grad_hidden))
    mine = jnp.concatenate([half_of(grad_update, core, 1), half_of(grad_hidden, core, 1)], axis=1)
    theirs = jnp.concatenate(
        [half_of(grad_update, 1 - core, 1), half_of(grad_hidden, 1 - core, 1)], axis=1
    )
    grad_gates2 = jnp.concatenate([mine, swap(theirs)], axis=0)

    grad_mixed = product(grad_hidden2, w_out)
    grad_attended = (grad_mixed * reset).astype(bf16)
    grad_reset = (grad_mixed * attended * silu_slope(reset_pre)).astype(bf16)
    grad_att_rows = grad_attended.reshape(micro, SPAN, -1)
    probs_part = jnp.einsum(
        "ctv,csv->cts", grad_att_rows, value_rows, preferred_element_type=f32
    )
    theirs_part = swap(probs_part)
    grad_probs = probs_part + jnp.concatenate([theirs_part[1:], theirs_part[:1]], axis=0)
    grad_value = jnp.einsum(
        "cts,ctv->csv", probs_low, grad_att_rows, preferred_element_type=f32
    ).reshape(micro * steps, -1)
    grad_value_pre = (grad_value * silu_slope(value_pre)).astype(bf16)
    own_probs, own_grad = probs[0], grad_probs[0]
    grad_scores = (
        own_probs * (own_grad - jnp.sum(own_grad * own_probs, axis=-1, keepdims=True))
    ).astype(bf16)
    grad_query = product(grad_scores, key_rows[0]) * scale
    grad_key = left_inner(grad_scores, query_rows[0]) * scale
    own_shared = shared[:steps]
    grad_shared = (
        (grad_query * asking_gain + grad_key * lookup_gain) * silu_slope(shared_pre[:steps])
    ).astype(bf16)
    grad_misc = jnp.concatenate(
        [grad_gates2, jnp.concatenate([grad_shared, jnp.zeros_like(grad_shared)], axis=0)], axis=1
    )
    smooth_part = right_inner(grad_reset, w_reset) + right_inner(grad_misc, w_misc)
    norm_part = right_inner(grad_value_pre, w_value)
    grad_both = absolute(
        jnp.concatenate([reduce_rows(smooth_part, bf16), reduce_rows(norm_part, bf16)], axis=0)
    )
    grad_row, grad_vectors, grad_zero, grad_first = ema_backward(
        row_in,
        earlier_normalizer_gain,
        direct_term_weight,
        folded,
        table,
        normed,
        pre,
        grad_both[:steps],
        grad_both[steps:],
        grad_input,
    )
    out_wout = scatter_one(grid, left_inner(grad_hidden2, mixed), scatter_orders[1])
    out_reset = scatter_one(grid, left_inner(smooth2, grad_reset), scatter_orders[0])
    out_value = scatter_one(grid, left_inner(norm2, grad_value_pre), scatter_orders[0])
    out_misc = scatter_one(grid, left_inner(smooth2, grad_misc), scatter_orders[1])

    lanes = COMMON_SPAN_DIM
    narrow = jnp.concatenate(
        [
            jnp.sum(grad_shared.astype(f32), axis=0),
            jnp.sum(grad_query * own_shared, axis=0),
            jnp.sum(grad_query, axis=0),
            jnp.sum(grad_key * own_shared, axis=0),
        ]
    )
    narrow = jnp.pad(narrow, (0, width - 4 * lanes))[None]
    states = grad_zero.shape[0]
    shared_sums = jnp.concatenate(
        [
            grad_zero.reshape(states, width),
            grad_first.reshape(states, width),
            grad_vectors,
            jnp.sum(grad_update.astype(f32), axis=0)[None],
            jnp.sum(grad_hidden.astype(f32), axis=0)[None],
            grad_postnorm[None],
            jnp.sum(seed, axis=0)[None],
            narrow,
            jnp.zeros((1, width), f32),
        ],
        axis=0,
    )
    rows = shared_sums.shape[0] // 2
    keep_rows = lax.dynamic_slice_in_dim(shared_sums, core * rows, rows, axis=0)
    send_rows = lax.dynamic_slice_in_dim(shared_sums, (1 - core) * rows, rows, axis=0)
    keep_rows = keep_rows + swap(send_rows)
    wide_sums = jnp.concatenate(
        [
            jnp.sum(grad_value_pre.astype(f32), axis=0)[None],
            jnp.sum(grad_reset.astype(f32), axis=0)[None],
            bffnin[0].reshape(-1, width),
            bffnin[1].reshape(-1, width),
        ],
        axis=0,
    )
    sums = grid.sum_all(jnp.concatenate([keep_rows, wide_sums], axis=0))
    first_rows = sums[:rows]
    whole = in_order(first_rows, swap(first_rows), 0)
    wide = sums[rows:]
    zero = whole[:states].T
    first = whole[states : 2 * states].T
    rate = jax.nn.sigmoid(inflow_logits)
    damp = jax.nn.sigmoid(decay_logits)
    grad_collapse = rate * channel_lifting * zero
    grad_inflow = channel_collapse * zero
    grad_keep = channel_collapse * rate * channel_lifting * first
    grad_lifting = grad_inflow * rate
    grad_rate = (grad_inflow * channel_lifting - grad_keep * damp) * rate * (1.0 - rate)
    grad_damp = -grad_keep * rate * damp * (1.0 - damp)
    rest = whole[2 * states :]
    thin = rest[6].reshape(-1, lanes)

    gates_half = out_misc[:, : 2 * half]
    gates_full_other = swap(gates_half)
    out_update = in_order(gates_half[:, :half], gates_full_other[:, :half], 1)
    out_hidden = in_order(gates_half[:, half:], gates_full_other[:, half:], 1)
    out_shared = out_misc[:, 2 * half :]
    out_shared = out_shared + swap(out_shared)

    rows_out = jnp.stack([out_row, grad_row])
    rows_other = swap(rows_out)
    outputs = in_order(rows_out[:1], rows_other[:1], 0)
    grad_tokens = in_order(rows_out[1:], rows_other[1:], 0)
    return (
        outputs,
        grad_tokens,
        rest[0],
        grad_rate,
        grad_damp,
        grad_lifting,
        grad_collapse,
        rest[1],
        out_value,
        wide[0],
        out_shared,
        thin[0],
        thin[1],
        thin[2],
        thin[3],
        out_reset,
        wide[1],
        out_update,
        rest[2],
        out_hidden,
        rest[3],
        out_wout.T,
        rest[4],
        jnp.concatenate([ffn_out[0], ffn_out[2]], axis=1),
        wide[2:].reshape(-1),
        jnp.concatenate([ffn_out[1].T, ffn_out[3].T], axis=0),
        rest[5],
    )


def solution(mesh):
    grid = Grid(mesh.shape["dp"])
    return jax.shard_map(
        functools.partial(per_device, grid),
        mesh=mesh,
        in_specs=(
            P(None, "dp", None),
            P(None, "dp", None),
            P(None, "dp"),
            P(),
            P(),
            P(),
            P(),
            P(),
            P(),
            P("dp", "mp"),
            P("mp"),
            P("dp", None),
            P(),
            P(),
            P(),
            P(),
            P("dp", "mp"),
            P("mp"),
            P("dp", None),
            P(),
            P("dp", None),
            P(),
            P("mp", "dp"),
            P(),
            P("dp", "mp"),
            P("mp"),
            P("mp", "dp"),
            P(),
        ),
        out_specs=(
            P(None, "dp", None),
            P(None, "dp", None),
            P(),
            P(),
            P(),
            P(),
            P(),
            P(),
            P("dp", "mp"),
            P("mp"),
            P("dp", None),
            P(),
            P(),
            P(),
            P(),
            P("dp", "mp"),
            P("mp"),
            P("dp", None),
            P(),
            P("dp", None),
            P(),
            P("mp", "dp"),
            P(),
            P("dp", "mp"),
            P("mp"),
            P("mp", "dp"),
            P(),
        ),
        check_vma=False,
    )
```

time: 2100 us -> 508 us (0.24)
  waiting for transfers between devices: 1220 us -> 169 us
  matrix products: 443 us -> 50.2 us
  starting transfers between devices: 1.18 us -> 174 us
  local copies, waits for them, and re-layouts: 209 us -> 42 us
  blocking collectives: 102 us -> 0 us
  other arithmetic: 88.9 us -> 38.9 us
  Pallas kernels: 0 us -> 21.7 us
    reduce_scatter x8 -> x0, waiting for transfers between devices: 817 us -> none  [the longest x1 183 us: per_device(): lax.psum_scatter(big_total[7], 'dp', scatter_dimension=1, tiled=True)]
    dot_general x46 -> x22, matrix products: 371 us -> 33.6 us  [the longest x15 22.4 us: product(): return jnp.dot(left, right, preferred_element_type=f32)]
    all_gather x7 -> x0, waiting for transfers between devices: 304 us -> none  [the longest x1 74.9 us: per_device(): lax.all_gather(outward_layer_matrix, 'dp', axis=1, tiled=True)]
    ppermute x0 -> x103, starting transfers between devices: none -> 174 us  [the longest x40 67.8 us: scatter_dim(): got.append(lax.ppermute(parts[k], 'dp', self.shift(dim, k)))]
    ppermute x0 -> x103, waiting for transfers between devices: none -> 169 us  [the longest x40 91 us: gather_dim(): got.append(lax.ppermute(array, 'dp', self.shift(dim, -k)))]
    psum x9 -> x0, waiting for transfers between devices: 94.8 us -> none  [the longest x2 25.1 us: micro_step(): grad_probs = lax.psum(probs_part, 'mp')]
    psum x1 -> x0, blocking collectives: 65.3 us -> none  [per_device(): lax.psum((sum_prenorm, sum_alphas, sum_deltas, sum_expand, sum_readout, s...]
    pad x28 -> x0, local copies, waits for them, and re-layouts: 46.7 us -> none  [ema_apply(): lax.associative_scan(combine_pieces, (full_keep, piece_state))]
  transfers between devices with their start and end apart: 24 -> 103, of which waited for: 19 -> 41; matrix products, arithmetic and copies ran while one was open for 24% -> 24% of each run, Pallas kernels for 0% -> 4%
where the time goes in v1:
time: 508 us; the launch traced here: 499 us
  starting transfers between devices  174 us (34%)
  waiting for transfers between devices  169 us (33%)
  matrix products  50.2 us (10%)
  local copies, waits for them, and re-layouts  42 us (8%)
  other arithmetic  38.9 us (8%)
  Pallas kernels  21.7 us (4%)
    ppermute x40, waiting for transfers between devices, gather_dim(): got.append(lax.ppermute(array, 'dp', self.shift(dim, -k)))  91 us
    ppermute x40, starting transfers between devices, scatter_dim(): got.append(lax.ppermute(parts[k], 'dp', self.shift(dim, k)))  67.8 us
    ppermute x40, waiting for transfers between devices, scatter_dim(): got.append(lax.ppermute(parts[k], 'dp', self.shift(dim, k)))  65.7 us
    ppermute x40, starting transfers between devices, gather_dim(): got.append(lax.ppermute(array, 'dp', self.shift(dim, -k)))  62.6 us
    ppermute x18, starting transfers between devices, swap(): return lax.ppermute(value, 'mp', swap_pairs)  39.5 us
    dot_general x15, matrix products, product(): return jnp.dot(left, right, preferred_element_type=f32)  22.4 us
    unnamed x154, local copies, waits for them, and re-layouts  15.7 us
    pallas_call x1, Pallas kernels, ema_backward(): pl.pallas_call(ema_backward_kernel, name='average_backward', out_shape=(l...  12.8 us
  transfers between devices with their start and end apart: 103, of which 41 were waited for; matrix products, arithmetic and copies ran while one was open for 24% of the time, Pallas kernels for 4%

profile of v1, /device:TPU:1, one launch (start us, length us, event | category | flops | bytes accessed | tf_op | source)
XLA Modules:
  0.0 499.0 jit_solution(11456683896732536936)
XLA Ops:
  18.6 8.9 %average_forward.1 = (f32[128,1024]{1,0:T(8,128)}, f32[128,1024]{1,0:T(8,128)}, bf16[128,1024]{1,0:T(8,128)(2,1)}, bf16[128,1024]{1,0:T(8,128)(2,1)}, f32[128,8,128]{2,1,0:T(8,128)}) custom-call(bf16[128,1024]{1,0:T(8,128)(2,1)} %dynamic-slice_bitcast_fusion.x_ref, f32[1,1024]{1,0:T(1,128)} %bitcast.271, f32[1,1024]{1,0:T(1,128)} %bitcast.273, ...), custom_call_target="tpu_custom_call" | custom-call | flops 20000000 | bytes 3000000 | tf_op jit(solution)/shard_map/average_forward/pallas_call | solution.py:280
  39.8 6.8 %collective-permute-done.5 = bf16[1,1,1,64,1152]{4,3,2,1,0:T(8,128)(2,1)S(1)} collective-permute-done((bf16[1,1,1,64,1152]{4,3,2,1,0:T(8,128)(2,1)S(1)}, bf16[1,1,1,64,1152]{4,3,2,1,0:T(8,128)(2,1)S(1)}, u32[]{:S(2)}, u32[]{:S(2)}) %collective-permute-start.5) | collective-permute-done | bytes 147488 | tf_op jit(solution)/shard_map/ppermute | solution.py:77
  46.7 3.5 collective-permute-start.12
  55.0 5.4 %collective-permute-done.11 = bf16[1,1,1,64,1024]{4,3,2,1,0:T(8,128)(2,1)S(1)} collective-permute-done((bf16[1,1,1,64,1024]{4,3,2,1,0:T(8,128)(2,1)S(1)}, bf16[1,1,1,64,1024]{4,3,2,1,0:T(8,128)(2,1)S(1)}, u32[]{:S(2)}, u32[]{:S(2)}) %collective-permute-start.11) | collective-permute-done | bytes 131104 | tf_op jit(solution)/shard_map/ppermute | solution.py:77
  60.4 3.1 collective-permute-start.20
  66.1 7.5 %collective-permute-done.19 = bf16[1,1,1,64,1024]{4,3,2,1,0:T(8,128)(2,1)S(1)} collective-permute-done((bf16[1,1,1,64,1024]{4,3,2,1,0:T(8,128)(2,1)S(1)}, bf16[1,1,1,64,1024]{4,3,2,1,0:T(8,128)(2,1)S(1)}, u32[]{:S(2)}, u32[]{:S(2)}) %collective-permute-start.19) | collective-permute-done | bytes 131104 | tf_op jit(solution)/shard_map/ppermute | solution.py:77
  73.7 3.1 collective-permute-start.27
  81.7 5.5 %collective-permute-done.26 = bf16[1,1,1,64,1024]{4,3,2,1,0:T(8,128)(2,1)S(1)} collective-permute-done((bf16[1,1,1,64,1024]{4,3,2,1,0:T(8,128)(2,1)S(1)}, bf16[1,1,1,64,1024]{4,3,2,1,0:T(8,128)(2,1)S(1)}, u32[]{:S(2)}, u32[]{:S(2)}) %collective-permute-start.26) | collective-permute-done | bytes 131104 | tf_op jit(solution)/shard_map/ppermute | solution.py:77
  87.3 3.1 collective-permute-start.32
  95.0 5.5 %collective-permute-done.31 = bf16[1,1,1,64,1024]{4,3,2,1,0:T(8,128)(2,1)S(1)} collective-permute-done((bf16[1,1,1,64,1024]{4,3,2,1,0:T(8,128)(2,1)S(1)}, bf16[1,1,1,64,1024]{4,3,2,1,0:T(8,128)(2,1)S(1)}, u32[]{:S(2)}, u32[]{:S(2)}) %collective-permute-start.31) | collective-permute-done | bytes 131104 | tf_op jit(solution)/shard_map/ppermute | solution.py:77
  100.6 3.1 collective-permute-start.37
  108.6 5.6 %collective-permute-done.36 = bf16[1,1,1,64,1024]{4,3,2,1,0:T(8,128)(2,1)S(1)} collective-permute-done((bf16[1,1,1,64,1024]{4,3,2,1,0:T(8,128)(2,1)S(1)}, bf16[1,1,1,64,1024]{4,3,2,1,0:T(8,128)(2,1)S(1)}, u32[]{:S(2)}, u32[]{:S(2)}) %collective-permute-start.36) | collective-permute-done | bytes 131104 | tf_op jit(solution)/shard_map/ppermute | solution.py:77
  116.4 3.1 collective-permute-start.40
  123.4 4.7 collective-permute-start.42
  128.1 5.9 %collective-permute-done.42 = bf16[1,1,1,64,1024]{4,3,2,1,0:T(8,128)(2,1)S(1)} collective-permute-done((bf16[1,1,1,64,1024]{4,3,2,1,0:T(8,128)(2,1)S(1)}, bf16[1,1,1,64,1024]{4,3,2,1,0:T(8,128)(2,1)S(1)}, u32[]{:S(2)}, u32[]{:S(2)}) %collective-permute-start.42) | collective-permute-done | bytes 131104 | tf_op jit(solution)/shard_map/ppermute | solution.py:77
  136.7 3.6 collective-permute-done.33
  146.1 4.8 collective-permute-start.46
  151.7 7.2 %collective-permute-start.15 = (bf16[128,1024]{1,0:T(8,128)(2,1)S(1)}, bf16[128,1024]{1,0:T(8,128)(2,1)S(1)}, u32[]{:S(2)}, u32[]{:S(2)}) collective-permute-start(bf16[128,1024]{1,0:T(8,128)(2,1)S(1)} %copy-done.30), channel_id=1, source_target_pairs={{0,1},{1,0},{2,3},{3,2},{4,5},{5,4},{6,7},{7,6},{8,9},{9,8},{10,11... | collective-permute-start | bytes 786440 | tf_op jit(solution)/shard_map/ppermute | solution.py:352
  163.3 10.7 %collective-permute-done.14 = bf16[4,1,2,64,1024]{4,3,2,1,0:T(8,128)(2,1)S(1)} collective-permute-done((bf16[4,1,2,64,1024]{4,3,2,1,0:T(8,128)(2,1)S(1)}, bf16[4,1,2,64,1024]{4,3,2,1,0:T(8,128)(2,1)S(1)}, u32[]{:S(2)}, u32[]{:S(2)}) %collective-permute-start.14) | collective-permute-done | bytes 1048608 | tf_op jit(solution)/shard_map/ppermute | solution.py:77
  187.5 6.5 %collective-permute-done.22 = bf16[4,2,1,64,1024]{4,3,2,1,0:T(8,128)(2,1)} collective-permute-done((bf16[4,2,1,64,1024]{4,3,2,1,0:T(8,128)(2,1)}, bf16[4,2,1,64,1024]{4,3,2,1,0:T(8,128)(2,1)}, u32[]{:S(2)}, u32[]{:S(2)}) %collective-permute-start.22) | collective-permute-done | bytes 1048608 | tf_op jit(solution)/shard_map/ppermute | solution.py:77
  193.9 4.1 collective-permute-start.9
  200.6 4.2 collective-permute-start.23
  206.5 9.9 %collective-permute-done.34 = bf16[4,2,1,64,1024]{4,3,2,1,0:T(8,128)(2,1)} collective-permute-done((bf16[4,2,1,64,1024]{4,3,2,1,0:T(8,128)(2,1)}, bf16[4,2,1,64,1024]{4,3,2,1,0:T(8,128)(2,1)}, u32[]{:S(2)}, u32[]{:S(2)}) %collective-permute-start.34) | collective-permute-done | bytes 1048608 | tf_op jit(solution)/shard_map/ppermute | solution.py:77
  228.5 10.3 %collective-permute-done.44 = bf16[4,2,1,64,1024]{4,3,2,1,0:T(8,128)(2,1)S(1)} collective-permute-done((bf16[4,2,1,64,1024]{4,3,2,1,0:T(8,128)(2,1)S(1)}, bf16[4,2,1,64,1024]{4,3,2,1,0:T(8,128)(2,1)S(1)}, u32[]{:S(2)}, u32[]{:S(2)}) %collective-permute-start.44) | collective-permute-done | bytes 1048608 | tf_op jit(solution)/shard_map/ppermute | solution.py:77
  245.5 3.2 collective-permute-start.45
  299.0 12.8 %average_backward.1 = (bf16[128,1024]{1,0:T(8,128)(2,1)}, f32[2,1024]{1,0:T(2,128)}, f32[16,8,128]{2,1,0:T(8,128)}, f32[16,8,128]{2,1,0:T(8,128)}) custom-call(bf16[128,1024]{1,0:T(8,128)(2,1)} %dynamic-slice_bitcast_fusion.x_ref, f32[1,1024]{1,0:T(1,128)} %bitcast.272, f32[1,1024]{1,0:T(1,128)} %bitcast.274, f32[16,8,128]{2,1,0:T(8,128)} %bitcast.245, ...), custom_call_target="tpu_custom_call" | custom-call | flops 40000000 | bytes 4000000 | tf_op jit(solution)/shard_map/average_backward/pallas_call | solution.py:298
  333.8 3.3 collective-permute-start.58
  350.2 9.7 %collective-permute-done.99 = bf16[4,1,1,64,1024]{4,3,2,1,0:T(8,128)(2,1)S(1)} collective-permute-done((bf16[4,1,1,64,1024]{4,3,2,1,0:T(8,128)(2,1)S(1)}, bf16[4,1,1,64,1024]{4,3,2,1,0:T(8,128)(2,1)S(1)}, u32[]{:S(2)}, u32[]{:S(2)}) %collective-permute-start.99) | collective-permute-done | bytes 524320 | tf_op jit(solution)/shard_map/ppermute | solution.py:87
  359.9 4.8 collective-permute-start.53
  372.0 3.7 collective-permute-start.102
  375.8 3.2 collective-permute-done.96
  379.0 3.7 collective-permute-start.85
  382.8 7.6 %collective-permute-done.101 = bf16[1,1,1,64,1024]{4,3,2,1,0:T(8,128)(2,1)S(1)} collective-permute-done((bf16[1,1,1,64,1024]{4,3,2,1,0:T(8,128)(2,1)S(1)}, bf16[1,1,1,64,1024]{4,3,2,1,0:T(8,128)(2,1)S(1)}, u32[]{:S(2)}, u32[]{:S(2)}) %collective-permute-start.101) | collective-permute-done | bytes 131104 | tf_op jit(solution)/shard_map/ppermute | solution.py:87
  393.8 7.3 %collective-permute-done.86 = bf16[1,1,1,64,1024]{4,3,2,1,0:T(8,128)(2,1)S(1)} collective-permute-done((bf16[1,1,1,64,1024]{4,3,2,1,0:T(8,128)(2,1)S(1)}, bf16[1,1,1,64,1024]{4,3,2,1,0:T(8,128)(2,1)S(1)}, u32[]{:S(2)}, u32[]{:S(2)}) %collective-permute-start.86) | collective-permute-done | bytes 131104 | tf_op jit(solution)/shard_map/ppermute | solution.py:87
  402.0 7.1 %collective-permute-start.72 = (bf16[4,1,2,64,1024]{4,3,2,1,0:T(8,128)(2,1)S(1)}, bf16[4,1,2,64,1024]{4,3,2,1,0:T(8,128)(2,1)S(1)}, u32[]{:S(2)}, u32[]{:S(2)}) collective-permute-start(bf16[4,1,2,64,1024]{4,3,2,1,0:T(8,128)(2,1)S(1)} %copy-done.21), channel_id=1, source_target_pairs={{0,4},{2,6},{4,0},{6,2},{8,12},{10,14},{12,8},{14,10},{16,20},{18,... | collective-permute-start | bytes 3145736 | tf_op jit(solution)/shard_map/ppermute | solution.py:87
  414.9 6.3 %collective-permute-start.79 = (bf16[4,1,1,64,1024]{4,3,2,1,0:T(8,128)(2,1)S(1)}, bf16[4,1,1,64,1024]{4,3,2,1,0:T(8,128)(2,1)S(1)}, u32[]{:S(2)}, u32[]{:S(2)}) collective-permute-start(bf16[4,1,1,64,1024]{4,3,2,1,0:T(8,128)(2,1)S(1)} %slice.592), channel_id=1, source_target_pairs={{0,4},{2,6},{4,0},{6,2},{8,12},{10,14},{12,8},{14,10},{16,20},{18,... | collective-permute-start | bytes 1572872 | tf_op jit(solution)/shard_map/ppermute | solution.py:87
  423.1 6.2 %collective-permute-done.72 = bf16[4,1,2,64,1024]{4,3,2,1,0:T(8,128)(2,1)S(1)} collective-permute-done((bf16[4,1,2,64,1024]{4,3,2,1,0:T(8,128)(2,1)S(1)}, bf16[4,1,2,64,1024]{4,3,2,1,0:T(8,128)(2,1)S(1)}, u32[]{:S(2)}, u32[]{:S(2)}) %collective-permute-start.72) | collective-permute-done | bytes 1048608 | tf_op jit(solution)/shard_map/ppermute | solution.py:87
  429.8 3.7 collective-permute-done.66
  434.1 6.4 %collective-permute-done.79 = bf16[4,1,1,64,1024]{4,3,2,1,0:T(8,128)(2,1)S(1)} collective-permute-done((bf16[4,1,1,64,1024]{4,3,2,1,0:T(8,128)(2,1)S(1)}, bf16[4,1,1,64,1024]{4,3,2,1,0:T(8,128)(2,1)S(1)}, u32[]{:S(2)}, u32[]{:S(2)}) %collective-permute-start.79) | collective-permute-done | bytes 524320 | tf_op jit(solution)/shard_map/ppermute | solution.py:87
  440.8 4.1 collective-permute-start.80
  446.7 3.1 collective-permute-start.81
  450.0 6.0 %collective-permute-done.73 = bf16[4,1,1,64,1024]{4,3,2,1,0:T(8,128)(2,1)S(1)} collective-permute-done((bf16[4,1,1,64,1024]{4,3,2,1,0:T(8,128)(2,1)S(1)}, bf16[4,1,1,64,1024]{4,3,2,1,0:T(8,128)(2,1)S(1)}, u32[]{:S(2)}, u32[]{:S(2)}) %collective-permute-start.73) | collective-permute-done | bytes 524320 | tf_op jit(solution)/shard_map/ppermute | solution.py:87
  456.0 4.3 collective-permute-start.63
  467.1 3.2 collective-permute-start.70
  473.0 4.5 collective-permute-done.68
  477.5 9.3 %collective-permute-start.75 = (bf16[1,1,1,64,1024]{4,3,2,1,0:T(8,128)(2,1)S(1)}, bf16[1,1,1,64,1024]{4,3,2,1,0:T(8,128)(2,1)S(1)}, u32[]{:S(2)}, u32[]{:S(2)}) collective-permute-start(bf16[1,1,1,64,1024]{4,3,2,1,0:T(8,128)(2,1)S(1)} %get-tuple-element.131), channel_id=1, source_target_pairs={{0,16},{2,18},{4,20},{6,22},{8,24},{10,26},{12,28},{14,30},{16,0},... | collective-permute-start | bytes 393224 | tf_op jit(solution)/shard_map/ppermute | solution.py:87
  486.7 4.5 collective-permute-done.69
  491.3 4.2 collective-permute-start.71
  (491 shorter events, 228.0 us)
Async XLA Ops:
  0.7 32.9 %collective-permute-start.3 = (bf16[1,1,1,64,1024]{4,3,2,1,0:T(8,128)(2,1)}, bf16[1,1,1,64,1024]{4,3,2,1,0:T(8,128)(2,1)S(1)}, u32[]{:S(2)}, u32[]{:S(2)}) collective-permute-start(bf16[1,1,1,64,1024]{4,3,2,1,0:T(8,128)(2,1)} %bitcast.257), channel_id=1, source_target_pairs={{0,8},{2,10},{4,12},{6,14},{8,16},{10,18},{12,20},{14,22},{16,24},... | collective-permute-start | bytes 393224 | tf_op jit(solution)/shard_map/ppermute | solution.py:77
  2.8 30.8 %collective-permute-start.2 = (bf16[1,1,1,64,1024]{4,3,2,1,0:T(8,128)(2,1)}, bf16[1,1,1,64,1024]{4,3,2,1,0:T(8,128)(2,1)S(1)}, u32[]{:S(2)}, u32[]{:S(2)}) collective-permute-start(bf16[1,1,1,64,1024]{4,3,2,1,0:T(8,128)(2,1)} %bitcast.258), channel_id=1, source_target_pairs={{0,16},{2,18},{4,20},{6,22},{8,24},{10,26},{12,28},{14,30},{16,0},... | collective-permute-start | bytes 393224 | tf_op jit(solution)/shard_map/ppermute | solution.py:77
  5.2 28.5 %collective-permute-start.1 = (bf16[1,1,1,64,1024]{4,3,2,1,0:T(8,128)(2,1)}, bf16[1,1,1,64,1024]{4,3,2,1,0:T(8,128)(2,1)S(1)}, u32[]{:S(2)}, u32[]{:S(2)}) collective-permute-start(bf16[1,1,1,64,1024]{4,3,2,1,0:T(8,128)(2,1)} %bitcast.259), channel_id=1, source_target_pairs={{0,24},{2,26},{4,28},{6,30},{8,0},{10,2},{12,4},{14,6},{16,8},{18,... | collective-permute-start | bytes 393224 | tf_op jit(solution)/shard_map/ppermute | solution.py:77
  52.4 38.8 %collective-permute-start.16 = (bf16[4,1,1,64,1024]{4,3,2,1,0:T(8,128)(2,1)S(1)}, bf16[4,1,1,64,1024]{4,3,2,1,0:T(8,128)(2,1)S(1)}, u32[]{:S(2)}, u32[]{:S(2)}) collective-permute-start(bf16[4,1,1,64,1024]{4,3,2,1,0:T(8,128)(2,1)S(1)} %pad_maximum_fusion.11), channel_id=1, source_target_pairs={{0,2},{2,0},{4,6},{6,4},{8,10},{10,8},{12,14},{14,12},{16,18},{18,... | collective-permute-start | bytes 1572872 | tf_op jit(solution)/shard_map/ppermute | solution.py:77
  53.7 52.0 %collective-permute-start.7 = (bf16[4,1,1,64,1152]{4,3,2,1,0:T(8,128)(2,1)S(1)}, bf16[4,1,1,64,1152]{4,3,2,1,0:T(8,128)(2,1)S(1)}, u32[]{:S(2)}, u32[]{:S(2)}) collective-permute-start(bf16[4,1,1,64,1152]{4,3,2,1,0:T(8,128)(2,1)S(1)} %pad_maximum_fusion.9), channel_id=1, source_target_pairs={{0,4},{2,6},{4,0},{6,2},{8,12},{10,14},{12,8},{14,10},{16,20},{18,... | collective-permute-start | bytes 1769480 | tf_op jit(solution)/shard_map/ppermute | solution.py:77
  80.5 39.8 %collective-permute-start.13 = (bf16[4,1,1,64,1024]{4,3,2,1,0:T(8,128)(2,1)S(1)}, bf16[4,1,1,64,1024]{4,3,2,1,0:T(8,128)(2,1)S(1)}, u32[]{:S(2)}, u32[]{:S(2)}) collective-permute-start(bf16[4,1,1,64,1024]{4,3,2,1,0:T(8,128)(2,1)S(1)} %pad_maximum_fusion.12), channel_id=1, source_target_pairs={{0,2},{2,0},{4,6},{6,4},{8,10},{10,8},{12,14},{14,12},{16,18},{18,... | collective-permute-start | bytes 1572872 | tf_op jit(solution)/shard_map/ppermute | solution.py:77
  93.7 41.5 %collective-permute-start.21 = (bf16[4,1,1,64,1024]{4,3,2,1,0:T(8,128)(2,1)S(1)}, bf16[4,1,1,64,1024]{4,3,2,1,0:T(8,128)(2,1)S(1)}, u32[]{:S(2)}, u32[]{:S(2)}) collective-permute-start(bf16[4,1,1,64,1024]{4,3,2,1,0:T(8,128)(2,1)S(1)} %pad_maximum_fusion.14), channel_id=1, source_target_pairs={{0,4},{2,6},{4,0},{6,2},{8,12},{10,14},{12,8},{14,10},{16,20},{18,... | collective-permute-start | bytes 1572872 | tf_op jit(solution)/shard_map/ppermute | solution.py:77
  107.3 52.6 %collective-permute-start.17 = (bf16[4,1,2,64,1024]{4,3,2,1,0:T(8,128)(2,1)S(1)}, bf16[4,1,2,64,1024]{4,3,2,1,0:T(8,128)(2,1)S(1)}, u32[]{:S(2)}, u32[]{:S(2)}) collective-permute-start(bf16[4,1,2,64,1024]{4,3,2,1,0:T(8,128)(2,1)S(1)} %constant_dynamic-update-slice_fusion.4), channel_id=1, source_target_pairs={{0,4},{2,6},{4,0},{6,2},{8,12},{10,14},{12,8},{14,10},{16,20},{18,... | collective-permute-start | bytes 3145736 | tf_op jit(solution)/shard_map/ppermute | solution.py:77
  120.3 16.1 %collective-permute-start.28 = (bf16[4,1,1,64,1024]{4,3,2,1,0:T(8,128)(2,1)S(1)}, bf16[4,1,1,64,1024]{4,3,2,1,0:T(8,128)(2,1)S(1)}, u32[]{:S(2)}, u32[]{:S(2)}) collective-permute-start(bf16[4,1,1,64,1024]{4,3,2,1,0:T(8,128)(2,1)S(1)} %pad_maximum_fusion.16), channel_id=1, source_target_pairs={{0,2},{2,0},{4,6},{6,4},{8,10},{10,8},{12,14},{14,12},{16,18},{18,... | collective-permute-start | bytes 1572872 | tf_op jit(solution)/shard_map/ppermute | solution.py:77
  121.5 18.8 %collective-permute-start.33 = (bf16[4,1,1,64,1024]{4,3,2,1,0:T(8,128)(2,1)S(1)}, bf16[4,1,1,64,1024]{4,3,2,1,0:T(8,128)(2,1)S(1)}, u32[]{:S(2)}, u32[]{:S(2)}) collective-permute-start(bf16[4,1,1,64,1024]{4,3,2,1,0:T(8,128)(2,1)S(1)} %pad_maximum_fusion.17), channel_id=1, source_target_pairs={{0,4},{2,6},{4,0},{6,2},{8,12},{10,14},{12,8},{14,10},{16,20},{18,... | collective-permute-start | bytes 1572872 | tf_op jit(solution)/shard_map/ppermute | solution.py:77
  135.2 16.5 %collective-permute-start.43 = (bf16[4,1,1,64,1024]{4,3,2,1,0:T(8,128)(2,1)S(1)}, bf16[4,1,1,64,1024]{4,3,2,1,0:T(8,128)(2,1)S(1)}, u32[]{:S(2)}, u32[]{:S(2)}) collective-permute-start(bf16[4,1,1,64,1024]{4,3,2,1,0:T(8,128)(2,1)S(1)} %constant_dynamic-update-slice_fusion.14), channel_id=1, source_target_pairs={{0,4},{2,6},{4,0},{6,2},{8,12},{10,14},{12,8},{14,10},{16,20},{18,... | collective-permute-start | bytes 1572872 | tf_op jit(solution)/shard_map/ppermute | solution.py:77
  136.4 40.3 %collective-permute-start.8 = (bf16[4,2,1,64,1152]{4,3,2,1,0:T(8,128)(2,1)S(1)}, bf16[4,2,1,64,1152]{4,3,2,1,0:T(8,128)(2,1)S(1)}, u32[]{:S(2)}, u32[]{:S(2)}) collective-permute-start(bf16[4,2,1,64,1152]{4,3,2,1,0:T(8,128)(2,1)S(1)} %constant_dynamic-update-slice_fusion), channel_id=1, source_target_pairs={{0,2},{2,0},{4,6},{6,4},{8,10},{10,8},{12,14},{14,12},{16,18},{18,... | collective-permute-start | bytes 3538952 | tf_op jit(solution)/shard_map/ppermute | solution.py:77
  140.3 33.7 %collective-permute-start.14 = (bf16[4,1,2,64,1024]{4,3,2,1,0:T(8,128)(2,1)S(1)}, bf16[4,1,2,64,1024]{4,3,2,1,0:T(8,128)(2,1)S(1)}, u32[]{:S(2)}, u32[]{:S(2)}) collective-permute-start(bf16[4,1,2,64,1024]{4,3,2,1,0:T(8,128)(2,1)S(1)} %constant_dynamic-update-slice_fusion.2), channel_id=1, source_target_pairs={{0,4},{2,6},{4,0},{6,2},{8,12},{10,14},{12,8},{14,10},{16,20},{18,... | collective-permute-start | bytes 3145736 | tf_op jit(solution)/shard_map/ppermute | solution.py:77
  146.1 94.4 %collective-permute-start.46 = (bf16[128,1024]{1,0:T(8,128)(2,1)}, bf16[128,1024]{1,0:T(8,128)(2,1)}, u32[]{:S(2)}, u32[]{:S(2)}) collective-permute-start(bf16[128,1024]{1,0:T(8,128)(2,1)} %fusion.30), channel_id=1, source_target_pairs={{0,1},{1,0},{2,3},{3,2},{4,5},{5,4},{6,7},{7,6},{8,9},{9,8},{10,11... | collective-permute-start | bytes 786440 | tf_op jit(solution)/shard_map/ppermute | solution.py:352
  159.9 18.2 %collective-permute-start = (bf16[128,1024]{1,0:T(8,128)(2,1)S(1)}, bf16[128,1024]{1,0:T(8,128)(2,1)S(1)}, u32[]{:S(2)}, u32[]{:S(2)}) collective-permute-start(bf16[128,1024]{1,0:T(8,128)(2,1)S(1)} %copy-done.27), channel_id=1, source_target_pairs={{0,1},{1,0},{2,3},{3,2},{4,5},{5,4},{6,7},{7,6},{8,9},{9,8},{10,11... | collective-permute-start | bytes 786440 | tf_op jit(solution)/shard_map/ppermute | solution.py:352
  160.3 33.6 %collective-permute-start.22 = (bf16[4,2,1,64,1024]{4,3,2,1,0:T(8,128)(2,1)}, bf16[4,2,1,64,1024]{4,3,2,1,0:T(8,128)(2,1)}, u32[]{:S(2)}, u32[]{:S(2)}) collective-permute-start(bf16[4,2,1,64,1024]{4,3,2,1,0:T(8,128)(2,1)} %constant_dynamic-update-slice_fusion.6), channel_id=1, source_target_pairs={{0,2},{2,0},{4,6},{6,4},{8,10},{10,8},{12,14},{14,12},{16,18},{18,... | collective-permute-start | bytes 3145736 | tf_op jit(solution)/shard_map/ppermute | solution.py:77
  174.0 26.6 %collective-permute-start.29 = (bf16[4,1,2,64,1024]{4,3,2,1,0:T(8,128)(2,1)}, bf16[4,1,2,64,1024]{4,3,2,1,0:T(8,128)(2,1)}, u32[]{:S(2)}, u32[]{:S(2)}) collective-permute-start(bf16[4,1,2,64,1024]{4,3,2,1,0:T(8,128)(2,1)} %constant_dynamic-update-slice_fusion.8), channel_id=1, source_target_pairs={{0,4},{2,6},{4,0},{6,2},{8,12},{10,14},{12,8},{14,10},{16,20},{18,... | collective-permute-start | bytes 3145736 | tf_op jit(solution)/shard_map/ppermute | solution.py:77
  176.7 39.7 %collective-permute-start.34 = (bf16[4,2,1,64,1024]{4,3,2,1,0:T(8,128)(2,1)}, bf16[4,2,1,64,1024]{4,3,2,1,0:T(8,128)(2,1)}, u32[]{:S(2)}, u32[]{:S(2)}) collective-permute-start(bf16[4,2,1,64,1024]{4,3,2,1,0:T(8,128)(2,1)} %constant_dynamic-update-slice_fusion.10), channel_id=1, source_target_pairs={{0,2},{2,0},{4,6},{6,4},{8,10},{10,8},{12,14},{14,12},{16,18},{18,... | collective-permute-start | bytes 3145736 | tf_op jit(solution)/shard_map/ppermute | solution.py:77
  178.2 48.5 %collective-permute-start.39 = (bf16[4,1,2,64,1024]{4,3,2,1,0:T(8,128)(2,1)}, bf16[4,1,2,64,1024]{4,3,2,1,0:T(8,128)(2,1)}, u32[]{:S(2)}, u32[]{:S(2)}) collective-permute-start(bf16[4,1,2,64,1024]{4,3,2,1,0:T(8,128)(2,1)} %constant_dynamic-update-slice_fusion.12), channel_id=1, source_target_pairs={{0,4},{2,6},{4,0},{6,2},{8,12},{10,14},{12,8},{14,10},{16,20},{18,... | collective-permute-start | bytes 3145736 | tf_op jit(solution)/shard_map/ppermute | solution.py:77
  193.9 25.5 %collective-permute-start.9 = (f32[128,1024]{1,0:T(8,128)S(1)}, f32[128,1024]{1,0:T(8,128)S(1)}, u32[]{:S(2)}, u32[]{:S(2)}) collective-permute-start(f32[128,1024]{1,0:T(8,128)S(1)} %copy-done.25), channel_id=1, source_target_pairs={{0,1},{1,0},{2,3},{3,2},{4,5},{5,4},{6,7},{7,6},{8,9},{9,8},{10,11... | collective-permute-start | bytes 1572872 | tf_op jit(solution)/shard_map/ppermute | solution.py:352
  200.6 18.9 %collective-permute-start.23 = (f32[128,1024]{1,0:T(8,128)S(1)}, f32[128,1024]{1,0:T(8,128)S(1)}, u32[]{:S(2)}, u32[]{:S(2)}) collective-permute-start(f32[128,1024]{1,0:T(8,128)S(1)} %slice.524), channel_id=1, source_target_pairs={{0,1},{1,0},{2,3},{3,2},{4,5},{5,4},{6,7},{7,6},{8,9},{9,8},{10,11... | collective-permute-start | bytes 1572872 | tf_op jit(solution)/shard_map/ppermute | solution.py:352
  216.4 22.4 %collective-permute-start.44 = (bf16[4,2,1,64,1024]{4,3,2,1,0:T(8,128)(2,1)S(1)}, bf16[4,2,1,64,1024]{4,3,2,1,0:T(8,128)(2,1)S(1)}, u32[]{:S(2)}, u32[]{:S(2)}) collective-permute-start(bf16[4,2,1,64,1024]{4,3,2,1,0:T(8,128)(2,1)S(1)} %copy-done.22), channel_id=1, source_target_pairs={{0,2},{2,0},{4,6},{6,4},{8,10},{10,8},{12,14},{14,12},{16,18},{18,... | collective-permute-start | bytes 3145736 | tf_op jit(solution)/shard_map/ppermute | solution.py:77
  224.1 14.9 %collective-permute-start.24 = (bf16[128,1024]{1,0:T(8,128)(2,1)S(1)}, bf16[128,1024]{1,0:T(8,128)(2,1)S(1)}, u32[]{:S(2)}, u32[]{:S(2)}) collective-permute-start(bf16[128,1024]{1,0:T(8,128)(2,1)S(1)} %fusion.29), channel_id=1, source_target_pairs={{0,1},{1,0},{2,3},{3,2},{4,5},{5,4},{6,7},{7,6},{8,9},{9,8},{10,11... | collective-permute-start | bytes 786440 | tf_op jit(solution)/shard_map/ppermute | solution.py:352
  245.5 17.4 %collective-permute-start.45 = (bf16[128,1024]{1,0:T(8,128)(2,1)S(1)}, bf16[128,1024]{1,0:T(8,128)(2,1)S(1)}, u32[]{:S(2)}, u32[]{:S(2)}) collective-permute-start(bf16[128,1024]{1,0:T(8,128)(2,1)S(1)} %slice.733), channel_id=1, source_target_pairs={{0,1},{1,0},{2,3},{3,2},{4,5},{5,4},{6,7},{7,6},{8,9},{9,8},{10,11... | collective-permute-start | bytes 786440 | tf_op jit(solution)/shard_map/ppermute | solution.py:352
  257.2 36.2 %collective-permute-start.93 = (bf16[4,2,1,64,1024]{4,3,2,1,0:T(8,128)(2,1)S(1)}, bf16[4,2,1,64,1024]{4,3,2,1,0:T(8,128)(2,1)S(1)}, u32[]{:S(2)}, u32[]{:S(2)}) collective-permute-start(bf16[4,2,1,64,1024]{4,3,2,1,0:T(8,128)(2,1)S(1)} %slice.616), channel_id=1, source_target_pairs={{0,2},{2,0},{4,6},{6,4},{8,10},{10,8},{12,14},{14,12},{16,18},{18,... | collective-permute-start | bytes 3145736 | tf_op jit(solution)/shard_map/ppermute | solution.py:87
  258.5 59.4 %collective-permute-start.98 = (bf16[4,2,1,64,1024]{4,3,2,1,0:T(8,128)(2,1)}, bf16[4,2,1,64,1024]{4,3,2,1,0:T(8,128)(2,1)}, u32[]{:S(2)}, u32[]{:S(2)}) collective-permute-start(bf16[4,2,1,64,1024]{4,3,2,1,0:T(8,128)(2,1)} %slice.624), channel_id=1, source_target_pairs={{0,2},{2,0},{4,6},{6,4},{8,10},{10,8},{12,14},{14,12},{16,18},{18,... | collective-permute-start | bytes 3145736 | tf_op jit(solution)/shard_map/ppermute | solution.py:87
  262.7 61.1 %collective-permute-start.83 = (bf16[4,1,2,64,1024]{4,3,2,1,0:T(8,128)(2,1)}, bf16[4,1,2,64,1024]{4,3,2,1,0:T(8,128)(2,1)}, u32[]{:S(2)}, u32[]{:S(2)}) collective-permute-start(bf16[4,1,2,64,1024]{4,3,2,1,0:T(8,128)(2,1)} %slice.599), channel_id=1, source_target_pairs={{0,4},{2,6},{4,0},{6,2},{8,12},{10,14},{12,8},{14,10},{16,20},{18,... | collective-permute-start | bytes 3145736 | tf_op jit(solution)/shard_map/ppermute | solution.py:87
  262.9 66.7 %collective-permute-start.88 = (bf16[4,1,2,64,1024]{4,3,2,1,0:T(8,128)(2,1)}, bf16[4,1,2,64,1024]{4,3,2,1,0:T(8,128)(2,1)}, u32[]{:S(2)}, u32[]{:S(2)}) collective-permute-start(bf16[4,1,2,64,1024]{4,3,2,1,0:T(8,128)(2,1)} %slice.607), channel_id=1, source_target_pairs={{0,4},{2,6},{4,0},{6,2},{8,12},{10,14},{12,8},{14,10},{16,20},{18,... | collective-permute-start | bytes 3145736 | tf_op jit(solution)/shard_map/ppermute | solution.py:87
  294.0 119.1 %collective-permute-start.78 = (bf16[4,2,1,64,1024]{4,3,2,1,0:T(8,128)(2,1)}, bf16[4,2,1,64,1024]{4,3,2,1,0:T(8,128)(2,1)}, u32[]{:S(2)}, u32[]{:S(2)}) collective-permute-start(bf16[4,2,1,64,1024]{4,3,2,1,0:T(8,128)(2,1)} %slice.590), channel_id=1, source_target_pairs={{0,2},{2,0},{4,6},{6,4},{8,10},{10,8},{12,14},{14,12},{16,18},{18,... | collective-permute-start | bytes 3145736 | tf_op jit(solution)/shard_map/ppermute | solution.py:87
  295.4 125.9 %collective-permute-start.61 = (bf16[4,1,2,64,1024]{4,3,2,1,0:T(8,128)(2,1)}, bf16[4,1,2,64,1024]{4,3,2,1,0:T(8,128)(2,1)}, u32[]{:S(2)}, u32[]{:S(2)}) collective-permute-start(bf16[4,1,2,64,1024]{4,3,2,1,0:T(8,128)(2,1)} %slice.552), channel_id=1, source_target_pairs={{0,4},{2,6},{4,0},{6,2},{8,12},{10,14},{12,8},{14,10},{16,20},{18,... | collective-permute-start | bytes 3145736 | tf_op jit(solution)/shard_map/ppermute | solution.py:87
  340.0 19.9 %collective-permute-start.99 = (bf16[4,1,1,64,1024]{4,3,2,1,0:T(8,128)(2,1)S(1)}, bf16[4,1,1,64,1024]{4,3,2,1,0:T(8,128)(2,1)S(1)}, u32[]{:S(2)}, u32[]{:S(2)}) collective-permute-start(bf16[4,1,1,64,1024]{4,3,2,1,0:T(8,128)(2,1)S(1)} %slice.626), channel_id=1, source_target_pairs={{0,4},{2,6},{4,0},{6,2},{8,12},{10,14},{12,8},{14,10},{16,20},{18,... | collective-permute-start | bytes 1572872 | tf_op jit(solution)/shard_map/ppermute | solution.py:87
  343.2 21.7 %collective-permute-start.84 = (bf16[4,1,1,64,1024]{4,3,2,1,0:T(8,128)(2,1)S(1)}, bf16[4,1,1,64,1024]{4,3,2,1,0:T(8,128)(2,1)S(1)}, u32[]{:S(2)}, u32[]{:S(2)}) collective-permute-start(bf16[4,1,1,64,1024]{4,3,2,1,0:T(8,128)(2,1)S(1)} %slice.601), channel_id=1, source_target_pairs={{0,2},{2,0},{4,6},{6,4},{8,10},{10,8},{12,14},{14,12},{16,18},{18,... | collective-permute-start | bytes 1572872 | tf_op jit(solution)/shard_map/ppermute | solution.py:87
  348.7 16.6 %collective-permute-start.89 = (bf16[4,1,1,64,1024]{4,3,2,1,0:T(8,128)(2,1)S(1)}, bf16[4,1,1,64,1024]{4,3,2,1,0:T(8,128)(2,1)S(1)}, u32[]{:S(2)}, u32[]{:S(2)}) collective-permute-start(bf16[4,1,1,64,1024]{4,3,2,1,0:T(8,128)(2,1)S(1)} %slice.609), channel_id=1, source_target_pairs={{0,2},{2,0},{4,6},{6,4},{8,10},{10,8},{12,14},{14,12},{16,18},{18,... | collective-permute-start | bytes 1572872 | tf_op jit(solution)/shard_map/ppermute | solution.py:87
  393.3 15.8 %collective-permute-start.92 = (bf16[1,1,1,64,1024]{4,3,2,1,0:T(8,128)(2,1)S(1)}, bf16[1,1,1,64,1024]{4,3,2,1,0:T(8,128)(2,1)S(1)}, u32[]{:S(2)}, u32[]{:S(2)}) collective-permute-start(bf16[1,1,1,64,1024]{4,3,2,1,0:T(8,128)(2,1)S(1)} %get-tuple-element.124), channel_id=1, source_target_pairs={{0,24},{2,26},{4,28},{6,30},{8,0},{10,2},{12,4},{14,6},{16,8},{18,... | collective-permute-start | bytes 393224 | tf_op jit(solution)/shard_map/ppermute | solution.py:87
  402.0 27.3 %collective-permute-start.72 = (bf16[4,1,2,64,1024]{4,3,2,1,0:T(8,128)(2,1)S(1)}, bf16[4,1,2,64,1024]{4,3,2,1,0:T(8,128)(2,1)S(1)}, u32[]{:S(2)}, u32[]{:S(2)}) collective-permute-start(bf16[4,1,2,64,1024]{4,3,2,1,0:T(8,128)(2,1)S(1)} %copy-done.21), channel_id=1, source_target_pairs={{0,4},{2,6},{4,0},{6,2},{8,12},{10,14},{12,8},{14,10},{16,20},{18,... | collective-permute-start | bytes 3145736 | tf_op jit(solution)/shard_map/ppermute | solution.py:87
  409.1 24.4 %collective-permute-start.66 = (bf16[4,2,1,64,1152]{4,3,2,1,0:T(8,128)(2,1)S(1)}, bf16[4,2,1,64,1152]{4,3,2,1,0:T(8,128)(2,1)S(1)}, u32[]{:S(2)}, u32[]{:S(2)}) collective-permute-start(bf16[4,2,1,64,1152]{4,3,2,1,0:T(8,128)(2,1)S(1)} %copy-done.17), channel_id=1, source_target_pairs={{0,2},{2,0},{4,6},{6,4},{8,10},{10,8},{12,14},{14,12},{16,18},{18,... | collective-permute-start | bytes 3538952 | tf_op jit(solution)/shard_map/ppermute | solution.py:87
  414.9 25.6 %collective-permute-start.79 = (bf16[4,1,1,64,1024]{4,3,2,1,0:T(8,128)(2,1)S(1)}, bf16[4,1,1,64,1024]{4,3,2,1,0:T(8,128)(2,1)S(1)}, u32[]{:S(2)}, u32[]{:S(2)}) collective-permute-start(bf16[4,1,1,64,1024]{4,3,2,1,0:T(8,128)(2,1)S(1)} %slice.592), channel_id=1, source_target_pairs={{0,4},{2,6},{4,0},{6,2},{8,12},{10,14},{12,8},{14,10},{16,20},{18,... | collective-permute-start | bytes 1572872 | tf_op jit(solution)/shard_map/ppermute | solution.py:87
  423.0 23.7 %collective-permute-start.62 = (bf16[4,1,1,64,1024]{4,3,2,1,0:T(8,128)(2,1)S(1)}, bf16[4,1,1,64,1024]{4,3,2,1,0:T(8,128)(2,1)S(1)}, u32[]{:S(2)}, u32[]{:S(2)}) collective-permute-start(bf16[4,1,1,64,1024]{4,3,2,1,0:T(8,128)(2,1)S(1)} %slice.554), channel_id=1, source_target_pairs={{0,2},{2,0},{4,6},{6,4},{8,10},{10,8},{12,14},{14,12},{16,18},{18,... | collective-permute-start | bytes 1572872 | tf_op jit(solution)/shard_map/ppermute | solution.py:87
  429.8 26.2 %collective-permute-start.73 = (bf16[4,1,1,64,1024]{4,3,2,1,0:T(8,128)(2,1)S(1)}, bf16[4,1,1,64,1024]{4,3,2,1,0:T(8,128)(2,1)S(1)}, u32[]{:S(2)}, u32[]{:S(2)}) collective-permute-start(bf16[4,1,1,64,1024]{4,3,2,1,0:T(8,128)(2,1)S(1)} %slice.576), channel_id=1, source_target_pairs={{0,2},{2,0},{4,6},{6,4},{8,10},{10,8},{12,14},{14,12},{16,18},{18,... | collective-permute-start | bytes 1572872 | tf_op jit(solution)/shard_map/ppermute | solution.py:87
  433.9 30.4 %collective-permute-start.67 = (bf16[4,1,1,64,1152]{4,3,2,1,0:T(8,128)(2,1)S(1)}, bf16[4,1,1,64,1152]{4,3,2,1,0:T(8,128)(2,1)S(1)}, u32[]{:S(2)}, u32[]{:S(2)}) collective-permute-start(bf16[4,1,1,64,1152]{4,3,2,1,0:T(8,128)(2,1)S(1)} %slice.563), channel_id=1, source_target_pairs={{0,4},{2,6},{4,0},{6,2},{8,12},{10,14},{12,8},{14,10},{16,20},{18,... | collective-permute-start | bytes 1769480 | tf_op jit(solution)/shard_map/ppermute | solution.py:87
  440.8 19.8 %collective-permute-start.80 = (bf16[1,1,1,64,1024]{4,3,2,1,0:T(8,128)(2,1)S(1)}, bf16[1,1,1,64,1024]{4,3,2,1,0:T(8,128)(2,1)S(1)}, u32[]{:S(2)}, u32[]{:S(2)}) collective-permute-start(bf16[1,1,1,64,1024]{4,3,2,1,0:T(8,128)(2,1)S(1)} %get-tuple-element.126), channel_id=1, source_target_pairs={{0,8},{2,10},{4,12},{6,14},{8,16},{10,18},{12,20},{14,22},{16,24},... | collective-permute-start | bytes 393224 | tf_op jit(solution)/shard_map/ppermute | solution.py:87
  444.8 16.9 %collective-permute-start.82 = (bf16[1,1,1,64,1024]{4,3,2,1,0:T(8,128)(2,1)S(1)}, bf16[1,1,1,64,1024]{4,3,2,1,0:T(8,128)(2,1)S(1)}, u32[]{:S(2)}, u32[]{:S(2)}) collective-permute-start(bf16[1,1,1,64,1024]{4,3,2,1,0:T(8,128)(2,1)S(1)} %get-tuple-element.127), channel_id=1, source_target_pairs={{0,24},{2,26},{4,28},{6,30},{8,0},{10,2},{12,4},{14,6},{16,8},{18,... | collective-permute-start | bytes 393224 | tf_op jit(solution)/shard_map/ppermute | solution.py:87
  446.7 16.1 %collective-permute-start.81 = (bf16[1,1,1,64,1024]{4,3,2,1,0:T(8,128)(2,1)S(1)}, bf16[1,1,1,64,1024]{4,3,2,1,0:T(8,128)(2,1)S(1)}, u32[]{:S(2)}, u32[]{:S(2)}) collective-permute-start(bf16[1,1,1,64,1024]{4,3,2,1,0:T(8,128)(2,1)S(1)} %get-tuple-element.128), channel_id=1, source_target_pairs={{0,16},{2,18},{4,20},{6,22},{8,24},{10,26},{12,28},{14,30},{16,0},... | collective-permute-start | bytes 393224 | tf_op jit(solution)/shard_map/ppermute | solution.py:87
  462.8 32.8 %collective-permute-start.74 = (bf16[1,1,1,64,1024]{4,3,2,1,0:T(8,128)(2,1)S(1)}, bf16[1,1,1,64,1024]{4,3,2,1,0:T(8,128)(2,1)S(1)}, u32[]{:S(2)}, u32[]{:S(2)}) collective-permute-start(bf16[1,1,1,64,1024]{4,3,2,1,0:T(8,128)(2,1)S(1)} %get-tuple-element.129), channel_id=1, source_target_pairs={{0,8},{2,10},{4,12},{6,14},{8,16},{10,18},{12,20},{14,22},{16,24},... | collective-permute-start | bytes 393224 | tf_op jit(solution)/shard_map/ppermute | solution.py:87
  464.3 31.4 %collective-permute-start.76 = (bf16[1,1,1,64,1024]{4,3,2,1,0:T(8,128)(2,1)S(1)}, bf16[1,1,1,64,1024]{4,3,2,1,0:T(8,128)(2,1)S(1)}, u32[]{:S(2)}, u32[]{:S(2)}) collective-permute-start(bf16[1,1,1,64,1024]{4,3,2,1,0:T(8,128)(2,1)S(1)} %get-tuple-element.130), channel_id=1, source_target_pairs={{0,24},{2,26},{4,28},{6,30},{8,0},{10,2},{12,4},{14,6},{16,8},{18,... | collective-permute-start | bytes 393224 | tf_op jit(solution)/shard_map/ppermute | solution.py:87
  467.1 19.6 %collective-permute-start.70 = (bf16[1,1,1,64,1152]{4,3,2,1,0:T(8,128)(2,1)S(1)}, bf16[1,1,1,64,1152]{4,3,2,1,0:T(8,128)(2,1)S(1)}, u32[]{:S(2)}, u32[]{:S(2)}) collective-permute-start(bf16[1,1,1,64,1152]{4,3,2,1,0:T(8,128)(2,1)S(1)} %get-tuple-element.107), channel_id=1, source_target_pairs={{0,24},{2,26},{4,28},{6,30},{8,0},{10,2},{12,4},{14,6},{16,8},{18,... | collective-permute-start | bytes 442376 | tf_op jit(solution)/shard_map/ppermute | solution.py:87
  472.2 19.0 %collective-permute-start.69 = (bf16[1,1,1,64,1152]{4,3,2,1,0:T(8,128)(2,1)S(1)}, bf16[1,1,1,64,1152]{4,3,2,1,0:T(8,128)(2,1)S(1)}, u32[]{:S(2)}, u32[]{:S(2)}) collective-permute-start(bf16[1,1,1,64,1152]{4,3,2,1,0:T(8,128)(2,1)S(1)} %get-tuple-element.108), channel_id=1, source_target_pairs={{0,16},{2,18},{4,20},{6,22},{8,24},{10,26},{12,28},{14,30},{16,0},... | collective-permute-start | bytes 442376 | tf_op jit(solution)/shard_map/ppermute | solution.py:87
  477.5 18.2 %collective-permute-start.75 = (bf16[1,1,1,64,1024]{4,3,2,1,0:T(8,128)(2,1)S(1)}, bf16[1,1,1,64,1024]{4,3,2,1,0:T(8,128)(2,1)S(1)}, u32[]{:S(2)}, u32[]{:S(2)}) collective-permute-start(bf16[1,1,1,64,1024]{4,3,2,1,0:T(8,128)(2,1)S(1)} %get-tuple-element.131), channel_id=1, source_target_pairs={{0,16},{2,18},{4,20},{6,22},{8,24},{10,26},{12,28},{14,30},{16,0},... | collective-permute-start | bytes 393224 | tf_op jit(solution)/shard_map/ppermute | solution.py:87
  (123 other events, 850.8 us)

commit v2 on v1

v2 whole, which is shorter than its diff:
```python
import functools

import jax
import jax.numpy as jnp
from jax import lax
from jax.experimental import pallas as pl
from jax.experimental.pallas import tpu as pltpu
from jax.sharding import PartitionSpec as P

COMMON_SPAN_DIM = 128
SPAN = 128
LANES = 128
SUBLANES = 8

epsilon = 1e-05
bf16 = jnp.bfloat16
f32 = jnp.float32


def product(left, right):
    return jnp.dot(left, right, preferred_element_type=f32)


def left_inner(left, right):
    return lax.dot_general(left, right, (((0,), (0,)), ((), ())), preferred_element_type=f32)


def right_inner(left, right):
    return lax.dot_general(left, right, (((1,), (1,)), ((), ())), preferred_element_type=f32)


def silu_slope(values):
    sigma = jax.nn.sigmoid(values)
    return sigma * (1.0 + values * (1.0 - sigma))


def radices_of(n):
    found = []
    left = n // 2
    while left > 1:
        r = 4 if left % 4 == 0 or not found and left > 4 else 2
        r = r if left % r == 0 else left
        found.append(r)
        left //= r
    while len(found) < 2:
        found.append(1)
    return tuple(found) + (2,)


class Grid:
    def __init__(self, n):
        self.n = n
        radix = radices_of(n)
        strides, left = [], n
        for r in radix:
            left //= r
            strides.append(left)
        self.radix = radix[1:-1] + radix[:1] + radix[-1:]
        self.stride = tuple(strides[1:-1] + strides[:1] + strides[-1:])
        self.near = len(radix) - 1
        self.line = len(radix) - 2

    def shift(self, dim, k):
        pairs = []
        for source in range(self.n):
            at = (source // self.stride[dim]) % self.radix[dim]
            to = (at + k) % self.radix[dim]
            pairs.append((source, source + (to - at) * self.stride[dim]))
        return pairs

    def fetch(self, array, dim):
        return [array] + [
            lax.ppermute(array, "dp", self.shift(dim, -k)) for k in range(1, self.radix[dim])
        ]

    def deliver(self, parts, dim):
        return [parts[0]] + [
            lax.ppermute(parts[k], "dp", self.shift(dim, k)) for k in range(1, self.radix[dim])
        ]

    def near_index(self):
        return lax.axis_index("dp") % 2

    def near_swap(self, value):
        return lax.ppermute(value, "dp", self.shift(self.near, 1))

    def sum_all(self, value):
        for dim, r in reversed(list(enumerate(self.radix))):
            got = self.fetch(value, dim)
            if r == 4:
                value = (got[0] + got[2]) + (got[1] + got[3])
            elif r == 2:
                value = got[0] + got[1]
            elif r > 2:
                value = lax.psum(value, "dp", axis_index_groups=self.groups(dim))
        return value

    def groups(self, dim):
        lines = {}
        for i in range(self.n):
            at = (i // self.stride[dim]) % self.radix[dim]
            lines.setdefault(i - at * self.stride[dim], []).append(i)
        return list(lines.values())

    def permutation(self, width):
        rows = width // self.n
        me = lax.axis_index("dp")
        place = jnp.arange(width)
        block = place // rows
        absolute = place % rows + (block % 2) * rows
        block = block // 2
        for s, r in list(zip(self.stride, self.radix))[-2::-1]:
            absolute = absolute + ((block % r + (me // s) % r) % r) * (s * rows)
            block = block // r
        return (jnp.arange(width)[:, None] == absolute[None, :]).astype(bf16)


def total_of(parts):
    total = parts[0].astype(f32)
    for p in parts[1:]:
        total = total + p.astype(f32)
    return total


def tie(values):
    return lax.optimization_barrier(values)


class Gather:
    def __init__(self, grid, mine, theirs):
        self.grid = grid
        near = grid.near_index()
        pack = functools.partial(jnp.concatenate, axis=1)
        kept = [pack(chunk) for chunk in mine]
        sent = [pack(chunk) for chunk in theirs]

        def beside(own, other):
            return jnp.stack([jnp.where(near == 0, own, other), jnp.where(near == 0, other, own)])

        first = beside(kept[0], grid.near_swap(sent[0]))
        rest = pack(sent[1:])
        first, rest = tie((first, rest))
        rest = grid.near_swap(rest)
        self.state, at = [first], 0
        for own in kept[1:]:
            self.state.append(beside(own, rest[:, at : at + own.shape[1]]))
            at += own.shape[1]
        self.middle = list(range(grid.line - 1, -1, -1))
        self.weights = {}
        self.stage = 0

    def advance(self, held=None):
        stage, count = self.stage, len(self.state)
        active = [k for k in range(count) if 0 <= stage - k <= len(self.middle)]
        last = stage - 1 - len(self.middle)
        done = self.weights[last] if last in self.weights else []
        if stage:
            tied, done, held = tie(([self.state[k] for k in active], done, held))
            for k, value in zip(active, tied):
                self.state[k] = value
            if last in self.weights:
                self.weights[last] = done
        for k in active:
            step = stage - k
            dim = self.grid.line if step == 0 else self.middle[step - 1]
            got = self.grid.fetch(self.state[k], dim)
            if step < len(self.middle):
                self.state[k] = jnp.stack(got)
            else:
                self.weights[k] = [g.reshape(-1, g.shape[-1]) for g in got]
        self.stage += 1
        return held

    def until(self, k):
        while k not in self.weights:
            self.advance()


class Moving:
    def __init__(self, grid, parts):
        self.grid = grid
        shape = grid.radix[1:] + (-1, parts[0].shape[-1])
        self.parts = [p.reshape(shape) for p in parts]
        self.value = None

    def across(self):
        self.value = total_of(self.grid.deliver(self.parts, 0))
        for dim in range(1, self.grid.line):
            value = self.value.astype(bf16)
            self.value = total_of(
                self.grid.deliver([value[k] for k in range(self.grid.radix[dim])], dim)
            )
        self.value = self.value.astype(bf16)

    def along(self):
        parts = [self.value[k] for k in range(self.grid.radix[self.grid.line])]
        self.value = total_of(self.grid.deliver(parts, self.grid.line))

    def near(self):
        near = self.grid.near_index()
        kept = lax.dynamic_index_in_dim(self.value, near, 0, keepdims=False)
        sent = lax.dynamic_index_in_dim(self.value, 1 - near, 0, keepdims=False)
        return kept, self.grid.near_swap(sent.astype(bf16)).astype(f32)


def tiles_of(array):
    return [array[i * SUBLANES : (i + 1) * SUBLANES] for i in range(array.shape[0] // SUBLANES)]


def row_tile(table_ref, lag, c):
    row = table_ref[lag, pl.ds(c, 1), :]
    return jnp.broadcast_to(row, (SUBLANES, LANES))


def norm_parts(x_ref):
    values = x_ref[...].astype(f32)
    center = values - jnp.mean(values, axis=-1, keepdims=True)
    scale = lax.rsqrt(jnp.mean(center * center, axis=-1, keepdims=True) + epsilon)
    return center * scale, scale


def sigma_of(values):
    return jax.nn.sigmoid(values)


def call(kernel, name, out, operands, scalars=0, scratch=()):
    specs = [pl.BlockSpec(memory_space=pltpu.SMEM)] * scalars
    specs += [pl.BlockSpec(memory_space=pltpu.VMEM)] * (len(operands) - scalars)
    return pl.pallas_call(
        kernel,
        name=name,
        out_shape=[jax.ShapeDtypeStruct(shape, dtype) for shape, dtype in out],
        in_specs=specs,
        out_specs=[pl.BlockSpec(memory_space=pltpu.VMEM)] * len(out),
        scratch_shapes=list(scratch),
        cost_estimate=pl.CostEstimate(flops=1, bytes_accessed=1, transcendentals=0),
    )(*operands)


def times(x, blocks, start, stop):
    total, at = None, 0
    for w in blocks:
        rows = w.shape[0]
        term = product(x[:, at : at + rows], w[:, start:stop])
        total = term if total is None else total + term
        at += rows
    return total


def times_t(x, blocks, start, stop):
    return jnp.concatenate([right_inner(x, w[:, start:stop]) for w in blocks], axis=1)


def to_absolute(value, spread):
    high = value.astype(bf16)
    low = (value - high.astype(f32)).astype(bf16)
    return right_inner(high, spread) + right_inner(low, spread)


def column_sum(values):
    return jnp.sum(values, axis=0, keepdims=True)


def ema_forward_kernel(
    place_ref, x_ref, seed_ref, gain_ref, direct_ref, params_ref, spread_ref,
    normed_ref, pre_ref, packed_ref, seed_low_ref, table_ref, seed_sum_ref,
):
    steps, width = x_ref.shape
    spread = spread_ref[...]
    hat, unused = norm_parts(x_ref)
    normed = hat * gain_ref[...]
    normed_ref[...] = normed
    packed_ref[:, width:] = product(normed.astype(bf16), spread).astype(bf16)
    live = lax.broadcasted_iota(jnp.int32, (steps, 1), 0) < place_ref[2]
    seed = jnp.where(live, seed_ref[...].astype(f32), 0.0)
    seed_sum_ref[...] = column_sum(seed)
    seed_low_ref[...] = product(seed.astype(bf16), spread).astype(bf16)
    rate = jax.nn.sigmoid(params_ref[0])
    keep = 1.0 - rate * jax.nn.sigmoid(params_ref[1])
    weight = params_ref[3] * (rate * params_ref[2])

    def lag_step(lag, power):
        table_ref[lag] = jnp.sum(weight * power, axis=0)
        return power * keep

    lax.fori_loop(0, steps, lag_step, jnp.ones_like(keep))
    count = steps // SUBLANES
    sub = lax.broadcasted_iota(jnp.int32, (steps, LANES), 0)

    def block(c, carry):
        columns = pl.ds(pl.multiple_of(c * LANES, LANES), LANES)
        base = normed_ref[:, columns]
        total = [jnp.zeros((SUBLANES, LANES), f32)] * count
        for r in range(SUBLANES):
            moved = base if r == 0 else jnp.where(sub >= r, pltpu.roll(base, r, 0), 0.0)
            moved = tiles_of(moved)
            for q in range(count):
                w = row_tile(table_ref, q * SUBLANES + r, c)
                for i in range(q, count):
                    total[i] = total[i] + w * moved[i - q]
        pre_ref[:, columns] = jnp.concatenate(total, axis=0) + direct_ref[:, columns] * base
        return carry

    lax.fori_loop(0, width // LANES, block, 0)
    pre = pre_ref[...]
    packed_ref[:, :width] = product((pre * jax.nn.sigmoid(pre)).astype(bf16), spread).astype(bf16)


def ema_backward_kernel(
    place_ref,
    x_ref, gain_ref, direct_ref, params_ref, spread_ref, table_ref, normed_ref, pre_ref,
    kept_ref, core_ref, near_ref, grad_shared_ref, grad_input_ref,
    down_kept_ref, down_core_ref, down_near_ref, blended_ref, offset_ref, *rest,
):
    weights = rest[:-8]
    (
        grad_row_ref, out_row_ref, vectors_ref, zero_ref, first_ref,
        smooth_ref, inner_ref, lag_ref,
    ) = rest[-8:]
    steps, width = x_ref.shape
    count = steps // SUBLANES
    sub = lax.broadcasted_iota(jnp.int32, (steps, LANES), 0)
    spread = spread_ref[...]

    down = down_kept_ref[:steps] + down_core_ref[:steps].astype(f32) + down_near_ref[...].astype(f32)
    down = right_inner(down.astype(bf16), spread)
    live = lax.broadcasted_iota(jnp.int32, (steps, 1), 0) < place_ref[2]
    out = blended_ref[...] + down + offset_ref[...]
    out_row_ref[...] = jnp.where(live, out, 0.0).astype(bf16)

    sums = kept_ref[:steps] + core_ref[:steps].astype(f32) + near_ref[...].astype(f32)
    span = weights[0].shape[1] - LANES
    smooth = sums[:, :width] + times_t(grad_shared_ref[...], weights, span, span + LANES)
    smooth_ref[...] = to_absolute(smooth, spread)
    inner_ref[...] = to_absolute(sums[:, width:], spread)

    def block(c, carry):
        columns = pl.ds(pl.multiple_of(c * LANES, LANES), LANES)
        pre = pre_ref[:, columns]
        grad_pre = smooth_ref[:, columns] * silu_slope(pre)
        normed = normed_ref[:, columns]
        vectors_ref[1:2, columns] = column_sum(grad_pre * normed)
        own = tiles_of(normed)
        total = tiles_of(inner_ref[:, columns] + direct_ref[:, columns] * grad_pre)
        for r in range(SUBLANES):
            moved = grad_pre
            if r:
                moved = jnp.where(sub < steps - r, pltpu.roll(grad_pre, steps - r, 0), 0.0)
            moved = tiles_of(moved)
            for q in range(count):
                w = row_tile(table_ref, q * SUBLANES + r, c)
                lag_sum = jnp.zeros((SUBLANES, LANES), f32)
                for i in range(count - q):
                    g = moved[i + q]
                    total[i] = total[i] + w * g
                    lag_sum = lag_sum + g * own[i]
                lag_ref[q * SUBLANES + r, pl.ds(c, 1), :] = column_sum(lag_sum)
        inner_ref[:, columns] = jnp.concatenate(total, axis=0)
        return carry

    lax.fori_loop(0, width // LANES, block, 0)

    keep_all = 1.0 - jax.nn.sigmoid(params_ref[0]) * jax.nn.sigmoid(params_ref[1])
    half = keep_all.shape[0] // 2
    for h in range(2):
        keep = keep_all[h * half : (h + 1) * half]

        def lag_step(lag, carry):
            power, zero, first = carry
            g = lag_ref[lag]
            first = first + (g * lag.astype(f32))[None] * power
            power = power * keep
            return (power, zero + g[None] * power, first)

        blank = jnp.zeros_like(keep)
        start = (jnp.ones_like(keep), blank + lag_ref[0][None], blank)
        unused, zero, first = lax.fori_loop(1, steps, lag_step, start)
        zero_ref[h * half : (h + 1) * half] = zero
        first_ref[h * half : (h + 1) * half] = first

    hat, scale = norm_parts(x_ref)
    grad = inner_ref[...]
    vectors_ref[0:1] = column_sum(grad * hat)
    grad = grad * gain_ref[...]
    grad = grad - jnp.mean(grad, axis=-1, keepdims=True) - hat * jnp.mean(
        grad * hat, axis=-1, keepdims=True
    )
    grad_row_ref[...] = (grad_input_ref[...] + scale * grad).astype(bf16)


def attention_kernel(
    place_ref, p0, p1, p2, p3, value_offset_ref, common_offset_ref, ask_gain_ref, ask_offset_ref,
    look_gain_ref, *rest,
):
    weights = rest[:-10]
    (
        value_pre_ref, value_ref, gates_kept_ref, gates_sent_ref, probs_low_ref, attended_ref,
        shared_pre_ref, query_ref, key_ref, probs_ref,
    ) = rest[-10:]
    steps = p0.shape[0]
    width = p0.shape[1] // 2
    span = value_ref.shape[1]
    gates_size = gates_kept_ref.shape[1]
    at = lax.broadcasted_iota(jnp.int32, (steps, steps), 0)
    to = lax.broadcasted_iota(jnp.int32, (steps, steps), 1)
    for p, packed in enumerate((p0, p1, p2, p3)):
        here = slice(p * steps, (p + 1) * steps)
        smooth = packed[:, :width]
        value_pre = times(packed[:, width:], weights, 0, span) + value_offset_ref[...]
        value_pre_ref[here] = value_pre
        value = (value_pre * sigma_of(value_pre)).astype(bf16)
        value_ref[here] = value
        gates = times(smooth, weights, span, span + gates_size)
        half = slice((p % 2) * steps, (p % 2 + 1) * steps)
        if p < 2:
            gates_kept_ref[half] = gates
        else:
            gates_sent_ref[half] = gates
        start = span + gates_size
        shared_pre = times(smooth, weights, start, start + LANES) + common_offset_ref[...]
        shared = shared_pre * sigma_of(shared_pre)
        query = (shared * ask_gain_ref[...] + ask_offset_ref[...]).astype(bf16)
        key = (shared * look_gain_ref[...]).astype(bf16)
        scores = right_inner(query, key) * (COMMON_SPAN_DIM ** (-0.5))
        allowed = (to <= at) & ((to < place_ref[2 + p]) | (to == at))
        scores = jnp.where(allowed, scores, -1e30)
        probs = jnp.exp(scores - jnp.max(scores, axis=-1, keepdims=True))
        probs = probs / jnp.sum(probs, axis=-1, keepdims=True)
        probs_low = probs.astype(bf16)
        probs_low_ref[here] = probs_low
        attended_ref[here] = product(probs_low, value)
        if p == 0:
            shared_pre_ref[...] = shared_pre
            query_ref[...] = query
            key_ref[...] = key
            probs_ref[...] = probs


def mix_kernel(p0, p1, p2, p3, offset_ref, attended_ref, *rest):
    weights = rest[:-4]
    reset_pre_ref, mixed_ref, kept_ref, sent_ref = rest[-4:]
    steps = p0.shape[0]
    width = p0.shape[1] // 2
    span = mixed_ref.shape[1]
    for p, packed in enumerate((p0, p1, p2, p3)):
        here = slice(p * steps, (p + 1) * steps)
        reset_pre = times(packed[:, :width], weights, 0, span) + offset_ref[...]
        reset_pre_ref[here] = reset_pre
        mixed = (reset_pre * sigma_of(reset_pre) * attended_ref[here]).astype(bf16)
        mixed_ref[here] = mixed
        part = times_t(mixed, weights, span, 2 * span)
        half = slice((p % 2) * steps, (p % 2 + 1) * steps)
        if p < 2:
            kept_ref[half] = part
        else:
            sent_ref[half] = part.astype(bf16)


def pick(index, own, other):
    zero = index == 0
    return [jnp.where(zero, own, other), jnp.where(zero, other, own)]


def hidden_kernel(
    place_ref, x_ref, kept_ref, core_ref, near_ref, gates_ref, gates_core_ref, gates_near_ref,
    update_offset_ref, hidden_offset_ref, gain_ref, spread_ref,
    hidden_pre_ref, update_ref, blended_ref, hat_ref, scale_ref, low_ref,
):
    steps = x_ref.shape[0]
    spread = spread_ref[...]
    part = kept_ref[:steps] + core_ref[:steps].astype(f32) + near_ref[...].astype(f32)
    size = gates_ref.shape[1] // 2
    sides = []
    for c, own in enumerate((gates_ref[:steps], gates_core_ref[:steps])):
        other = gates_near_ref[:, c * 2 * size : (c + 1) * 2 * size].astype(f32)
        sides.append(
            [
                jnp.concatenate(
                    pick(place_ref[0], own[:, k * size : (k + 1) * size], other[:, k * size : (k + 1) * size]),
                    axis=1,
                )
                for k in range(2)
            ]
        )
    whole = [jnp.concatenate(pick(place_ref[1], sides[0][k], sides[1][k]), axis=1) for k in range(2)]
    update = sigma_of(whole[0] + update_offset_ref[...])
    hidden_pre = whole[1] + hidden_offset_ref[...] + to_absolute(part, spread)
    hidden = hidden_pre * sigma_of(hidden_pre)
    values = x_ref[...].astype(f32)
    blended = values + update * (hidden - values)
    center = blended - jnp.mean(blended, axis=-1, keepdims=True)
    scale = lax.rsqrt(jnp.mean(center * center, axis=-1, keepdims=True) + epsilon)
    hat = center * scale
    hidden_pre_ref[...] = hidden_pre
    update_ref[...] = update
    blended_ref[...] = blended
    hat_ref[...] = hat
    scale_ref[...] = scale
    low_ref[...] = product((hat * gain_ref[...]).astype(bf16), spread).astype(bf16)


def ffn_kernel(first, count, *refs):
    f = refs[:4]
    seeds = refs[4:8]
    offset_ref = refs[8]
    at = 9
    if not first:
        down_before_ref, back_before_ref = refs[9:11]
        at = 11
    weights = refs[at : at + count]
    outs = refs[at + count :]
    grad_pre_ref, act_ref, bias_ref = outs[:3]
    steps = f[0].shape[0]
    width = f[0].shape[1]
    span = act_ref.shape[1]
    for p in range(4):
        here = slice(p * steps, (p + 1) * steps)
        pre = times(f[p][...], weights, 0, span) + offset_ref[...]
        sigma = sigma_of(pre)
        act = (pre * sigma).astype(bf16)
        act_ref[here] = act
        grad = times(seeds[p][...], weights, span, 2 * span)
        grad = (grad * (sigma * (1.0 + pre * (1.0 - sigma)))).astype(bf16)
        grad_pre_ref[here] = grad
        bias = column_sum(grad.astype(f32))
        bias_ref[...] = bias if p == 0 else bias_ref[...] + bias
        down = times_t(act, weights, span, 2 * span)
        back = times_t(grad, weights, 0, span)
        if first:
            down_ref, back_ref = outs[3:5]
            down_ref[here] = down
            back_ref[here] = back
            continue
        down = down + down_before_ref[here]
        back = back + back_before_ref[here]
        down_kept_ref, down_sent_ref, back_kept_ref, back_sent_ref = outs[3:7]
        half = slice((p % 2) * steps, (p % 2 + 1) * steps)
        if p < 2:
            down_kept_ref[half] = down
            back_kept_ref[half] = back
        else:
            down_sent_ref[half] = down.astype(bf16)
            back_sent_ref[half] = back.astype(bf16)


def blend_grad_kernel(
    place_ref, x_ref, seed_ref, kept_ref, core_ref, near_ref, hidden_pre_ref, update_ref, hat_ref,
    scale_ref, gain_ref, spread_ref,
    grad_input_ref, hidden_low_ref, update_low_ref, sums_ref,
):
    steps = x_ref.shape[0]
    spread = spread_ref[...]
    part = kept_ref[:steps] + core_ref[:steps].astype(f32) + near_ref[...].astype(f32)
    grad_norm = to_absolute(part, spread)
    hat = hat_ref[...]
    grad_hat = grad_norm * gain_ref[...]
    live = lax.broadcasted_iota(jnp.int32, (steps, 1), 0) < place_ref[2]
    seed = jnp.where(live, seed_ref[...].astype(f32), 0.0)
    grad_blended = seed + scale_ref[...] * (
        grad_hat
        - jnp.mean(grad_hat, axis=-1, keepdims=True)
        - hat * jnp.mean(grad_hat * hat, axis=-1, keepdims=True)
    )
    update = update_ref[...]
    hidden_pre = hidden_pre_ref[...]
    sigma = sigma_of(hidden_pre)
    values = x_ref[...].astype(f32)
    grad_input_ref[...] = grad_blended * (1.0 - update)
    grad_hidden = (
        grad_blended * update * (sigma * (1.0 + hidden_pre * (1.0 - sigma)))
    ).astype(bf16)
    grad_update = (
        grad_blended * (hidden_pre * sigma - values) * update * (1.0 - update)
    ).astype(bf16)
    hidden_low_ref[...] = product(grad_hidden, spread).astype(bf16)
    update_low_ref[...] = grad_update
    sums_ref[0:1] = column_sum(grad_update.astype(f32))
    sums_ref[1:2] = column_sum(grad_hidden.astype(f32))
    sums_ref[2:3] = column_sum(grad_norm * hat)


def attention_grad_kernel(
    h0, h1, h2, h3, reset_pre_ref, attended_ref, value_ref, value_pre_ref, probs_low_ref, *rest,
):
    weights = rest[:-5]
    grad_reset_ref, grad_value_ref, kept_ref, sent_ref, sums_ref = rest[-5:]
    steps = h0.shape[0]
    span = value_ref.shape[1]
    for p, h in enumerate((h0, h1, h2, h3)):
        here = slice(p * steps, (p + 1) * steps)
        grad_mixed = times(h[...], weights, span, 2 * span)
        reset_pre = reset_pre_ref[here]
        sigma = sigma_of(reset_pre)
        grad_attended = (grad_mixed * (reset_pre * sigma)).astype(bf16)
        grad_reset = (
            grad_mixed * attended_ref[here] * (sigma * (1.0 + reset_pre * (1.0 - sigma)))
        ).astype(bf16)
        grad_reset_ref[here] = grad_reset
        part = right_inner(grad_attended, value_ref[here])
        half = slice((p % 2) * steps, (p % 2 + 1) * steps)
        if p < 2:
            kept_ref[half] = part
        else:
            sent_ref[half] = part
        grad_value = left_inner(probs_low_ref[here], grad_attended)
        grad_value = (grad_value * silu_slope(value_pre_ref[here])).astype(bf16)
        grad_value_ref[here] = grad_value
        terms = (column_sum(grad_value.astype(f32)), column_sum(grad_reset.astype(f32)))
        for k, term in enumerate(terms):
            row = slice(k, k + 1)
            sums_ref[row] = term if p == 0 else sums_ref[row] + term


def input_grad_kernel(count, place_ref, *refs):
    h = refs[:4]
    u = refs[4:8]
    grad_reset_ref, grad_value_ref, spread_ref = refs[8:11]
    first = refs[11 : 11 + count]
    second = refs[11 + count : 11 + 2 * count]
    gates_ref, kept_ref, sent_ref = refs[11 + 2 * count :]
    steps, width = h[0].shape
    span = grad_value_ref.shape[1]
    size = gates_ref.shape[1] // 2
    gate = pl.ds(pl.multiple_of(place_ref[6], size), size)
    rows = spread_ref[gate, :]
    for p in range(4):
        here = slice(p * steps, (p + 1) * steps)
        gates = jnp.concatenate(
            [u[p][:, gate], right_inner(h[p][...], rows).astype(bf16)], axis=1
        )
        gates_ref[here] = gates
        smooth = times_t(grad_reset_ref[here], second, 0, span) + times_t(
            gates, first, span, span + 2 * size
        )
        norm = times_t(grad_value_ref[here], first, 0, span)
        half = slice((p % 2) * steps, (p % 2 + 1) * steps)
        if p < 2:
            kept_ref[half, :width] = smooth
            kept_ref[half, width:] = norm
        else:
            sent_ref[half, :width] = smooth.astype(bf16)
            sent_ref[half, width:] = norm.astype(bf16)


def score_grad_kernel(
    kept_ref, core_ref, near_ref, probs_ref, query_ref, key_ref, shared_pre_ref, ask_gain_ref,
    look_gain_ref, grad_shared_ref, sums_ref,
):
    steps = probs_ref.shape[0]
    grad_probs = kept_ref[:steps] + core_ref[:steps] + near_ref[...]
    probs = probs_ref[...]
    grad_scores = (
        probs * (grad_probs - jnp.sum(grad_probs * probs, axis=-1, keepdims=True))
    ).astype(bf16)
    scale = COMMON_SPAN_DIM ** (-0.5)
    grad_query = product(grad_scores, key_ref[...]) * scale
    grad_key = left_inner(grad_scores, query_ref[...]) * scale
    shared_pre = shared_pre_ref[...]
    sigma = sigma_of(shared_pre)
    shared = shared_pre * sigma
    grad_shared = (
        (grad_query * ask_gain_ref[...] + grad_key * look_gain_ref[...])
        * (sigma * (1.0 + shared_pre * (1.0 - sigma)))
    ).astype(bf16)
    grad_shared_ref[...] = grad_shared
    sums_ref[0:1] = column_sum(grad_shared.astype(f32))
    sums_ref[1:2] = column_sum(grad_query * shared)
    sums_ref[2:3] = column_sum(grad_query)
    sums_ref[3:4] = column_sum(grad_key * shared)


def weight_grad_kernel(plan, count, *refs):
    outs = refs[len(refs) - count :]
    at = 0
    for lefts, start, right in plan:
        columns = refs[right].shape[1]
        for k, out in enumerate(outs):
            size = out.shape[0]
            cut = slice(start + k * size, start + (k + 1) * size)
            left = jnp.concatenate([refs[i][:, cut] for i in lefts], axis=0)
            out[:, at : at + columns] = left_inner(left, refs[right][...]).astype(bf16)
        at += columns


def weight_grad(grid, name, width, plan, operands):
    count = grid.radix[0]
    columns = sum(operands[right].shape[1] for unused, start, right in plan)
    return call(
        functools.partial(weight_grad_kernel, plan, count),
        name,
        [((width // count, columns), bf16)] * count,
        operands,
    )


def per_device(
    grid,
    layer_entries,
    loss_sensitivity,
    occupied_counts,
    earlier_normalizer_gain,
    inflow_logits,
    decay_logits,
    channel_lifting,
    channel_collapse,
    direct_term_weight,
    content_projector,
    content_offset,
    common_projector,
    common_offset,
    asking_gain,
    asking_offset,
    lookup_gain,
    forget_gate_matrix,
    forget_gate_offset,
    renewal_gate_matrix,
    renewal_gate_offset,
    candidate_matrix,
    candidate_offset,
    attended_projector,
    later_normalizer_gain,
    hidden_layer_matrix,
    hidden_layer_offset,
    outward_layer_matrix,
    outward_layer_offset,
):
    core = lax.axis_index("mp")
    near = grid.near_index()
    micro, steps, width = layer_entries.shape
    half, quarter = width // 2, width // 4
    span = content_projector.shape[1] // 2
    ff = hidden_layer_matrix.shape[1] // 4
    swap_pairs = [(0, 1), (1, 0)]

    def swap(value):
        return lax.ppermute(value, "mp", swap_pairs)

    def group(own):
        near_own = grid.near_swap(own)
        return [own, near_own, swap(own), swap(near_own)]

    def gathered(kept, sent, near_type=bf16):
        came = swap(sent)
        rows = kept.shape[0] // 2
        near_part = (kept[rows:] + came[rows:].astype(f32)).astype(near_type)
        return kept, came, grid.near_swap(near_part)

    def ordered(index, own, other, axis):
        first = jnp.where(index == 0, own, other)
        second = jnp.where(index == 0, other, own)
        return jnp.concatenate([first, second], axis=axis)

    in_order = functools.partial(ordered, core)
    near_order = functools.partial(ordered, near)

    def cut(value, start, size, axis):
        return lax.dynamic_slice_in_dim(value, start, size, axis=axis)

    def chunks_of(side):
        gate = (2 * core + side) * quarter
        hidden = [side * 2 * ff, side * 2 * ff + ff]
        return [
            [
                cut(content_projector, side * span, span, 1),
                cut(renewal_gate_matrix, gate, quarter, 1),
                cut(candidate_matrix, gate, quarter, 1),
                common_projector,
            ],
            [
                cut(forget_gate_matrix, side * span, span, 1),
                cut(attended_projector, side * span, span, 0).T,
            ],
        ] + [
            [cut(hidden_layer_matrix, at, ff, 1), cut(outward_layer_matrix, at, ff, 0).T]
            for at in hidden
        ]

    gather = Gather(grid, chunks_of(near), chunks_of(1 - near))
    gather.advance()

    row_in = lax.dynamic_index_in_dim(layer_entries, core, 0, keepdims=False)
    row_seed = lax.dynamic_index_in_dim(loss_sensitivity, core, 0, keepdims=False)
    counts = ordered(core, occupied_counts[:1, 0], occupied_counts[1:, 0], 0)
    near_counts = grid.near_swap(counts)
    gate = (2 * core + near) * quarter
    place = jnp.stack(
        [near, core, counts[0], near_counts[0], counts[1], near_counts[1], gate]
    ).astype(jnp.int32)
    spread = grid.permutation(width)
    params = jnp.concatenate(
        [inflow_logits, decay_logits, channel_lifting, channel_collapse], axis=1
    )
    states = inflow_logits.shape[1]
    params = params.T.reshape(4, states, width // LANES, LANES)

    def line_of(value):
        return value.reshape(1, -1)

    gain, direct = line_of(earlier_normalizer_gain), line_of(direct_term_weight)
    tokens = 4 * steps
    normed, pre, packed, seed_low, table, seed_sum = call(
        ema_forward_kernel,
        "average_forward",
        [
            ((steps, width), f32),
            ((steps, width), f32),
            ((steps, 2 * width), bf16),
            ((steps, width), bf16),
            ((steps, width // LANES, LANES), f32),
            ((1, width), f32),
        ],
        [place, row_in, row_seed, gain, direct, params, spread],
        1,
    )
    gather.until(0) if gather.middle[1:] else None
    packed = gather.advance(packed)
    pieces = group(packed)
    seed_low = gather.advance(seed_low)
    near_seed = grid.near_swap(seed_low)
    w_first = gather.weights[0]
    blocks = len(w_first)

    value_pre, value, gates, gates_sent, probs_low, attended, shared_pre, query, key, probs = call(
        attention_kernel,
        "attention_forward",
        [
            ((tokens, span), f32),
            ((tokens, span), bf16),
            ((2 * steps, half), f32),
            ((2 * steps, half), f32),
            ((tokens, SPAN), bf16),
            ((tokens, span), f32),
            ((steps, LANES), f32),
            ((steps, LANES), bf16),
            ((steps, LANES), bf16),
            ((steps, SPAN), f32),
        ],
        [
            place,
            *pieces,
            line_of(cut(content_offset, near * span, span, 0)),
            line_of(common_offset),
            line_of(asking_gain),
            line_of(asking_offset),
            line_of(lookup_gain),
            *w_first,
        ],
        1,
    )
    gates_core = swap(gates_sent)
    attended, gates, gates_core, near_seed = gather.advance((attended, gates, gates_core, near_seed))
    seeds = [seed_low, near_seed, swap(seed_low), swap(near_seed)]
    gates_near = grid.near_swap(
        jnp.concatenate([gates[steps:], gates_core[steps:]], axis=1).astype(bf16)
    )
    w_second = gather.weights[1]
    reset_pre, mixed, mix_kept, mix_sent = call(
        mix_kernel,
        "reset_and_mix",
        [
            ((tokens, span), f32),
            ((tokens, span), bf16),
            ((2 * steps, width), f32),
            ((2 * steps, width), bf16),
        ],
        [*pieces, line_of(cut(forget_gate_offset, near * span, span, 0)), attended, *w_second],
    )
    mix_kept, mix_came = gather.advance((mix_kept, swap(mix_sent)))
    mix_near = grid.near_swap((mix_kept[steps:] + mix_came[steps:].astype(f32)).astype(bf16))
    hidden_pre, update, blended, hat, post_scale, ffn_low = call(
        hidden_kernel,
        "hidden_and_norm",
        [((steps, width), f32)] * 4 + [((steps, 1), f32), ((steps, width), bf16)],
        [
            place,
            row_in,
            mix_kept,
            mix_came,
            mix_near,
            gates,
            gates_core,
            gates_near,
            line_of(renewal_gate_offset),
            line_of(candidate_offset),
            line_of(later_normalizer_gain),
            spread,
        ],
        1,
    )
    ffn_pieces = group(ffn_low)
    while gather.stage < len(gather.state) + len(gather.middle):
        gather.advance()

    ffn_offset = line_of(cut(hidden_layer_offset, near * 2 * ff, 2 * ff, 0))
    moving = []
    bffnin = []
    before = []
    for at in range(2):
        first = at == 0
        out = [((tokens, ff), bf16), ((tokens, ff), bf16), ((1, ff), f32)]
        if first:
            out += [((tokens, width), f32)] * 2
        else:
            out += [((2 * steps, width), f32), ((2 * steps, width), bf16)] * 2
        grad_pre, act, bias, *before = call(
            functools.partial(ffn_kernel, first, blocks),
            "feed_forward",
            out,
            [*ffn_pieces, *seeds, ffn_offset[:, at * ff : (at + 1) * ff], *before, *gather.weights[2 + at]],
        )
        bffnin.append(bias[0])
        if not first:
            down_kept, down_sent, back_kept, back_sent = before
            came = swap(back_sent)
        parts = weight_grad(
            grid,
            "feed_forward_weights",
            width,
            (((0, 1, 2, 3), 0, 8), ((4, 5, 6, 7), 0, 9)),
            [*ffn_pieces, *seeds, grad_pre, act],
        )
        moving.append(Moving(grid, parts))
        if first:
            moving[0].across()
    near_part = (back_kept[steps:] + came[steps:].astype(f32)).astype(bf16)
    near_part = grid.near_swap(near_part)

    grad_input, grad_hidden, grad_update, row_sums = call(
        blend_grad_kernel,
        "blend_backward",
        [
            ((steps, width), f32),
            ((steps, width), bf16),
            ((steps, width), bf16),
            ((3, width), f32),
        ],
        [
            place,
            row_in,
            row_seed,
            back_kept,
            came,
            near_part,
            hidden_pre,
            update,
            hat,
            post_scale,
            line_of(later_normalizer_gain),
            spread,
        ],
        1,
    )
    (m_a, m_b) = moving
    m_a.value, m_b.parts, grad_hidden, grad_update = tie(
        (m_a.value, m_b.parts, grad_hidden, grad_update)
    )
    m_a.along()
    m_b.across()
    hidden_pieces = group(grad_hidden)
    update_pieces = group(grad_update)
    down = gathered(down_kept, down_sent)

    grad_reset, grad_value, probs_kept, probs_sent, span_sums = call(
        attention_grad_kernel,
        "attention_backward",
        [
            ((tokens, span), bf16),
            ((tokens, span), bf16),
            ((2 * steps, SPAN), f32),
            ((2 * steps, SPAN), f32),
            ((2, span), f32),
        ],
        [*hidden_pieces, reset_pre, attended, value, value_pre, probs_low, *w_second],
    )
    parts = weight_grad(
        grid,
        "reset_weights",
        width,
        (((0, 1, 2, 3), 0, 8), ((4, 5, 6, 7), 0, 9)),
        [*pieces, *hidden_pieces, grad_reset, mixed],
    )
    moving.append(Moving(grid, parts))
    m_c = moving[2]
    m_a.value, m_b.value, m_c.parts, grad_reset, grad_value = tie(
        (m_a.value, m_b.value, m_c.parts, grad_reset, grad_value)
    )
    m_b.along()
    m_c.across()
    probs_gathered = gathered(probs_kept, probs_sent, f32)
    grad_gates, in_kept, in_sent = call(
        functools.partial(input_grad_kernel, blocks),
        "input_backward",
        [((tokens, half), bf16), ((2 * steps, 2 * width), f32), ((2 * steps, 2 * width), bf16)],
        [place, *hidden_pieces, *update_pieces, grad_reset, grad_value, spread, *w_first, *w_second],
        1,
    )
    in_gathered = gathered(in_kept, in_sent)
    grad_shared, narrow = call(
        score_grad_kernel,
        "scores_backward",
        [((steps, LANES), bf16), ((4, LANES), f32)],
        [*probs_gathered, probs, query, key, shared_pre, line_of(asking_gain), line_of(lookup_gain)],
    )
    parts = weight_grad(
        grid,
        "value_weights",
        width,
        (((0, 1, 2, 3), width, 4), ((0, 1, 2, 3), 0, 5), ((0,), 0, 6)),
        [*pieces, grad_value, grad_gates, grad_shared],
    )
    moving.append(Moving(grid, parts))
    m_d = moving[3]
    m_b.value, m_c.value, m_d.parts = tie((m_b.value, m_c.value, m_d.parts))
    m_c.along()
    m_d.across()
    averages = call(
        ema_backward_kernel,
        "average_backward",
        [
            ((steps, width), bf16),
            ((steps, width), bf16),
            ((2, width), f32),
            (params.shape[1:], f32),
            (params.shape[1:], f32),
        ],
        [
            place,
            row_in,
            gain,
            direct,
            params,
            spread,
            table,
            normed,
            pre,
            *in_gathered,
            grad_shared,
            grad_input,
            *down,
            blended,
            line_of(outward_layer_offset),
            *w_first,
        ],
        1,
        [
            pltpu.VMEM((steps, width), f32),
            pltpu.VMEM((steps, width), f32),
            pltpu.VMEM((steps, width // LANES, LANES), f32),
        ],
    )
    m_c.value, m_d.value, averages = tie((m_c.value, m_d.value, averages))
    m_d.along()
    grad_row, out_row, grad_vectors, grad_zero, grad_first = averages

    lanes = COMMON_SPAN_DIM
    narrow = jnp.pad(narrow.reshape(1, -1), ((0, 0), (0, width - 4 * lanes)))
    shared_sums = jnp.concatenate(
        [
            grad_zero.reshape(states, width),
            grad_first.reshape(states, width),
            grad_vectors,
            row_sums,
            seed_sum,
            narrow,
            jnp.zeros((1, width), f32),
        ],
        axis=0,
    )
    kept = shared_sums.shape[0] // 2
    keep_rows = cut(shared_sums, core * kept, kept, 0) + swap(
        cut(shared_sums, (1 - core) * kept, kept, 0)
    )

    def placed(value):
        return near_order(value, jnp.zeros_like(value), 0).reshape(-1, width)

    wide_sums = [
        placed(span_sums[0]),
        placed(span_sums[1]),
        placed(jnp.concatenate(bffnin)),
    ]
    small = jnp.concatenate([keep_rows] + wide_sums, axis=0)
    sums = grid.sum_all(small)
    first_rows = sums[:kept]
    whole = in_order(first_rows, swap(first_rows), 0)
    wide = sums[kept:]
    zero = whole[:states].T
    first = whole[states : 2 * states].T
    rate = jax.nn.sigmoid(inflow_logits)
    damp = jax.nn.sigmoid(decay_logits)
    grad_collapse = rate * channel_lifting * zero
    grad_inflow = channel_collapse * zero
    grad_keep = channel_collapse * rate * channel_lifting * first
    grad_lifting = grad_inflow * rate
    grad_rate = (grad_inflow * channel_lifting - grad_keep * damp) * rate * (1.0 - rate)
    grad_damp = -grad_keep * rate * damp * (1.0 - damp)
    rest = whole[2 * states :]
    thin = rest[6].reshape(-1, lanes)

    (own_a, near_a), (own_b, near_b), (own_c, near_c), (own_d, near_d) = [m.near() for m in moving]
    out_in = near_order(
        jnp.concatenate([own_a[:, :ff], own_b[:, :ff]], axis=1),
        jnp.concatenate([near_a[:, :ff], near_b[:, :ff]], axis=1),
        1,
    )
    out_down = near_order(
        jnp.concatenate([own_a[:, ff:], own_b[:, ff:]], axis=1),
        jnp.concatenate([near_a[:, ff:], near_b[:, ff:]], axis=1),
        1,
    )
    out_reset = near_order(own_c[:, :span], near_c[:, :span], 1)
    out_wout = near_order(own_c[:, span:], near_c[:, span:], 1)
    out_value = near_order(own_d[:, :span], near_d[:, :span], 1)
    own_d, near_d = own_d[:, span:], near_d[:, span:]
    gates_half = jnp.concatenate(
        [
            near_order(own_d[:, :quarter], near_d[:, :quarter], 1),
            near_order(own_d[:, quarter:half], near_d[:, quarter:half], 1),
            own_d[:, half:] + near_d[:, half:],
        ],
        axis=1,
    )
    gates_other = swap(gates_half)
    out_update = in_order(gates_half[:, :half], gates_other[:, :half], 1)
    out_hidden = in_order(gates_half[:, half : 2 * half], gates_other[:, half : 2 * half], 1)
    out_shared = gates_half[:, 2 * half :] + gates_other[:, 2 * half :]

    rows_out = jnp.stack([out_row, grad_row])
    rows_other = swap(rows_out)
    outputs = in_order(rows_out[:1], rows_other[:1], 0)
    grad_tokens = in_order(rows_out[1:], rows_other[1:], 0)
    return (
        outputs,
        grad_tokens,
        rest[0],
        grad_rate,
        grad_damp,
        grad_lifting,
        grad_collapse,
        rest[1],
        out_value,
        wide[0],
        out_shared,
        thin[0],
        thin[1],
        thin[2],
        thin[3],
        out_reset,
        wide[1],
        out_update,
        rest[2],
        out_hidden,
        rest[3],
        out_wout.T,
        rest[4],
        out_in,
        wide[2:].reshape(-1),
        out_down.T,
        rest[5],
    )


def solution(mesh):
    grid = Grid(mesh.shape["dp"])
    return jax.shard_map(
        functools.partial(per_device, grid),
        mesh=mesh,
        in_specs=(
            P(None, "dp", None),
            P(None, "dp", None),
            P(None, "dp"),
            P(),
            P(),
            P(),
            P(),
            P(),
            P(),
            P("dp", "mp"),
            P("mp"),
            P("dp", None),
            P(),
            P(),
            P(),
            P(),
            P("dp", "mp"),
            P("mp"),
            P("dp", None),
            P(),
            P("dp", None),
            P(),
            P("mp", "dp"),
            P(),
            P("dp", "mp"),
            P("mp"),
            P("mp", "dp"),
            P(),
        ),
        out_specs=(
            P(None, "dp", None),
            P(None, "dp", None),
            P(),
            P(),
            P(),
            P(),
            P(),
            P(),
            P("dp", "mp"),
            P("mp"),
            P("dp", None),
            P(),
            P(),
            P(),
            P(),
            P("dp", "mp"),
            P("mp"),
            P("dp", None),
            P(),
            P("dp", None),
            P(),
            P("mp", "dp"),
            P(),
            P("dp", "mp"),
            P("mp"),
            P("mp", "dp"),
            P(),
        ),
        check_vma=False,
    )
```

time: 508 us -> 408 us (0.80)
  Pallas kernels: 21.7 us -> 107 us
  starting transfers between devices: 174 us -> 112 us
  waiting for transfers between devices: 169 us -> 113 us
  matrix products: 50.2 us -> 0 us
  local copies, waits for them, and re-layouts: 42 us -> 32.7 us
  other arithmetic: 38.9 us -> 31 us
    pallas_call x2 -> x15, Pallas kernels: 21.7 us -> 107 us  [call(): pl.pallas_call(kernel, name=name, out_shape=[jax.ShapeDtypeStruct(shape,...]
    ppermute x85 -> x55, starting transfers between devices: 135 us -> 69.8 us  [the longest x16 30.2 us: deliver(): lax.ppermute(parts[k], 'dp', self.shift(dim, k))]
    ppermute x85 -> x55, waiting for transfers between devices: 166 us -> 110 us  [the longest x21 74.2 us: fetch(): lax.ppermute(array, 'dp', self.shift(dim, -k))]
    dot_general x39 -> x0, matrix products: 48.5 us -> none  [the longest x15 22.4 us: product(): return jnp.dot(left, right, preferred_element_type=f32)]
    concatenate x24 -> x15, other arithmetic: 15.4 us -> 6.27 us  [the longest x11 5.49 us: ordered(): return jnp.concatenate([first, second], axis=axis)]
    slice x35 -> x9, local copies, waits for them, and re-layouts: 10.8 us -> 4.49 us  [the longest x1 1.31 us: per_device(): counts = ordered(core, occupied_counts[:1, 0], occupied_counts[1:, 0], 0)]
    unnamed x154 -> x152, local copies, waits for them, and re-layouts: 15.7 us -> 11.4 us
    ppermute x18 -> x20, starting transfers between devices: 39.5 us -> 42 us  [swap(): return lax.ppermute(value, 'mp', swap_pairs)]
  transfers between devices with their start and end apart: 103 -> 75, of which waited for: 41 -> 22; matrix products, arithmetic and copies ran while one was open for 24% -> 12% of each run, Pallas kernels for 4% -> 27%
where the time goes in v2:
time: 408 us; the launch traced here: 400 us
  waiting for transfers between devices  113 us (28%)
  starting transfers between devices  112 us (27%)
  Pallas kernels  107 us (26%)
  local copies, waits for them, and re-layouts  32.7 us (8%)
  other arithmetic  31 us (8%)
  between operations  4.99 us (1%)
    pallas_call x15, Pallas kernels, call(): pl.pallas_call(kernel, name=name, out_shape=[jax.ShapeDtypeStruct(shape,...  107 us
    ppermute x21, waiting for transfers between devices, fetch(): lax.ppermute(array, 'dp', self.shift(dim, -k))  74.2 us
    ppermute x20, starting transfers between devices, swap(): return lax.ppermute(value, 'mp', swap_pairs)  42 us
    ppermute x16, starting transfers between devices, deliver(): lax.ppermute(parts[k], 'dp', self.shift(dim, k))  30.2 us
    ppermute x21, starting transfers between devices, fetch(): lax.ppermute(array, 'dp', self.shift(dim, -k))  23.4 us
    ppermute x16, waiting for transfers between devices, deliver(): lax.ppermute(parts[k], 'dp', self.shift(dim, k))  22 us
    ppermute x18, starting transfers between devices, near_swap(): return lax.ppermute(value, 'dp', self.shift(self.near, 1))  16.3 us
    ppermute x18, waiting for transfers between devices, near_swap(): return lax.ppermute(value, 'dp', self.shift(self.near, 1))  13.6 us
  transfers between devices with their start and end apart: 75, of which 22 were waited for; matrix products, arithmetic and copies ran while one was open for 12% of the time, Pallas kernels for 27%

profile of v2, /device:TPU:1, one launch (start us, length us, event | category | flops | bytes accessed | tf_op | source)
XLA Modules:
  0.0 400.4 jit_solution(15924929442633382587)
XLA Ops:
  4.0 2.1 collective-permute-start.1
  10.3 2.2 fusion.spread_ref.refs_10_
  16.7 3.5 collective-permute-start.2
  25.9 10.3 %average_forward.1 = (f32[128,1024]{1,0:T(8,128)}, f32[128,1024]{1,0:T(8,128)}, bf16[128,2048]{1,0:T(8,128)(2,1)}, bf16[128,1024]{1,0:T(8,128)(2,1)}, f32[128,8,128]{2,1,0:T(8,128)}, /*index=5*/f32[1,1024]{1,0:T(1,128)}) custom-call(s32[7]{0:T(128)} %stack.120.place_ref, bf16[128,1024]{1,0:T(8,128)(2,1)} %get-tuple-element.353.x_ref, ...), custom_call_target="tpu_custom_call" | custom-call | flops 1 | bytes 1 | tf_op jit(solution)/shard_map/average_forward/pallas_call | solution.py:229
  36.2 7.9 %collective-permute-done.3 = bf16[2,64,1152]{2,1,0:T(8,128)(2,1)S(1)} collective-permute-done((bf16[2,64,1152]{2,1,0:T(8,128)(2,1)S(1)}, bf16[2,64,1152]{2,1,0:T(8,128)(2,1)S(1)}, u32[]{:S(2)}, u32[]{:S(2)}) %collective-permute-start.3) | collective-permute-done | bytes 294944 | tf_op jit(solution)/shard_map/ppermute | solution.py:73
  48.0 3.4 collective-permute-start.7
  53.6 4.0 collective-permute-start.15
  57.7 3.4 collective-permute-start.16
  61.1 11.9 %collective-permute-done.7 = bf16[2,64,1024]{2,1,0:T(8,128)(2,1)S(1)} collective-permute-done((bf16[2,64,1024]{2,1,0:T(8,128)(2,1)S(1)}, bf16[2,64,1024]{2,1,0:T(8,128)(2,1)S(1)}, u32[]{:S(2)}, u32[]{:S(2)}) %collective-permute-start.7) | collective-permute-done | bytes 262176 | tf_op jit(solution)/shard_map/ppermute | solution.py:73
  76.1 7.1 %attention_forward.1 = (f32[512,512]{1,0:T(8,128)}, bf16[512,512]{1,0:T(8,128)(2,1)}, f32[256,512]{1,0:T(8,128)}, f32[256,512]{1,0:T(8,128)}, bf16[512,128]{1,0:...) custom-call(s32[7]{0:T(128)} %stack.120.place_ref, ...), custom_call_target="tpu_custom_call" | custom-call | flops 1 | bytes 1 | tf_op jit(solution)/shard_map/attention_forward/pallas_call | solution.py:229
  83.2 2.6 collective-permute-start.17
  85.8 2.5 collective-permute-start.11
  92.0 14.3 %collective-permute-done.11 = bf16[2,64,1024]{2,1,0:T(8,128)(2,1)S(1)} collective-permute-done((bf16[2,64,1024]{2,1,0:T(8,128)(2,1)}, bf16[2,64,1024]{2,1,0:T(8,128)(2,1)S(1)}, u32[]{:S(2)}, u32[]{:S(2)}) %collective-permute-start.11) | collective-permute-done | bytes 262176 | tf_op jit(solution)/shard_map/ppermute | solution.py:73
  109.9 6.2 %reset_and_mix.1 = (f32[512,512]{1,0:T(8,128)}, bf16[512,512]{1,0:T(8,128)(2,1)}, f32[256,1024]{1,0:T(8,128)}, bf16[256,1024]{1,0:T(8,128)(2,1)}) custom-call(bf16[128,2048]{1,0:T(8,128)(2,1)} %get-tuple-element.145.p0.refs_0_, bf16[128,2048]{1,0:T(8,128)(2,1)} %copy-done.5, bf16[128,2048]{1,0:T(8,128)(2,1)} %copy-done.6, bf16[128,2048]{1,0:T(8,128)(2,1)} %copy-done.7, ...), custom_call_target="tpu_custom_call" | custom-call | flops 1 | bytes 1 | tf_op jit(solution)/shard_map/reset_and_mix/pallas_call | solution.py:229
  122.4 2.9 collective-permute-done.19
  125.7 16.8 %collective-permute-done.20 = bf16[2,64,1024]{2,1,0:T(8,128)(2,1)S(1)} collective-permute-done((bf16[2,64,1024]{2,1,0:T(8,128)(2,1)}, bf16[2,64,1024]{2,1,0:T(8,128)(2,1)S(1)}, u32[]{:S(2)}, u32[]{:S(2)}) %collective-permute-start.20) | collective-permute-done | bytes 262176 | tf_op jit(solution)/shard_map/ppermute | solution.py:73
  146.3 5.8 %collective-permute-done.24.near_ref = bf16[128,1024]{1,0:T(8,128)(2,1)S(1)} collective-permute-done((bf16[128,1024]{1,0:T(8,128)(2,1)S(1)}, bf16[128,1024]{1,0:T(8,128)(2,1)S(1)}, u32[]{:S(2)}, u32[]{:S(2)}) %collective-permute-start.24) | collective-permute-done | bytes 262176 | tf_op jit(solution)/shard_map/ppermute | solution.py:85
  152.8 5.7 %hidden_and_norm.1 = (f32[128,1024]{1,0:T(8,128)}, f32[128,1024]{1,0:T(8,128)}, f32[128,1024]{1,0:T(8,128)}, f32[128,1024]{1,0:T(8,128)}, f32[128,1]{1,0:T(8,128)}, /*index=5*/bf16[128,1024]{1,0:T(8,128)(2,1)}) custom-call(s32[7]{0:T(128)} %stack.120.place_ref, bf16[128,1024]{1,0:T(8,128)(2,1)} %get-tuple-element.353.x_ref, ...), custom_call_target="tpu_custom_call" | custom-call | flops 1 | bytes 1 | tf_op jit(solution)/shard_map/hidden_and_norm/pallas_call | solution.py:229
  162.3 2.7 collective-permute-done.26.refs_1_
  164.9 2.5 collective-permute-start.28
  169.4 8.0 %feed_forward.2 = (bf16[512,512]{1,0:T(8,128)(2,1)}, bf16[512,512]{1,0:T(8,128)(2,1)}, f32[1,512]{1,0:T(1,128)}, f32[512,1024]{1,0:T(8,128)}, f32[512,1024]{1,0:T(8,128)}) custom-call(bf16[128,1024]{1,0:T(8,128)(2,1)} %get-tuple-element.163.refs_0_, bf16[128,1024]{1,0:T(8,128)(2,1)} %copy-done.13, bf16[128,1024]{1,0:T(8,128)(2,1)} %copy-done.16, ...), custom_call_target="tpu_custom_call" | custom-call | flops 1 | bytes 1 | tf_op jit(solution)/shard_map/feed_forward/pallas_call | solution.py:229
  177.4 4.2 %feed_forward_weights.2 = (bf16[512,1024]{1,0:T(8,128)(2,1)}, bf16[512,1024]{1,0:T(8,128)(2,1)}) custom-call(bf16[128,1024]{1,0:T(8,128)(2,1)} %get-tuple-element.163.refs_0_, bf16[128,1024]{1,0:T(8,128)(2,1)} %copy-done.13, bf16[128,1024]{1,0:T(8,128)(2,1)} %copy-done.16, bf16[128,1024]{1,0:T(8,128)(2,1)} %copy-done.17, ...), custom_call_target="tpu_custom_call" | custom-call | flops 1 | bytes 1 | tf_op jit(solution)/shard_map/feed_forward_weights/pallas_call | solution.py:229
  181.8 8.4 %feed_forward.3 = (bf16[512,512]{1,0:T(8,128)(2,1)}, bf16[512,512]{1,0:T(8,128)(2,1)}, f32[1,512]{1,0:T(1,128)}, f32[256,1024]{1,0:T(8,128)}, bf16[256,1024]{1,0...) custom-call(bf16[128,1024]{1,0:T(8,128)(2,1)} %get-tuple-element.163.refs_0_, ...), custom_call_target="tpu_custom_call" | custom-call | flops 1 | bytes 1 | tf_op jit(solution)/shard_map/feed_forward/pallas_call | solution.py:229
  195.8 4.2 %feed_forward_weights.3 = (bf16[512,1024]{1,0:T(8,128)(2,1)}, bf16[512,1024]{1,0:T(8,128)(2,1)}) custom-call(bf16[128,1024]{1,0:T(8,128)(2,1)} %get-tuple-element.163.refs_0_, bf16[128,1024]{1,0:T(8,128)(2,1)} %copy-done.13, bf16[128,1024]{1,0:T(8,128)(2,1)} %copy-done.16, bf16[128,1024]{1,0:T(8,128)(2,1)} %copy-done.17, ...), custom_call_target="tpu_custom_call" | custom-call | flops 1 | bytes 1 | tf_op jit(solution)/shard_map/feed_forward_weights/pallas_call | solution.py:229
  202.3 6.2 %blend_backward.1 = (f32[128,1024]{1,0:T(8,128)}, bf16[128,1024]{1,0:T(8,128)(2,1)}, bf16[128,1024]{1,0:T(8,128)(2,1)}, f32[3,1024]{1,0:T(4,128)}) custom-call(s32[7]{0:T(128)} %stack.120.place_ref, bf16[128,1024]{1,0:T(8,128)(2,1)} %get-tuple-element.353.x_ref, bf16[128,1024]{1,0:T(8,128)(2,1)} %get-tuple-element.352.seed_ref, ...), custom_call_target="tpu_custom_call" | custom-call | flops 1 | bytes 1 | tf_op jit(solution)/shard_map/blend_backward/pallas_call | solution.py:229
  214.0 2.9 collective-permute-start.37
  222.2 4.4 %collective-permute-start.40 = (bf16[128,1024]{1,0:T(8,128)(2,1)S(1)}, bf16[128,1024]{1,0:T(8,128)(2,1)S(1)}, u32[]{:S(2)}, u32[]{:S(2)}) collective-permute-start(bf16[128,1024]{1,0:T(8,128)(2,1)S(1)} %copy-done.19), channel_id=1, source_target_pairs={{0,1},{1,0},{2,3},{3,2},{4,5},{5,4},{6,7},{7,6},{8,9},{9,8},{10,11... | collective-permute-start | bytes 786440 | tf_op jit(solution)/shard_map/ppermute | solution.py:736
  226.6 6.8 %collective-permute-done.36 = bf16[2,64,1024]{2,1,0:T(8,128)(2,1)} collective-permute-done((bf16[2,64,1024]{2,1,0:T(8,128)(2,1)}, bf16[2,64,1024]{2,1,0:T(8,128)(2,1)}, u32[]{:S(2)}, u32[]{:S(2)}) %collective-permute-start.36) | collective-permute-done | bytes 262176 | tf_op jit(solution)/shard_map/ppermute | solution.py:78
  233.4 2.5 collective-permute-start.47
  238.6 5.5 %attention_backward.1 = (bf16[512,512]{1,0:T(8,128)(2,1)}, bf16[512,512]{1,0:T(8,128)(2,1)}, f32[256,128]{1,0:T(8,128)}, f32[256,128]{1,0:T(8,128)}, f32[2,512]{1,0:T(2,128)}) custom-call(bf16[128,1024]{1,0:T(8,128)(2,1)} %get-tuple-element.189.h0.refs_4_.refs_0_, bf16[128,1024]{1,0:T(8,128)(2,1)} %copy-done.20, bf16[128,1024]{1,0:T(8,128)(2,1)} %copy-done.21, ...), custom_call_target="tpu_custom_call" | custom-call | flops 1 | bytes 1 | tf_op jit(solution)/shard_map/attention_backward/pallas_call | solution.py:229
  244.9 4.6 %reset_weights.1 = (bf16[512,1024]{1,0:T(8,128)(2,1)}, bf16[512,1024]{1,0:T(8,128)(2,1)}) custom-call(bf16[128,2048]{1,0:T(8,128)(2,1)} %get-tuple-element.145.p0.refs_0_, bf16[128,2048]{1,0:T(8,128)(2,1)} %copy-done.5, bf16[128,2048]{1,0:T(8,128)(2,1)} %copy-done.6, bf16[128,2048]{1,0:T(8,128)(2,1)} %copy-done.7, ...), custom_call_target="tpu_custom_call" | custom-call | flops 1 | bytes 1 | tf_op jit(solution)/shard_map/reset_weights/pallas_call | solution.py:229
  250.0 2.8 collective-permute-done.50.near_ref
  260.8 5.3 %collective-permute-start.42 = (bf16[2,64,1024]{2,1,0:T(8,128)(2,1)}, bf16[2,64,1024]{2,1,0:T(8,128)(2,1)}, u32[]{:S(2)}, u32[]{:S(2)}) collective-permute-start(bf16[2,64,1024]{2,1,0:T(8,128)(2,1)} %get-tuple-element.261), channel_id=1, source_target_pairs={{0,8},{2,10},{4,12},{6,14},{8,16},{10,18},{12,20},{14,22},{16,24},... | collective-permute-start | bytes 786440 | tf_op jit(solution)/shard_map/ppermute | solution.py:78
  266.2 2.1 collective-permute-start.44
  268.3 9.5 %input_backward.1 = (bf16[512,512]{1,0:T(8,128)(2,1)}, f32[256,2048]{1,0:T(8,128)}, bf16[256,2048]{1,0:T(8,128)(2,1)}) custom-call(s32[7]{0:T(128)} %stack.120.place_ref, bf16[128,1024]{1,0:T(8,128)(2,1)} %get-tuple-element.189.h0.refs_4_.refs_0_, bf16[128,1024]{1,0:T(8,128)(2,1)} %copy-done.20, bf16[128,1024]{1,0:T(8,128)(2,1)} %copy-done.21, ...), custom_call_target="tpu_custom_call" | custom-call | flops 1 | bytes 1 | tf_op jit(solution)/shard_map/input_backward/pallas_call | solution.py:229
  277.9 2.1 collective-permute-start.55
  280.0 4.7 %value_weights.1 = (bf16[512,1152]{1,0:T(8,128)(2,1)}, bf16[512,1152]{1,0:T(8,128)(2,1)}) custom-call(bf16[128,2048]{1,0:T(8,128)(2,1)} %get-tuple-element.145.p0.refs_0_, bf16[128,2048]{1,0:T(8,128)(2,1)} %copy-done.5, bf16[128,2048]{1,0:T(8,128)(2,1)} %copy-done.6, bf16[128,2048]{1,0:T(8,128)(2,1)} %copy-done.7, ...), custom_call_target="tpu_custom_call" | custom-call | flops 1 | bytes 1 | tf_op jit(solution)/shard_map/value_weights/pallas_call | solution.py:229
  289.9 6.1 %collective-permute-start.51 = (bf16[2,64,1024]{2,1,0:T(8,128)(2,1)S(1)}, bf16[2,64,1024]{2,1,0:T(8,128)(2,1)S(1)}, u32[]{:S(2)}, u32[]{:S(2)}) collective-permute-start(bf16[2,64,1024]{2,1,0:T(8,128)(2,1)S(1)} %get-tuple-element.258), channel_id=1, source_target_pairs={{0,8},{2,10},{4,12},{6,14},{8,16},{10,18},{12,20},{14,22},{16,24},... | collective-permute-start | bytes 786440 | tf_op jit(solution)/shard_map/ppermute | solution.py:78
  301.0 12.9 %collective-permute-done.52 = bf16[2,64,1024]{2,1,0:T(8,128)(2,1)S(1)} collective-permute-done((bf16[2,64,1024]{2,1,0:T(8,128)(2,1)S(1)}, bf16[2,64,1024]{2,1,0:T(8,128)(2,1)S(1)}, u32[]{:S(2)}, u32[]{:S(2)}) %collective-permute-start.52) | collective-permute-done | bytes 262176 | tf_op jit(solution)/shard_map/ppermute | solution.py:78
  314.9 20.2 %average_backward.1 = (bf16[128,1024]{1,0:T(8,128)(2,1)}, bf16[128,1024]{1,0:T(8,128)(2,1)}, f32[2,1024]{1,0:T(2,128)}, f32[16,8,128]{2,1,0:T(8,128)}, f32[16,8,128]{2,1,0:T(8,128)}) custom-call(s32[7]{0:T(128)} %stack.120.place_ref, bf16[128,1024]{1,0:T(8,128)(2,1)} %get-tuple-element.353.x_ref, f32[1,1024]{1,0:T(1,128)} %bitcast.255, f32[1,1024]{1,0:T(1,128)} %bitcast.257, ...), custom_call_target="tpu_custom_call" | custom-call | flops 1 | bytes 1 | tf_op jit(solution)/shard_map/average_backward/pallas_call | solution.py:229
  339.5 6.0 %collective-permute-start.67 = (bf16[2,64,1152]{2,1,0:T(8,128)(2,1)}, bf16[2,64,1152]{2,1,0:T(8,128)(2,1)S(1)}, u32[]{:S(2)}, u32[]{:S(2)}) collective-permute-start(bf16[2,64,1152]{2,1,0:T(8,128)(2,1)} %get-tuple-element.255), channel_id=1, source_target_pairs={{0,8},{2,10},{4,12},{6,14},{8,16},{10,18},{12,20},{14,22},{16,24},... | collective-permute-start | bytes 884744 | tf_op jit(solution)/shard_map/ppermute | solution.py:78
  345.5 2.1 collective-permute-start.69
  349.0 4.3 %collective-permute-start.60 = (f32[20,1024]{1,0:T(8,128)S(1)}, f32[20,1024]{1,0:T(8,128)S(1)}, u32[]{:S(2)}, u32[]{:S(2)}) collective-permute-start(f32[20,1024]{1,0:T(8,128)S(1)} %constant_dynamic-slice_fusion), channel_id=1, source_target_pairs={{0,1},{1,0},{2,3},{3,2},{4,5},{5,4},{6,7},{7,6},{8,9},{9,8},{10,11... | collective-permute-start | bytes 245768 | tf_op jit(solution)/shard_map/ppermute | solution.py:736
  355.5 3.0 collective-permute-done.61
  360.1 15.8 %collective-permute-done.62 = f32[24,1024]{1,0:T(8,128)S(1)} collective-permute-done((f32[24,1024]{1,0:T(8,128)S(1)}, f32[24,1024]{1,0:T(8,128)S(1)}, u32[]{:S(2)}, u32[]{:S(2)}) %collective-permute-start.62) | collective-permute-done | bytes 98336 | tf_op jit(solution)/shard_map/ppermute | solution.py:73
  376.7 3.6 collective-permute-start.59
  384.8 5.0 %collective-permute-start.66 = (f32[20,1024]{1,0:T(8,128)S(1)}, f32[20,1024]{1,0:T(8,128)S(1)}, u32[]{:S(2)}, u32[]{:S(2)}) collective-permute-start(f32[20,1024]{1,0:T(8,128)S(1)} %bitcast.234), channel_id=1, source_target_pairs={{0,1},{1,0},{2,3},{3,2},{4,5},{5,4},{6,7},{7,6},{8,9},{9,8},{10,11... | collective-permute-start | bytes 245768 | tf_op jit(solution)/shard_map/ppermute | solution.py:736
  391.2 2.1 collective-permute-start.71
  (374 shorter events, 112.3 us)
Async XLA Ops:
  10.1 13.3 %collective-permute-start = (s32[2]{0:T(128)S(1)}, s32[2]{0:T(128)S(1)}, u32[]{:S(2)}, u32[]{:S(2)}) collective-permute-start(s32[2]{0:T(128)S(1)} %pad_add_fusion), channel_id=1, source_target_pairs={{0,2},{2,0},{4,6},{6,4},{8,10},{10,8},{12,14},{14,12},{16,18},{18,... | collective-permute-start | bytes 32 | tf_op jit(solution)/shard_map/ppermute | solution.py:85
  16.7 19.6 %collective-permute-start.2 = (bf16[2,64,1152]{2,1,0:T(8,128)(2,1)S(1)}, bf16[2,64,1152]{2,1,0:T(8,128)(2,1)S(1)}, u32[]{:S(2)}, u32[]{:S(2)}) collective-permute-start(bf16[2,64,1152]{2,1,0:T(8,128)(2,1)S(1)} %pad_maximum_fusion.8), channel_id=1, source_target_pairs={{0,24},{2,26},{4,28},{6,30},{8,0},{10,2},{12,4},{14,6},{16,8},{18,... | collective-permute-start | bytes 884744 | tf_op jit(solution)/shard_map/ppermute | solution.py:73
  20.2 23.9 %collective-permute-start.3 = (bf16[2,64,1152]{2,1,0:T(8,128)(2,1)S(1)}, bf16[2,64,1152]{2,1,0:T(8,128)(2,1)S(1)}, u32[]{:S(2)}, u32[]{:S(2)}) collective-permute-start(bf16[2,64,1152]{2,1,0:T(8,128)(2,1)S(1)} %pad_maximum_fusion.8), channel_id=1, source_target_pairs={{0,16},{2,18},{4,20},{6,22},{8,24},{10,26},{12,28},{14,30},{16,0},... | collective-permute-start | bytes 884744 | tf_op jit(solution)/shard_map/ppermute | solution.py:73
  20.2 23.9 %collective-permute-start.4 = (bf16[2,64,1152]{2,1,0:T(8,128)(2,1)S(1)}, bf16[2,64,1152]{2,1,0:T(8,128)(2,1)S(1)}, u32[]{:S(2)}, u32[]{:S(2)}) collective-permute-start(bf16[2,64,1152]{2,1,0:T(8,128)(2,1)S(1)} %pad_maximum_fusion.8), channel_id=1, source_target_pairs={{0,8},{2,10},{4,12},{6,14},{8,16},{10,18},{12,20},{14,22},{16,24},... | collective-permute-start | bytes 884744 | tf_op jit(solution)/shard_map/ppermute | solution.py:73
  20.7 23.6 %collective-permute-start.5 = (bf16[64,3072]{1,0:T(8,128)(2,1)}, bf16[64,3072]{1,0:T(8,128)(2,1)S(1)}, u32[]{:S(2)}, u32[]{:S(2)}) collective-permute-start(bf16[64,3072]{1,0:T(8,128)(2,1)} %bitcast_dynamic-update-slice_fusion), channel_id=1, source_target_pairs={{0,2},{2,0},{4,6},{6,4},{8,10},{10,8},{12,14},{14,12},{16,18},{18,... | collective-permute-start | bytes 1179656 | tf_op jit(solution)/shard_map/ppermute | solution.py:85
  45.4 27.7 %collective-permute-start.9 = (bf16[4,2,64,1152]{3,2,1,0:T(8,128)(2,1)S(1)}, bf16[4,2,64,1152]{3,2,1,0:T(8,128)(2,1)S(1)}, u32[]{:S(2)}, u32[]{:S(2)}) collective-permute-start(bf16[4,2,64,1152]{3,2,1,0:T(8,128)(2,1)S(1)} %pad_maximum_fusion), channel_id=1, source_target_pairs={{0,4},{2,6},{4,0},{6,2},{8,12},{10,14},{12,8},{14,10},{16,20},{18,... | collective-permute-start | bytes 3538952 | tf_op jit(solution)/shard_map/ppermute | solution.py:73
  48.0 25.0 %collective-permute-start.7 = (bf16[2,64,1024]{2,1,0:T(8,128)(2,1)S(1)}, bf16[2,64,1024]{2,1,0:T(8,128)(2,1)S(1)}, u32[]{:S(2)}, u32[]{:S(2)}) collective-permute-start(bf16[2,64,1024]{2,1,0:T(8,128)(2,1)S(1)} %pad_maximum_fusion.9), channel_id=1, source_target_pairs={{0,16},{2,18},{4,20},{6,22},{8,24},{10,26},{12,28},{14,30},{16,0},... | collective-permute-start | bytes 786440 | tf_op jit(solution)/shard_map/ppermute | solution.py:73
  51.4 21.6 %collective-permute-start.8 = (bf16[2,64,1024]{2,1,0:T(8,128)(2,1)S(1)}, bf16[2,64,1024]{2,1,0:T(8,128)(2,1)S(1)}, u32[]{:S(2)}, u32[]{:S(2)}) collective-permute-start(bf16[2,64,1024]{2,1,0:T(8,128)(2,1)S(1)} %pad_maximum_fusion.9), channel_id=1, source_target_pairs={{0,8},{2,10},{4,12},{6,14},{8,16},{10,18},{12,20},{14,22},{16,24},... | collective-permute-start | bytes 786440 | tf_op jit(solution)/shard_map/ppermute | solution.py:73
  53.6 20.8 %collective-permute-start.15 = (bf16[128,2048]{1,0:T(8,128)(2,1)S(1)}, bf16[128,2048]{1,0:T(8,128)(2,1)S(1)}, u32[]{:S(2)}, u32[]{:S(2)}) collective-permute-start(bf16[128,2048]{1,0:T(8,128)(2,1)S(1)} %copy-done.4), channel_id=1, source_target_pairs={{0,1},{1,0},{2,3},{3,2},{4,5},{5,4},{6,7},{7,6},{8,9},{9,8},{10,11... | collective-permute-start | bytes 1572872 | tf_op jit(solution)/shard_map/ppermute | solution.py:736
  57.7 16.7 %collective-permute-start.16 = (bf16[128,2048]{1,0:T(8,128)(2,1)S(1)}, bf16[128,2048]{1,0:T(8,128)(2,1)S(1)}, u32[]{:S(2)}, u32[]{:S(2)}) collective-permute-start(bf16[128,2048]{1,0:T(8,128)(2,1)S(1)} %collective-permute-done.14.p1.refs_1_), channel_id=1, source_target_pairs={{0,1},{1,0},{2,3},{3,2},{4,5},{5,4},{6,7},{7,6},{8,9},{9,8},{10,11... | collective-permute-start | bytes 1572872 | tf_op jit(solution)/shard_map/ppermute | solution.py:736
  73.2 34.4 %collective-permute-start.13 = (bf16[4,2,64,1024]{3,2,1,0:T(8,128)(2,1)S(1)}, bf16[4,2,64,1024]{3,2,1,0:T(8,128)(2,1)S(1)}, u32[]{:S(2)}, u32[]{:S(2)}) collective-permute-start(bf16[4,2,64,1024]{3,2,1,0:T(8,128)(2,1)S(1)} %pad_maximum_fusion.1), channel_id=1, source_target_pairs={{0,4},{2,6},{4,0},{6,2},{8,12},{10,14},{12,8},{14,10},{16,20},{18,... | collective-permute-start | bytes 3145736 | tf_op jit(solution)/shard_map/ppermute | solution.py:73
  74.4 15.7 %collective-permute-start.10 = (bf16[2,64,1024]{2,1,0:T(8,128)(2,1)}, bf16[2,64,1024]{2,1,0:T(8,128)(2,1)}, u32[]{:S(2)}, u32[]{:S(2)}) collective-permute-start(bf16[2,64,1024]{2,1,0:T(8,128)(2,1)} %pad_maximum_fusion.10), channel_id=1, source_target_pairs={{0,24},{2,26},{4,28},{6,30},{8,0},{10,2},{12,4},{14,6},{16,8},{18,... | collective-permute-start | bytes 786440 | tf_op jit(solution)/shard_map/ppermute | solution.py:73
  83.2 24.4 %collective-permute-start.17 = (f32[256,512]{1,0:T(8,128)}, f32[256,512]{1,0:T(8,128)S(1)}, u32[]{:S(2)}, u32[]{:S(2)}) collective-permute-start(f32[256,512]{1,0:T(8,128)} %get-tuple-element.150), channel_id=1, source_target_pairs={{0,1},{1,0},{2,3},{3,2},{4,5},{5,4},{6,7},{7,6},{8,9},{9,8},{10,11... | collective-permute-start | bytes 1572872 | tf_op jit(solution)/shard_map/ppermute | solution.py:736
  85.8 20.5 %collective-permute-start.11 = (bf16[2,64,1024]{2,1,0:T(8,128)(2,1)}, bf16[2,64,1024]{2,1,0:T(8,128)(2,1)S(1)}, u32[]{:S(2)}, u32[]{:S(2)}) collective-permute-start(bf16[2,64,1024]{2,1,0:T(8,128)(2,1)} %pad_maximum_fusion.10), channel_id=1, source_target_pairs={{0,16},{2,18},{4,20},{6,22},{8,24},{10,26},{12,28},{14,30},{16,0},... | collective-permute-start | bytes 786440 | tf_op jit(solution)/shard_map/ppermute | solution.py:73
  88.3 18.0 %collective-permute-start.12 = (bf16[2,64,1024]{2,1,0:T(8,128)(2,1)}, bf16[2,64,1024]{2,1,0:T(8,128)(2,1)S(1)}, u32[]{:S(2)}, u32[]{:S(2)}) collective-permute-start(bf16[2,64,1024]{2,1,0:T(8,128)(2,1)} %pad_maximum_fusion.10), channel_id=1, source_target_pairs={{0,8},{2,10},{4,12},{6,14},{8,16},{10,18},{12,20},{14,22},{16,24},... | collective-permute-start | bytes 786440 | tf_op jit(solution)/shard_map/ppermute | solution.py:73
  90.1 17.4 %collective-permute-start.18 = (bf16[128,1024]{1,0:T(8,128)(2,1)}, bf16[128,1024]{1,0:T(8,128)(2,1)S(1)}, u32[]{:S(2)}, u32[]{:S(2)}) collective-permute-start(bf16[128,1024]{1,0:T(8,128)(2,1)} %get-tuple-element.151.refs_4_), channel_id=1, source_target_pairs={{0,2},{2,0},{4,6},{6,4},{8,10},{10,8},{12,14},{14,12},{16,18},{18,... | collective-permute-start | bytes 786440 | tf_op jit(solution)/shard_map/ppermute | solution.py:85
  108.4 35.3 %collective-permute-start.22 = (bf16[4,2,64,1024]{3,2,1,0:T(8,128)(2,1)S(1)}, bf16[4,2,64,1024]{3,2,1,0:T(8,128)(2,1)S(1)}, u32[]{:S(2)}, u32[]{:S(2)}) collective-permute-start(bf16[4,2,64,1024]{3,2,1,0:T(8,128)(2,1)S(1)} %pad_maximum_fusion.2), channel_id=1, source_target_pairs={{0,4},{2,6},{4,0},{6,2},{8,12},{10,14},{12,8},{14,10},{16,20},{18,... | collective-permute-start | bytes 3145736 | tf_op jit(solution)/shard_map/ppermute | solution.py:73
  116.1 27.5 %collective-permute-start.23 = (bf16[256,1024]{1,0:T(8,128)(2,1)}, bf16[256,1024]{1,0:T(8,128)(2,1)S(1)}, u32[]{:S(2)}, u32[]{:S(2)}) collective-permute-start(bf16[256,1024]{1,0:T(8,128)(2,1)} %get-tuple-element.158), channel_id=1, source_target_pairs={{0,1},{1,0},{2,3},{3,2},{4,5},{5,4},{6,7},{7,6},{8,9},{9,8},{10,11... | collective-permute-start | bytes 1572872 | tf_op jit(solution)/shard_map/ppermute | solution.py:736
  117.2 25.3 %collective-permute-start.20 = (bf16[2,64,1024]{2,1,0:T(8,128)(2,1)}, bf16[2,64,1024]{2,1,0:T(8,128)(2,1)S(1)}, u32[]{:S(2)}, u32[]{:S(2)}) collective-permute-start(bf16[2,64,1024]{2,1,0:T(8,128)(2,1)} %pad_maximum_fusion.11), channel_id=1, source_target_pairs={{0,16},{2,18},{4,20},{6,22},{8,24},{10,26},{12,28},{14,30},{16,0},... | collective-permute-start | bytes 786440 | tf_op jit(solution)/shard_map/ppermute | solution.py:73
  118.9 23.7 %collective-permute-start.21 = (bf16[2,64,1024]{2,1,0:T(8,128)(2,1)}, bf16[2,64,1024]{2,1,0:T(8,128)(2,1)S(1)}, u32[]{:S(2)}, u32[]{:S(2)}) collective-permute-start(bf16[2,64,1024]{2,1,0:T(8,128)(2,1)} %pad_maximum_fusion.11), channel_id=1, source_target_pairs={{0,8},{2,10},{4,12},{6,14},{8,16},{10,18},{12,20},{14,22},{16,24},... | collective-permute-start | bytes 786440 | tf_op jit(solution)/shard_map/ppermute | solution.py:73
  125.3 20.9 %collective-permute-start.25 = (bf16[128,1024]{1,0:T(8,128)(2,1)S(1)}, bf16[128,1024]{1,0:T(8,128)(2,1)S(1)}, u32[]{:S(2)}, u32[]{:S(2)}) collective-permute-start(bf16[128,1024]{1,0:T(8,128)(2,1)S(1)} %pad_maximum_fusion.12), channel_id=1, source_target_pairs={{0,2},{2,0},{4,6},{6,4},{8,10},{10,8},{12,14},{14,12},{16,18},{18,... | collective-permute-start | bytes 786440 | tf_op jit(solution)/shard_map/ppermute | solution.py:85
  143.7 38.2 %collective-permute-start.32 = (bf16[4,2,64,1024]{3,2,1,0:T(8,128)(2,1)S(1)}, bf16[4,2,64,1024]{3,2,1,0:T(8,128)(2,1)}, u32[]{:S(2)}, u32[]{:S(2)}) collective-permute-start(bf16[4,2,64,1024]{3,2,1,0:T(8,128)(2,1)S(1)} %pad_maximum_fusion.3), channel_id=1, source_target_pairs={{0,4},{2,6},{4,0},{6,2},{8,12},{10,14},{12,8},{14,10},{16,20},{18,... | collective-permute-start | bytes 3145736 | tf_op jit(solution)/shard_map/ppermute | solution.py:73
  181.6 26.9 %collective-permute-start.31 = (bf16[4,2,64,1024]{3,2,1,0:T(8,128)(2,1)}, bf16[4,2,64,1024]{3,2,1,0:T(8,128)(2,1)S(1)}, u32[]{:S(2)}, u32[]{:S(2)}) collective-permute-start(bf16[4,2,64,1024]{3,2,1,0:T(8,128)(2,1)} %bitcast.289), channel_id=1, source_target_pairs={{0,4},{2,6},{4,0},{6,2},{8,12},{10,14},{12,8},{14,10},{16,20},{18,... | collective-permute-start | bytes 3145736 | tf_op jit(solution)/shard_map/ppermute | solution.py:78
  195.2 21.7 %collective-permute-start.57 = (bf16[256,1024]{1,0:T(8,128)(2,1)}, bf16[256,1024]{1,0:T(8,128)(2,1)S(1)}, u32[]{:S(2)}, u32[]{:S(2)}) collective-permute-start(bf16[256,1024]{1,0:T(8,128)(2,1)} %get-tuple-element.225), channel_id=1, source_target_pairs={{0,1},{1,0},{2,3},{3,2},{4,5},{5,4},{6,7},{7,6},{8,9},{9,8},{10,11... | collective-permute-start | bytes 1572872 | tf_op jit(solution)/shard_map/ppermute | solution.py:736
  213.7 19.8 %collective-permute-start.36 = (bf16[2,64,1024]{2,1,0:T(8,128)(2,1)}, bf16[2,64,1024]{2,1,0:T(8,128)(2,1)}, u32[]{:S(2)}, u32[]{:S(2)}) collective-permute-start(bf16[2,64,1024]{2,1,0:T(8,128)(2,1)} %get-tuple-element.266), channel_id=1, source_target_pairs={{0,16},{2,18},{4,20},{6,22},{8,24},{10,26},{12,28},{14,30},{16,0},... | collective-permute-start | bytes 786440 | tf_op jit(solution)/shard_map/ppermute | solution.py:78
  214.0 21.9 %collective-permute-start.37 = (bf16[2,64,1024]{2,1,0:T(8,128)(2,1)}, bf16[2,64,1024]{2,1,0:T(8,128)(2,1)}, u32[]{:S(2)}, u32[]{:S(2)}) collective-permute-start(bf16[2,64,1024]{2,1,0:T(8,128)(2,1)} %get-tuple-element.265), channel_id=1, source_target_pairs={{0,24},{2,26},{4,28},{6,30},{8,0},{10,2},{12,4},{14,6},{16,8},{18,... | collective-permute-start | bytes 786440 | tf_op jit(solution)/shard_map/ppermute | solution.py:78
  216.9 19.0 %collective-permute-start.46 = (bf16[128,1024]{1,0:T(8,128)(2,1)S(1)}, bf16[128,1024]{1,0:T(8,128)(2,1)}, u32[]{:S(2)}, u32[]{:S(2)}) collective-permute-start(bf16[128,1024]{1,0:T(8,128)(2,1)S(1)} %copy-done.40), channel_id=1, source_target_pairs={{0,2},{2,0},{4,6},{6,4},{8,10},{10,8},{12,14},{14,12},{16,18},{18,... | collective-permute-start | bytes 786440 | tf_op jit(solution)/shard_map/ppermute | solution.py:85
  218.2 38.4 %collective-permute-start.38 = (bf16[4,2,64,1024]{3,2,1,0:T(8,128)(2,1)}, bf16[4,2,64,1024]{3,2,1,0:T(8,128)(2,1)}, u32[]{:S(2)}, u32[]{:S(2)}) collective-permute-start(bf16[4,2,64,1024]{3,2,1,0:T(8,128)(2,1)} %bitcast.288), channel_id=1, source_target_pairs={{0,4},{2,6},{4,0},{6,2},{8,12},{10,14},{12,8},{14,10},{16,20},{18,... | collective-permute-start | bytes 3145736 | tf_op jit(solution)/shard_map/ppermute | solution.py:78
  222.2 15.5 %collective-permute-start.40 = (bf16[128,1024]{1,0:T(8,128)(2,1)S(1)}, bf16[128,1024]{1,0:T(8,128)(2,1)S(1)}, u32[]{:S(2)}, u32[]{:S(2)}) collective-permute-start(bf16[128,1024]{1,0:T(8,128)(2,1)S(1)} %copy-done.19), channel_id=1, source_target_pairs={{0,1},{1,0},{2,3},{3,2},{4,5},{5,4},{6,7},{7,6},{8,9},{9,8},{10,11... | collective-permute-start | bytes 786440 | tf_op jit(solution)/shard_map/ppermute | solution.py:736
  233.4 32.7 %collective-permute-start.47 = (bf16[128,1024]{1,0:T(8,128)(2,1)S(1)}, bf16[128,1024]{1,0:T(8,128)(2,1)S(1)}, u32[]{:S(2)}, u32[]{:S(2)}) collective-permute-start(bf16[128,1024]{1,0:T(8,128)(2,1)S(1)} %copy-done.40), channel_id=1, source_target_pairs={{0,1},{1,0},{2,3},{3,2},{4,5},{5,4},{6,7},{7,6},{8,9},{9,8},{10,11... | collective-permute-start | bytes 786440 | tf_op jit(solution)/shard_map/ppermute | solution.py:736
  236.0 30.2 %collective-permute-start.48 = (bf16[128,1024]{1,0:T(8,128)(2,1)}, bf16[128,1024]{1,0:T(8,128)(2,1)}, u32[]{:S(2)}, u32[]{:S(2)}) collective-permute-start(bf16[128,1024]{1,0:T(8,128)(2,1)} %collective-permute-done.46.refs_5_), channel_id=1, source_target_pairs={{0,1},{1,0},{2,3},{3,2},{4,5},{5,4},{6,7},{7,6},{8,9},{9,8},{10,11... | collective-permute-start | bytes 786440 | tf_op jit(solution)/shard_map/ppermute | solution.py:736
  258.3 27.7 %collective-permute-start.45 = (bf16[4,2,64,1024]{3,2,1,0:T(8,128)(2,1)}, bf16[4,2,64,1024]{3,2,1,0:T(8,128)(2,1)}, u32[]{:S(2)}, u32[]{:S(2)}) collective-permute-start(bf16[4,2,64,1024]{3,2,1,0:T(8,128)(2,1)} %bitcast.68), channel_id=1, source_target_pairs={{0,4},{2,6},{4,0},{6,2},{8,12},{10,14},{12,8},{14,10},{16,20},{18,... | collective-permute-start | bytes 3145736 | tf_op jit(solution)/shard_map/ppermute | solution.py:78
  259.6 18.3 %collective-permute-start.73 = (bf16[64,1024]{1,0:T(8,128)(2,1)S(1)}, bf16[64,1024]{1,0:T(8,128)(2,1)S(1)}, u32[]{:S(2)}, u32[]{:S(2)}) collective-permute-start(bf16[64,1024]{1,0:T(8,128)(2,1)S(1)} %fusion.16), channel_id=1, source_target_pairs={{0,2},{2,0},{4,6},{6,4},{8,10},{10,8},{12,14},{14,12},{16,18},{18,... | collective-permute-start | bytes 393224 | tf_op jit(solution)/shard_map/ppermute | solution.py:85
  260.8 23.9 %collective-permute-start.42 = (bf16[2,64,1024]{2,1,0:T(8,128)(2,1)}, bf16[2,64,1024]{2,1,0:T(8,128)(2,1)}, u32[]{:S(2)}, u32[]{:S(2)}) collective-permute-start(bf16[2,64,1024]{2,1,0:T(8,128)(2,1)} %get-tuple-element.261), channel_id=1, source_target_pairs={{0,8},{2,10},{4,12},{6,14},{8,16},{10,18},{12,20},{14,22},{16,24},... | collective-permute-start | bytes 786440 | tf_op jit(solution)/shard_map/ppermute | solution.py:78
  266.1 18.6 %collective-permute-start.43 = (bf16[2,64,1024]{2,1,0:T(8,128)(2,1)}, bf16[2,64,1024]{2,1,0:T(8,128)(2,1)S(1)}, u32[]{:S(2)}, u32[]{:S(2)}) collective-permute-start(bf16[2,64,1024]{2,1,0:T(8,128)(2,1)} %get-tuple-element.263), channel_id=1, source_target_pairs={{0,16},{2,18},{4,20},{6,22},{8,24},{10,26},{12,28},{14,30},{16,0},... | collective-permute-start | bytes 786440 | tf_op jit(solution)/shard_map/ppermute | solution.py:78
  266.2 18.6 %collective-permute-start.44 = (bf16[2,64,1024]{2,1,0:T(8,128)(2,1)}, bf16[2,64,1024]{2,1,0:T(8,128)(2,1)S(1)}, u32[]{:S(2)}, u32[]{:S(2)}) collective-permute-start(bf16[2,64,1024]{2,1,0:T(8,128)(2,1)} %get-tuple-element.262), channel_id=1, source_target_pairs={{0,24},{2,26},{4,28},{6,30},{8,0},{10,2},{12,4},{14,6},{16,8},{18,... | collective-permute-start | bytes 786440 | tf_op jit(solution)/shard_map/ppermute | solution.py:78
  289.2 24.8 %collective-permute-start.56 = (bf16[128,2048]{1,0:T(8,128)(2,1)S(1)}, bf16[128,2048]{1,0:T(8,128)(2,1)S(1)}, u32[]{:S(2)}, u32[]{:S(2)}) collective-permute-start(bf16[128,2048]{1,0:T(8,128)(2,1)S(1)} %add_convert_fusion.3), channel_id=1, source_target_pairs={{0,2},{2,0},{4,6},{6,4},{8,10},{10,8},{12,14},{14,12},{16,18},{18,... | collective-permute-start | bytes 1572872 | tf_op jit(solution)/shard_map/ppermute | solution.py:85
  289.6 45.6 %collective-permute-start.54 = (bf16[4,2,64,1152]{3,2,1,0:T(8,128)(2,1)}, bf16[4,2,64,1152]{3,2,1,0:T(8,128)(2,1)}, u32[]{:S(2)}, u32[]{:S(2)}) collective-permute-start(bf16[4,2,64,1152]{3,2,1,0:T(8,128)(2,1)} %bitcast.74), channel_id=1, source_target_pairs={{0,4},{2,6},{4,0},{6,2},{8,12},{10,14},{12,8},{14,10},{16,20},{18,... | collective-permute-start | bytes 3538952 | tf_op jit(solution)/shard_map/ppermute | solution.py:78
  296.0 17.9 %collective-permute-start.52 = (bf16[2,64,1024]{2,1,0:T(8,128)(2,1)S(1)}, bf16[2,64,1024]{2,1,0:T(8,128)(2,1)S(1)}, u32[]{:S(2)}, u32[]{:S(2)}) collective-permute-start(bf16[2,64,1024]{2,1,0:T(8,128)(2,1)S(1)} %get-tuple-element.260), channel_id=1, source_target_pairs={{0,16},{2,18},{4,20},{6,22},{8,24},{10,26},{12,28},{14,30},{16,0},... | collective-permute-start | bytes 786440 | tf_op jit(solution)/shard_map/ppermute | solution.py:78
  296.2 17.7 %collective-permute-start.53 = (bf16[2,64,1024]{2,1,0:T(8,128)(2,1)S(1)}, bf16[2,64,1024]{2,1,0:T(8,128)(2,1)S(1)}, u32[]{:S(2)}, u32[]{:S(2)}) collective-permute-start(bf16[2,64,1024]{2,1,0:T(8,128)(2,1)S(1)} %get-tuple-element.259), channel_id=1, source_target_pairs={{0,24},{2,26},{4,28},{6,30},{8,0},{10,2},{12,4},{14,6},{16,8},{18,... | collective-permute-start | bytes 786440 | tf_op jit(solution)/shard_map/ppermute | solution.py:78
  300.3 13.8 %collective-permute-start.58 = (bf16[128,1024]{1,0:T(8,128)(2,1)S(1)}, bf16[128,1024]{1,0:T(8,128)(2,1)S(1)}, u32[]{:S(2)}, u32[]{:S(2)}) collective-permute-start(bf16[128,1024]{1,0:T(8,128)(2,1)S(1)} %copy-done.51), channel_id=1, source_target_pairs={{0,2},{2,0},{4,6},{6,4},{8,10},{10,8},{12,14},{14,12},{16,18},{18,... | collective-permute-start | bytes 786440 | tf_op jit(solution)/shard_map/ppermute | solution.py:85
  337.4 18.0 %collective-permute-start.72 = (bf16[64,1024]{1,0:T(8,128)(2,1)}, bf16[64,1024]{1,0:T(8,128)(2,1)S(1)}, u32[]{:S(2)}, u32[]{:S(2)}) collective-permute-start(bf16[64,1024]{1,0:T(8,128)(2,1)} %fusion.15), channel_id=1, source_target_pairs={{0,2},{2,0},{4,6},{6,4},{8,10},{10,8},{12,14},{14,12},{16,18},{18,... | collective-permute-start | bytes 393224 | tf_op jit(solution)/shard_map/ppermute | solution.py:85
  339.5 43.1 %collective-permute-start.67 = (bf16[2,64,1152]{2,1,0:T(8,128)(2,1)}, bf16[2,64,1152]{2,1,0:T(8,128)(2,1)S(1)}, u32[]{:S(2)}, u32[]{:S(2)}) collective-permute-start(bf16[2,64,1152]{2,1,0:T(8,128)(2,1)} %get-tuple-element.255), channel_id=1, source_target_pairs={{0,8},{2,10},{4,12},{6,14},{8,16},{10,18},{12,20},{14,22},{16,24},... | collective-permute-start | bytes 884744 | tf_op jit(solution)/shard_map/ppermute | solution.py:78
  345.5 37.1 %collective-permute-start.68 = (bf16[2,64,1152]{2,1,0:T(8,128)(2,1)}, bf16[2,64,1152]{2,1,0:T(8,128)(2,1)S(1)}, u32[]{:S(2)}, u32[]{:S(2)}) collective-permute-start(bf16[2,64,1152]{2,1,0:T(8,128)(2,1)} %get-tuple-element.257), channel_id=1, source_target_pairs={{0,16},{2,18},{4,20},{6,22},{8,24},{10,26},{12,28},{14,30},{16,0},... | collective-permute-start | bytes 884744 | tf_op jit(solution)/shard_map/ppermute | solution.py:78
  345.5 37.1 %collective-permute-start.69 = (bf16[2,64,1152]{2,1,0:T(8,128)(2,1)S(1)}, bf16[2,64,1152]{2,1,0:T(8,128)(2,1)}, u32[]{:S(2)}, u32[]{:S(2)}) collective-permute-start(bf16[2,64,1152]{2,1,0:T(8,128)(2,1)S(1)} %get-tuple-element.256), channel_id=1, source_target_pairs={{0,24},{2,26},{4,28},{6,30},{8,0},{10,2},{12,4},{14,6},{16,8},{18,... | collective-permute-start | bytes 884744 | tf_op jit(solution)/shard_map/ppermute | solution.py:78
  358.5 17.4 %collective-permute-start.62 = (f32[24,1024]{1,0:T(8,128)S(1)}, f32[24,1024]{1,0:T(8,128)S(1)}, u32[]{:S(2)}, u32[]{:S(2)}) collective-permute-start(f32[24,1024]{1,0:T(8,128)S(1)} %fusion.58), channel_id=1, source_target_pairs={{0,16},{2,18},{4,20},{6,22},{8,24},{10,26},{12,28},{14,30},{16,0},... | collective-permute-start | bytes 294920 | tf_op jit(solution)/shard_map/ppermute | solution.py:73
  359.3 17.3 %collective-permute-start.63 = (f32[24,1024]{1,0:T(8,128)S(1)}, f32[24,1024]{1,0:T(8,128)S(1)}, u32[]{:S(2)}, u32[]{:S(2)}) collective-permute-start(f32[24,1024]{1,0:T(8,128)S(1)} %fusion.58), channel_id=1, source_target_pairs={{0,24},{2,26},{4,28},{6,30},{8,0},{10,2},{12,4},{14,6},{16,8},{18,... | collective-permute-start | bytes 294920 | tf_op jit(solution)/shard_map/ppermute | solution.py:73
  376.7 19.3 %collective-permute-start.59 = (bf16[2,128,1024]{2,1,0:T(8,128)(2,1)S(1)}, bf16[2,128,1024]{2,1,0:T(8,128)(2,1)S(1)}, u32[]{:S(2)}, u32[]{:S(2)}) collective-permute-start(bf16[2,128,1024]{2,1,0:T(8,128)(2,1)S(1)} %pad_maximum_fusion.4), channel_id=1, source_target_pairs={{0,1},{1,0},{2,3},{3,2},{4,5},{5,4},{6,7},{7,6},{8,9},{9,8},{10,11... | collective-permute-start | bytes 1572872 | tf_op jit(solution)/shard_map/ppermute | solution.py:736
  (100 other events, 930.1 us)

commit v3 on v2

--- a/solution.py
+++ b/solution.py
@@ -85,8 +85,10 @@
         return lax.ppermute(value, "dp", self.shift(self.near, 1))
 
     def sum_all(self, value):
-        for dim, r in reversed(list(enumerate(self.radix))):
-            got = self.fetch(value, dim)
+        for dim in [self.near, *range(self.line), self.line]:
+            r = self.radix[dim]
+            got = self.fetch(value.astype(bf16) if dim == self.line else value, dim)
+            got = [g.astype(f32) for g in got]
             if r == 4:
                 value = (got[0] + got[2]) + (got[1] + got[3])
             elif r == 2:
@@ -196,11 +198,16 @@
         parts = [self.value[k] for k in range(self.grid.radix[self.grid.line])]
         self.value = total_of(self.grid.deliver(parts, self.grid.line))
 
-    def near(self):
+    def near(self, cuts=()):
         near = self.grid.near_index()
         kept = lax.dynamic_index_in_dim(self.value, near, 0, keepdims=False)
         sent = lax.dynamic_index_in_dim(self.value, 1 - near, 0, keepdims=False)
-        return kept, self.grid.near_swap(sent.astype(bf16)).astype(f32)
+        edges = [0, *cuts, sent.shape[1]]
+        came = [
+            self.grid.near_swap(sent[:, a:b].astype(bf16)).astype(f32)
+            for a, b in zip(edges, edges[1:])
+        ]
+        return (kept, *came)
 
 
 def tiles_of(array):
@@ -251,10 +258,15 @@
     return jnp.concatenate([right_inner(x, w[:, start:stop]) for w in blocks], axis=1)
 
 
+def two_terms(value):
+    high = value.astype(bf16)
+    return [high, (value - high.astype(f32)).astype(bf16)]
+
+
 def to_absolute(value, spread):
-    high = value.astype(bf16)
-    low = (value - high.astype(f32)).astype(bf16)
-    return right_inner(high, spread) + right_inner(low, spread)
+    rows = value.shape[0]
+    out = right_inner(jnp.concatenate(two_terms(value), axis=0), spread)
+    return out[:rows] + out[rows:]
 
 
 def column_sum(values):
@@ -270,11 +282,9 @@
     hat, unused = norm_parts(x_ref)
     normed = hat * gain_ref[...]
     normed_ref[...] = normed
-    packed_ref[:, width:] = product(normed.astype(bf16), spread).astype(bf16)
     live = lax.broadcasted_iota(jnp.int32, (steps, 1), 0) < place_ref[2]
     seed = jnp.where(live, seed_ref[...].astype(f32), 0.0)
     seed_sum_ref[...] = column_sum(seed)
-    seed_low_ref[...] = product(seed.astype(bf16), spread).astype(bf16)
     rate = jax.nn.sigmoid(params_ref[0])
     keep = 1.0 - rate * jax.nn.sigmoid(params_ref[1])
     weight = params_ref[3] * (rate * params_ref[2])
@@ -303,36 +313,42 @@
 
     lax.fori_loop(0, width // LANES, block, 0)
     pre = pre_ref[...]
-    packed_ref[:, :width] = product((pre * jax.nn.sigmoid(pre)).astype(bf16), spread).astype(bf16)
+    smooth = (pre * jax.nn.sigmoid(pre)).astype(bf16)
+    rows = jnp.concatenate([smooth, normed_ref[...].astype(bf16), seed.astype(bf16)], axis=0)
+    rows = product(rows, spread).astype(bf16)
+    packed_ref[:, :width] = rows[:steps]
+    packed_ref[:, width:] = rows[steps : 2 * steps]
+    seed_low_ref[...] = rows[2 * steps :]
 
 
 def ema_backward_kernel(
     place_ref,
     x_ref, gain_ref, direct_ref, params_ref, spread_ref, table_ref, normed_ref, pre_ref,
-    kept_ref, core_ref, near_ref, grad_shared_ref, grad_input_ref,
-    down_kept_ref, down_core_ref, down_near_ref, blended_ref, offset_ref, *rest,
+    kept_ref, core_0, core_1, core_2, core_3, near_ref,
+    grad_shared_ref, grad_input_ref, row_sums_ref, seed_sum_ref,
+    narrow_ref, down_kept_ref, down_core_ref, down_near_ref, blended_ref, offset_ref, *rest,
 ):
-    weights = rest[:-8]
-    (
-        grad_row_ref, out_row_ref, vectors_ref, zero_ref, first_ref,
-        smooth_ref, inner_ref, lag_ref,
-    ) = rest[-8:]
+    weights = rest[:-7]
+    grad_row_ref, out_row_ref, keep_ref, send_ref, smooth_ref, inner_ref, lag_ref = rest[-7:]
+    vectors_ref = send_ref
     steps, width = x_ref.shape
     count = steps // SUBLANES
     sub = lax.broadcasted_iota(jnp.int32, (steps, LANES), 0)
     spread = spread_ref[...]
 
     down = down_kept_ref[:steps] + down_core_ref[:steps].astype(f32) + down_near_ref[...].astype(f32)
-    down = right_inner(down.astype(bf16), spread)
+    core = [p[:steps].astype(f32) for p in (core_0, core_1, core_2, core_3)]
+    sums = kept_ref[:steps] + jnp.concatenate(core, axis=1) + near_ref[...].astype(f32)
+    smooth, norm = sums[:, :width], sums[:, width:]
+    span = weights[0].shape[1] - LANES
+    smooth = smooth + times_t(grad_shared_ref[...], weights, span, span + LANES)
+    terms = [down.astype(bf16), *two_terms(smooth), *two_terms(norm)]
+    out = right_inner(jnp.concatenate(terms, axis=0), spread)
+    smooth_ref[...] = out[steps : 2 * steps] + out[2 * steps : 3 * steps]
+    inner_ref[...] = out[3 * steps : 4 * steps] + out[4 * steps :]
     live = lax.broadcasted_iota(jnp.int32, (steps, 1), 0) < place_ref[2]
-    out = blended_ref[...] + down + offset_ref[...]
-    out_row_ref[...] = jnp.where(live, out, 0.0).astype(bf16)
-
-    sums = kept_ref[:steps] + core_ref[:steps].astype(f32) + near_ref[...].astype(f32)
-    span = weights[0].shape[1] - LANES
-    smooth = sums[:, :width] + times_t(grad_shared_ref[...], weights, span, span + LANES)
-    smooth_ref[...] = to_absolute(smooth, spread)
-    inner_ref[...] = to_absolute(sums[:, width:], spread)
+    out_row = blended_ref[...] + out[:steps] + offset_ref[...]
+    out_row_ref[...] = jnp.where(live, out_row, 0.0).astype(bf16)
 
     def block(c, carry):
         columns = pl.ds(pl.multiple_of(c * LANES, LANES), LANES)
@@ -361,7 +377,9 @@
     lax.fori_loop(0, width // LANES, block, 0)
 
     keep_all = 1.0 - jax.nn.sigmoid(params_ref[0]) * jax.nn.sigmoid(params_ref[1])
-    half = keep_all.shape[0] // 2
+    states = keep_all.shape[0]
+    half = states // 2
+    sums_of_lags = [[], []]
     for h in range(2):
         keep = keep_all[h * half : (h + 1) * half]
 
@@ -375,64 +393,80 @@
         blank = jnp.zeros_like(keep)
         start = (jnp.ones_like(keep), blank + lag_ref[0][None], blank)
         unused, zero, first = lax.fori_loop(1, steps, lag_step, start)
-        zero_ref[h * half : (h + 1) * half] = zero
-        first_ref[h * half : (h + 1) * half] = first
+        sums_of_lags[0].append(zero)
+        sums_of_lags[1].append(first)
 
     hat, scale = norm_parts(x_ref)
     grad = inner_ref[...]
-    vectors_ref[0:1] = column_sum(grad * hat)
+    prenorm = column_sum(grad * hat)
     grad = grad * gain_ref[...]
     grad = grad - jnp.mean(grad, axis=-1, keepdims=True) - hat * jnp.mean(
         grad * hat, axis=-1, keepdims=True
     )
     grad_row_ref[...] = (grad_input_ref[...] + scale * grad).astype(bf16)
+
+    def flat(states_first):
+        blocks = range(width // LANES)
+        return jnp.concatenate([states_first[:, c] for c in blocks], axis=1)
+
+    zero, first = [flat(jnp.concatenate(part, axis=0)) for part in sums_of_lags]
+    narrow = jnp.concatenate([narrow_ref[k : k + 1] for k in range(4)], axis=1)
+    narrow = jnp.concatenate([narrow, jnp.zeros((1, width - narrow.shape[1]), f32)], axis=1)
+    rest_rows = [prenorm, vectors_ref[1:2], row_sums_ref[...], seed_sum_ref[...], narrow]
+    rest_rows = jnp.concatenate(rest_rows + [jnp.zeros((1, width), f32)], axis=0)
+    keep, send = pick(place_ref[1], zero, first)
+    keep_rest, send_rest = pick(place_ref[1], rest_rows, jnp.zeros_like(rest_rows))
+    keep_ref[:states] = keep
+    keep_ref[states:] = keep_rest
+    send_ref[:states] = send
+    send_ref[states:] = send_rest
 
 
 def attention_kernel(
     place_ref, p0, p1, p2, p3, value_offset_ref, common_offset_ref, ask_gain_ref, ask_offset_ref,
     look_gain_ref, *rest,
 ):
-    weights = rest[:-10]
+    weights = rest[:-11]
     (
-        value_pre_ref, value_ref, gates_kept_ref, gates_sent_ref, probs_low_ref, attended_ref,
-        shared_pre_ref, query_ref, key_ref, probs_ref,
-    ) = rest[-10:]
+        value_pre_ref, value_ref, gates_ref, gates_core_ref, gates_near_ref, probs_low_ref,
+        attended_ref, shared_pre_ref, query_ref, key_ref, probs_ref,
+    ) = rest[-11:]
     steps = p0.shape[0]
     width = p0.shape[1] // 2
     span = value_ref.shape[1]
-    gates_size = gates_kept_ref.shape[1]
+    gates_size = gates_ref.shape[1]
     at = lax.broadcasted_iota(jnp.int32, (steps, steps), 0)
     to = lax.broadcasted_iota(jnp.int32, (steps, steps), 1)
-    for p, packed in enumerate((p0, p1, p2, p3)):
+    pieces = (p0, p1, p2, p3)
+    smooth = jnp.concatenate([p[:, :width] for p in pieces], axis=0)
+    norm = jnp.concatenate([p[:, width:] for p in pieces], axis=0)
+    value_pre = times(norm, weights, 0, span) + value_offset_ref[...]
+    value_pre_ref[...] = value_pre
+    value_ref[...] = (value_pre * sigma_of(value_pre)).astype(bf16)
+    gates = times(smooth, weights, span, span + gates_size)
+    gates_ref[...] = gates[:steps]
+    gates_core_ref[...] = gates[2 * steps : 3 * steps]
+    gates_near_ref[:steps] = gates[steps : 2 * steps].astype(bf16)
+    gates_near_ref[steps:] = gates[3 * steps :].astype(bf16)
+    start = span + gates_size
+    shared_pre = times(smooth, weights, start, start + LANES) + common_offset_ref[...]
+    shared = shared_pre * sigma_of(shared_pre)
+    query = (shared * ask_gain_ref[...] + ask_offset_ref[...]).astype(bf16)
+    key = (shared * look_gain_ref[...]).astype(bf16)
+    shared_pre_ref[...] = shared_pre[:steps]
+    query_ref[...] = query[:steps]
+    key_ref[...] = key[:steps]
+    for p in range(4):
         here = slice(p * steps, (p + 1) * steps)
-        smooth = packed[:, :width]
-        value_pre = times(packed[:, width:], weights, 0, span) + value_offset_ref[...]
-        value_pre_ref[here] = value_pre
-        value = (value_pre * sigma_of(value_pre)).astype(bf16)
-        value_ref[here] = value
-        gates = times(smooth, weights, span, span + gates_size)
-        half = slice((p % 2) * steps, (p % 2 + 1) * steps)
-        if p < 2:
-            gates_kept_ref[half] = gates
-        else:
-            gates_sent_ref[half] = gates
-        start = span + gates_size
-        shared_pre = times(smooth, weights, start, start + LANES) + common_offset_ref[...]
-        shared = shared_pre * sigma_of(shared_pre)
-        query = (shared * ask_gain_ref[...] + ask_offset_ref[...]).astype(bf16)
-        key = (shared * look_gain_ref[...]).astype(bf16)
-        scores = right_inner(query, key) * (COMMON_SPAN_DIM ** (-0.5))
+        scores = right_inner(query[here], key[here]) * (COMMON_SPAN_DIM ** (-0.5))
         allowed = (to <= at) & ((to < place_ref[2 + p]) | (to == at))
         scores = jnp.where(allowed, scores, -1e30)
         probs = jnp.exp(scores - jnp.max(scores, axis=-1, keepdims=True))
         probs = probs / jnp.sum(probs, axis=-1, keepdims=True)
         probs_low = probs.astype(bf16)
         probs_low_ref[here] = probs_low
-        attended_ref[here] = product(probs_low, value)
+        attended_ref[here] = product(probs_low, value_ref[here])
         if p == 0:
-            shared_pre_ref[...] = shared_pre
-            query_ref[...] = query
-            key_ref[...] = key
             probs_ref[...] = probs
 
 
@@ -442,18 +476,14 @@
     steps = p0.shape[0]
     width = p0.shape[1] // 2
     span = mixed_ref.shape[1]
-    for p, packed in enumerate((p0, p1, p2, p3)):
-        here = slice(p * steps, (p + 1) * steps)
-        reset_pre = times(packed[:, :width], weights, 0, span) + offset_ref[...]
-        reset_pre_ref[here] = reset_pre
-        mixed = (reset_pre * sigma_of(reset_pre) * attended_ref[here]).astype(bf16)
-        mixed_ref[here] = mixed
-        part = times_t(mixed, weights, span, 2 * span)
-        half = slice((p % 2) * steps, (p % 2 + 1) * steps)
-        if p < 2:
-            kept_ref[half] = part
-        else:
-            sent_ref[half] = part.astype(bf16)
+    smooth = jnp.concatenate([p[:, :width] for p in (p0, p1, p2, p3)], axis=0)
+    reset_pre = times(smooth, weights, 0, span) + offset_ref[...]
+    reset_pre_ref[...] = reset_pre
+    mixed = (reset_pre * sigma_of(reset_pre) * attended_ref[...]).astype(bf16)
+    mixed_ref[...] = mixed
+    part = times_t(mixed, weights, span, 2 * span)
+    kept_ref[...] = part[: 2 * steps]
+    sent_ref[...] = part[2 * steps :].astype(bf16)
 
 
 def pick(index, own, other):
@@ -462,7 +492,8 @@
 
 
 def hidden_kernel(
-    place_ref, x_ref, kept_ref, core_ref, near_ref, gates_ref, gates_core_ref, gates_near_ref,
+    place_ref, x_ref, kept_ref, core_ref, near_ref,
+    gates_ref, gates_core_ref, gates_near_ref, gates_far_ref,
     update_offset_ref, hidden_offset_ref, gain_ref, spread_ref,
     hidden_pre_ref, update_ref, blended_ref, hat_ref, scale_ref, low_ref,
 ):
@@ -471,8 +502,10 @@
     part = kept_ref[:steps] + core_ref[:steps].astype(f32) + near_ref[...].astype(f32)
     size = gates_ref.shape[1] // 2
     sides = []
-    for c, own in enumerate((gates_ref[:steps], gates_core_ref[:steps])):
-        other = gates_near_ref[:, c * 2 * size : (c + 1) * 2 * size].astype(f32)
+    for own, other in (
+        (gates_ref[...], gates_near_ref[:steps].astype(f32)),
+        (gates_core_ref[...], gates_far_ref[...].astype(f32)),
+    ):
         sides.append(
             [
                 jnp.concatenate(
@@ -511,44 +544,38 @@
     outs = refs[at + count :]
     grad_pre_ref, act_ref, bias_ref = outs[:3]
     steps = f[0].shape[0]
-    width = f[0].shape[1]
     span = act_ref.shape[1]
-    for p in range(4):
-        here = slice(p * steps, (p + 1) * steps)
-        pre = times(f[p][...], weights, 0, span) + offset_ref[...]
-        sigma = sigma_of(pre)
-        act = (pre * sigma).astype(bf16)
-        act_ref[here] = act
-        grad = times(seeds[p][...], weights, span, 2 * span)
-        grad = (grad * (sigma * (1.0 + pre * (1.0 - sigma)))).astype(bf16)
-        grad_pre_ref[here] = grad
-        bias = column_sum(grad.astype(f32))
-        bias_ref[...] = bias if p == 0 else bias_ref[...] + bias
-        down = times_t(act, weights, span, 2 * span)
-        back = times_t(grad, weights, 0, span)
-        if first:
-            down_ref, back_ref = outs[3:5]
-            down_ref[here] = down
-            back_ref[here] = back
-            continue
-        down = down + down_before_ref[here]
-        back = back + back_before_ref[here]
-        down_kept_ref, down_sent_ref, back_kept_ref, back_sent_ref = outs[3:7]
-        half = slice((p % 2) * steps, (p % 2 + 1) * steps)
-        if p < 2:
-            down_kept_ref[half] = down
-            back_kept_ref[half] = back
-        else:
-            down_sent_ref[half] = down.astype(bf16)
-            back_sent_ref[half] = back.astype(bf16)
+    pre = times(jnp.concatenate([p[...] for p in f], axis=0), weights, 0, span) + offset_ref[...]
+    sigma = sigma_of(pre)
+    act = (pre * sigma).astype(bf16)
+    act_ref[...] = act
+    seed = jnp.concatenate([p[...] for p in seeds], axis=0)
+    grad = times(seed, weights, span, 2 * span)
+    grad = (grad * (sigma * (1.0 + pre * (1.0 - sigma)))).astype(bf16)
+    grad_pre_ref[...] = grad
+    bias_ref[...] = column_sum(grad.astype(f32))
+    down = times_t(act, weights, span, 2 * span)
+    back = times_t(grad, weights, 0, span)
+    if first:
+        down_ref, back_ref = outs[3:5]
+        down_ref[...] = down
+        back_ref[...] = back
+        return
+    down_kept_ref, down_sent_ref, back_kept_ref, back_sent_ref = outs[3:7]
+    down = down + down_before_ref[...]
+    down_kept_ref[...] = down[: 2 * steps]
+    down_sent_ref[...] = down[2 * steps :].astype(bf16)
+    back = back + back_before_ref[...]
+    back_kept_ref[...] = back[: 2 * steps]
+    back_sent_ref[...] = back[2 * steps :].astype(bf16)
 
 
 def blend_grad_kernel(
     place_ref, x_ref, seed_ref, kept_ref, core_ref, near_ref, hidden_pre_ref, update_ref, hat_ref,
     scale_ref, gain_ref, spread_ref,
-    grad_input_ref, hidden_low_ref, update_low_ref, sums_ref,
+    grad_input_ref, packed_ref, sums_ref,
 ):
-    steps = x_ref.shape[0]
+    steps, width = x_ref.shape
     spread = spread_ref[...]
     part = kept_ref[:steps] + core_ref[:steps].astype(f32) + near_ref[...].astype(f32)
     grad_norm = to_absolute(part, spread)
@@ -572,8 +599,8 @@
     grad_update = (
         grad_blended * (hidden_pre * sigma - values) * update * (1.0 - update)
     ).astype(bf16)
-    hidden_low_ref[...] = product(grad_hidden, spread).astype(bf16)
-    update_low_ref[...] = grad_update
+    packed_ref[:, :width] = product(grad_hidden, spread).astype(bf16)
+    packed_ref[:, width:] = grad_update
     sums_ref[0:1] = column_sum(grad_update.astype(f32))
     sums_ref[1:2] = column_sum(grad_hidden.astype(f32))
     sums_ref[2:3] = column_sum(grad_norm * hat)
@@ -586,60 +613,62 @@
     grad_reset_ref, grad_value_ref, kept_ref, sent_ref, sums_ref = rest[-5:]
     steps = h0.shape[0]
     span = value_ref.shape[1]
-    for p, h in enumerate((h0, h1, h2, h3)):
+    grad_mixed = times(
+        jnp.concatenate([h[:, : h.shape[1] // 2] for h in (h0, h1, h2, h3)], axis=0),
+        weights,
+        span,
+        2 * span,
+    )
+    reset_pre = reset_pre_ref[...]
+    sigma = sigma_of(reset_pre)
+    grad_attended = (grad_mixed * (reset_pre * sigma)).astype(bf16)
+    grad_reset = (
+        grad_mixed * attended_ref[...] * (sigma * (1.0 + reset_pre * (1.0 - sigma)))
+    ).astype(bf16)
+    grad_reset_ref[...] = grad_reset
+    sums_ref[1:2] = column_sum(grad_reset.astype(f32))
+    for p in range(4):
         here = slice(p * steps, (p + 1) * steps)
-        grad_mixed = times(h[...], weights, span, 2 * span)
-        reset_pre = reset_pre_ref[here]
-        sigma = sigma_of(reset_pre)
-        grad_attended = (grad_mixed * (reset_pre * sigma)).astype(bf16)
-        grad_reset = (
-            grad_mixed * attended_ref[here] * (sigma * (1.0 + reset_pre * (1.0 - sigma)))
-        ).astype(bf16)
-        grad_reset_ref[here] = grad_reset
-        part = right_inner(grad_attended, value_ref[here])
+        part = right_inner(grad_attended[here], value_ref[here])
         half = slice((p % 2) * steps, (p % 2 + 1) * steps)
         if p < 2:
             kept_ref[half] = part
         else:
             sent_ref[half] = part
-        grad_value = left_inner(probs_low_ref[here], grad_attended)
+        grad_value = left_inner(probs_low_ref[here], grad_attended[here])
         grad_value = (grad_value * silu_slope(value_pre_ref[here])).astype(bf16)
         grad_value_ref[here] = grad_value
-        terms = (column_sum(grad_value.astype(f32)), column_sum(grad_reset.astype(f32)))
-        for k, term in enumerate(terms):
-            row = slice(k, k + 1)
-            sums_ref[row] = term if p == 0 else sums_ref[row] + term
+        term = column_sum(grad_value.astype(f32))
+        sums_ref[0:1] = term if p == 0 else sums_ref[0:1] + term
 
 
 def input_grad_kernel(count, place_ref, *refs):
     h = refs[:4]
-    u = refs[4:8]
-    grad_reset_ref, grad_value_ref, spread_ref = refs[8:11]
-    first = refs[11 : 11 + count]
-    second = refs[11 + count : 11 + 2 * count]
-    gates_ref, kept_ref, sent_ref = refs[11 + 2 * count :]
-    steps, width = h[0].shape
+    grad_reset_ref, grad_value_ref, spread_ref = refs[4:7]
+    first = refs[7 : 7 + count]
+    second = refs[7 + count : 7 + 2 * count]
+    gates_ref, kept_ref, *sent = refs[7 + 2 * count :]
+    steps = h[0].shape[0]
+    width = h[0].shape[1] // 2
     span = grad_value_ref.shape[1]
     size = gates_ref.shape[1] // 2
     gate = pl.ds(pl.multiple_of(place_ref[6], size), size)
     rows = spread_ref[gate, :]
-    for p in range(4):
-        here = slice(p * steps, (p + 1) * steps)
-        gates = jnp.concatenate(
-            [u[p][:, gate], right_inner(h[p][...], rows).astype(bf16)], axis=1
-        )
-        gates_ref[here] = gates
-        smooth = times_t(grad_reset_ref[here], second, 0, span) + times_t(
-            gates, first, span, span + 2 * size
-        )
-        norm = times_t(grad_value_ref[here], first, 0, span)
-        half = slice((p % 2) * steps, (p % 2 + 1) * steps)
-        if p < 2:
-            kept_ref[half, :width] = smooth
-            kept_ref[half, width:] = norm
-        else:
-            sent_ref[half, :width] = smooth.astype(bf16)
-            sent_ref[half, width:] = norm.astype(bf16)
+    late = pl.ds(pl.multiple_of(width + place_ref[6], size), size)
+    update = jnp.concatenate([p[:, late] for p in h], axis=0)
+    hidden = right_inner(jnp.concatenate([p[:, :width] for p in h], axis=0), rows).astype(bf16)
+    gates = jnp.concatenate([update, hidden], axis=1)
+    gates_ref[...] = gates
+    smooth = times_t(grad_reset_ref[...], second, 0, span) + times_t(
+        gates, first, span, span + 2 * size
+    )
+    norm = times_t(grad_value_ref[...], first, 0, span)
+    kept_ref[:, :width] = smooth[: 2 * steps]
+    kept_ref[:, width:] = norm[: 2 * steps]
+    for k, out in enumerate(sent):
+        part = (smooth, norm)[k // 2][2 * steps :]
+        at = (k % 2) * out.shape[1]
+        out[...] = part[:, at : at + out.shape[1]].astype(bf16)
 
 
 def score_grad_kernel(
@@ -820,14 +849,17 @@
     w_first = gather.weights[0]
     blocks = len(w_first)
 
-    value_pre, value, gates, gates_sent, probs_low, attended, shared_pre, query, key, probs = call(
+    (
+        value_pre, value, gates, gates_core, gates_near, probs_low, attended, shared_pre, query, key, probs
+    ) = call(
         attention_kernel,
         "attention_forward",
         [
             ((tokens, span), f32),
             ((tokens, span), bf16),
-            ((2 * steps, half), f32),
-            ((2 * steps, half), f32),
+            ((steps, half), f32),
+            ((steps, half), f32),
+            ((2 * steps, half), bf16),
             ((tokens, SPAN), bf16),
             ((tokens, span), f32),
             ((steps, LANES), f32),
@@ -847,12 +879,11 @@
         ],
         1,
     )
-    gates_core = swap(gates_sent)
-    attended, gates, gates_core, near_seed = gather.advance((attended, gates, gates_core, near_seed))
+    attended, gates_near, gates_core, near_seed = gather.advance(
+        (attended, gates_near, gates_core, near_seed)
+    )
     seeds = [seed_low, near_seed, swap(seed_low), swap(near_seed)]
-    gates_near = grid.near_swap(
-        jnp.concatenate([gates[steps:], gates_core[steps:]], axis=1).astype(bf16)
-    )
+    gates_near = grid.near_swap(gates_near)
     w_second = gather.weights[1]
     reset_pre, mixed, mix_kept, mix_sent = call(
         mix_kernel,
@@ -865,7 +896,8 @@
         ],
         [*pieces, line_of(cut(forget_gate_offset, near * span, span, 0)), attended, *w_second],
     )
-    mix_kept, mix_came = gather.advance((mix_kept, swap(mix_sent)))
+    mix_kept, mix_sent, gates_near = gather.advance((mix_kept, mix_sent, gates_near))
+    mix_came = swap(mix_sent)
     mix_near = grid.near_swap((mix_kept[steps:] + mix_came[steps:].astype(f32)).astype(bf16))
     hidden_pre, update, blended, hat, post_scale, ffn_low = call(
         hidden_kernel,
@@ -878,8 +910,9 @@
             mix_came,
             mix_near,
             gates,
-            gates_core,
+            swap(gates_core),
             gates_near,
+            swap(gates_near[steps:]),
             line_of(renewal_gate_offset),
             line_of(candidate_offset),
             line_of(later_normalizer_gain),
@@ -925,13 +958,12 @@
     near_part = (back_kept[steps:] + came[steps:].astype(f32)).astype(bf16)
     near_part = grid.near_swap(near_part)
 
-    grad_input, grad_hidden, grad_update, row_sums = call(
+    grad_input, grad_blend, row_sums = call(
         blend_grad_kernel,
         "blend_backward",
         [
             ((steps, width), f32),
-            ((steps, width), bf16),
-            ((steps, width), bf16),
+            ((steps, 2 * width), bf16),
             ((3, width), f32),
         ],
         [
@@ -951,14 +983,15 @@
         1,
     )
     (m_a, m_b) = moving
-    m_a.value, m_b.parts, grad_hidden, grad_update = tie(
-        (m_a.value, m_b.parts, grad_hidden, grad_update)
-    )
+    m_a.value, m_b.parts, grad_blend = tie((m_a.value, m_b.parts, grad_blend))
     m_a.along()
     m_b.across()
-    hidden_pieces = group(grad_hidden)
-    update_pieces = group(grad_update)
+    hidden_pieces = group(grad_blend)
     down = gathered(down_kept, down_sent)
+
+    held = (m_a.value, m_b.value, hidden_pieces)
+    m_a.value, m_b.value, hidden_pieces = tie(held)
+    m_b.along()
 
     grad_reset, grad_value, probs_kept, probs_sent, span_sums = call(
         attention_grad_kernel,
@@ -981,20 +1014,21 @@
     )
     moving.append(Moving(grid, parts))
     m_c = moving[2]
-    m_a.value, m_b.value, m_c.parts, grad_reset, grad_value = tie(
-        (m_a.value, m_b.value, m_c.parts, grad_reset, grad_value)
-    )
-    m_b.along()
     m_c.across()
     probs_gathered = gathered(probs_kept, probs_sent, f32)
-    grad_gates, in_kept, in_sent = call(
+    grad_gates, in_kept, *in_sent = call(
         functools.partial(input_grad_kernel, blocks),
         "input_backward",
-        [((tokens, half), bf16), ((2 * steps, 2 * width), f32), ((2 * steps, 2 * width), bf16)],
-        [place, *hidden_pieces, *update_pieces, grad_reset, grad_value, spread, *w_first, *w_second],
+        [((tokens, half), bf16), ((2 * steps, 2 * width), f32)]
+        + [((2 * steps, half), bf16)] * 4,
+        [place, *hidden_pieces, grad_reset, grad_value, spread, *w_first, *w_second],
         1,
     )
-    in_gathered = gathered(in_kept, in_sent)
+    m_b.value, in_kept, in_sent, down = tie((m_b.value, in_kept, in_sent, down))
+    in_came = [swap(p) for p in in_sent]
+    in_near = in_kept[steps:] + jnp.concatenate([p[steps:] for p in in_came], axis=1).astype(f32)
+    in_near = grid.near_swap(in_near.astype(bf16))
+    in_gathered = [in_kept, *in_came, in_near]
     grad_shared, narrow = call(
         score_grad_kernel,
         "scores_backward",
@@ -1010,7 +1044,8 @@
     )
     moving.append(Moving(grid, parts))
     m_d = moving[3]
-    m_b.value, m_c.value, m_d.parts = tie((m_b.value, m_c.value, m_d.parts))
+    held = (m_c.value, m_d.parts, m_a.value, in_gathered)
+    m_c.value, m_d.parts, m_a.value, in_gathered = tie(held)
     m_c.along()
     m_d.across()
     averages = call(
@@ -1019,9 +1054,8 @@
         [
             ((steps, width), bf16),
             ((steps, width), bf16),
-            ((2, width), f32),
-            (params.shape[1:], f32),
-            (params.shape[1:], f32),
+            ((states + 8, width), f32),
+            ((states + 8, width), f32),
         ],
         [
             place,
@@ -1036,6 +1070,9 @@
             *in_gathered,
             grad_shared,
             grad_input,
+            row_sums,
+            seed_sum,
+            narrow,
             *down,
             blended,
             line_of(outward_layer_offset),
@@ -1048,28 +1085,15 @@
             pltpu.VMEM((steps, width // LANES, LANES), f32),
         ],
     )
-    m_c.value, m_d.value, averages = tie((m_c.value, m_d.value, averages))
+    sides = [m_a.near(), m_b.near()]
+    held = (m_c.value, m_d.value, averages, sides)
+    m_c.value, m_d.value, averages, sides = tie(held)
     m_d.along()
-    grad_row, out_row, grad_vectors, grad_zero, grad_first = averages
+    grad_row, out_row, keep_rows, send_rows = averages
 
     lanes = COMMON_SPAN_DIM
-    narrow = jnp.pad(narrow.reshape(1, -1), ((0, 0), (0, width - 4 * lanes)))
-    shared_sums = jnp.concatenate(
-        [
-            grad_zero.reshape(states, width),
-            grad_first.reshape(states, width),
-            grad_vectors,
-            row_sums,
-            seed_sum,
-            narrow,
-            jnp.zeros((1, width), f32),
-        ],
-        axis=0,
-    )
-    kept = shared_sums.shape[0] // 2
-    keep_rows = cut(shared_sums, core * kept, kept, 0) + swap(
-        cut(shared_sums, (1 - core) * kept, kept, 0)
-    )
+    keep_rows = keep_rows + swap(send_rows)
+    kept = keep_rows.shape[0]
 
     def placed(value):
         return near_order(value, jnp.zeros_like(value), 0).reshape(-1, width)
@@ -1082,10 +1106,10 @@
     small = jnp.concatenate([keep_rows] + wide_sums, axis=0)
     sums = grid.sum_all(small)
     first_rows = sums[:kept]
-    whole = in_order(first_rows, swap(first_rows), 0)
+    whole = in_order(first_rows, swap(sums)[:kept], 0)
     wide = sums[kept:]
     zero = whole[:states].T
-    first = whole[states : 2 * states].T
+    first = whole[kept : kept + states].T
     rate = jax.nn.sigmoid(inflow_logits)
     damp = jax.nn.sigmoid(decay_logits)
     grad_collapse = rate * channel_lifting * zero
@@ -1094,10 +1118,12 @@
     grad_lifting = grad_inflow * rate
     grad_rate = (grad_inflow * channel_lifting - grad_keep * damp) * rate * (1.0 - rate)
     grad_damp = -grad_keep * rate * damp * (1.0 - damp)
-    rest = whole[2 * states :]
+    rest = whole[states:]
     thin = rest[6].reshape(-1, lanes)
 
-    (own_a, near_a), (own_b, near_b), (own_c, near_c), (own_d, near_d) = [m.near() for m in moving]
+    (own_a, near_a), (own_b, near_b) = sides
+    own_c, near_c = m_c.near()
+    own_d, near_value, near_d = m_d.near((span,))
     out_in = near_order(
         jnp.concatenate([own_a[:, :ff], own_b[:, :ff]], axis=1),
         jnp.concatenate([near_a[:, :ff], near_b[:, :ff]], axis=1),
@@ -1110,20 +1136,14 @@
     )
     out_reset = near_order(own_c[:, :span], near_c[:, :span], 1)
     out_wout = near_order(own_c[:, span:], near_c[:, span:], 1)
-    out_value = near_order(own_d[:, :span], near_d[:, :span], 1)
-    own_d, near_d = own_d[:, span:], near_d[:, span:]
-    gates_half = jnp.concatenate(
-        [
-            near_order(own_d[:, :quarter], near_d[:, :quarter], 1),
-            near_order(own_d[:, quarter:half], near_d[:, quarter:half], 1),
-            own_d[:, half:] + near_d[:, half:],
-        ],
-        axis=1,
-    )
-    gates_other = swap(gates_half)
-    out_update = in_order(gates_half[:, :half], gates_other[:, :half], 1)
-    out_hidden = in_order(gates_half[:, half : 2 * half], gates_other[:, half : 2 * half], 1)
-    out_shared = gates_half[:, 2 * half :] + gates_other[:, 2 * half :]
+    out_value = near_order(own_d[:, :span], near_value, 1)
+    own_d = own_d[:, span:]
+    update_half = near_order(own_d[:, :quarter], near_d[:, :quarter], 1)
+    hidden_half = near_order(own_d[:, quarter:half], near_d[:, quarter:half], 1)
+    shared_half = own_d[:, half:] + near_d[:, half:]
+    out_update = in_order(update_half, swap(update_half), 1)
+    out_hidden = in_order(hidden_half, swap(hidden_half), 1)
+    out_shared = shared_half + swap(shared_half)
 
     rows_out = jnp.stack([out_row, grad_row])
     rows_other = swap(rows_out)

time: 408 us -> 362 us (0.89); the launches traced: 400 us -> 361 us
  waiting for transfers between devices: 113 us -> 98.3 us
  Pallas kernels: 107 us -> 96.7 us
  starting transfers between devices: 112 us -> 102 us
  local copies, waits for them, and re-layouts: 32.7 us -> 27.8 us
    ppermute x21, waiting for transfers between devices: 74.2 us -> 39.1 us  [fetch(): lax.ppermute(array, 'dp', self.shift(dim, -k))]
    ppermute x16, waiting for transfers between devices: 22 us -> 46.1 us  [deliver(): lax.ppermute(parts[k], 'dp', self.shift(dim, k))]
    ppermute x20 -> x24, starting transfers between devices: 42 us -> 23.6 us  [swap(): return lax.ppermute(value, 'mp', swap_pairs)]
    ppermute x21, starting transfers between devices: 23.4 us -> 38.7 us  [fetch(): lax.ppermute(array, 'dp', self.shift(dim, -k))]
    pallas_call x15, Pallas kernels: 107 us -> 96.7 us  [call(): pl.pallas_call(kernel, name=name, out_shape=[jax.ShapeDtypeStruct(shape,...]
    ppermute x16, starting transfers between devices: 30.2 us -> 21.8 us  [deliver(): lax.ppermute(parts[k], 'dp', self.shift(dim, k))]
    unnamed x152 -> x142, local copies, waits for them, and re-layouts: 11.4 us -> 8.97 us
  transfers between devices with their start and end apart: 75 -> 79, of which waited for: 22 -> 23; matrix products, arithmetic and copies ran while one was open for 12% -> 14% of each run, Pallas kernels for 27% -> 27%
where the time goes in v3:
time: 362 us; the launch traced here: 361 us
  starting transfers between devices  102 us (28%)
  waiting for transfers between devices  98.3 us (27%)
  Pallas kernels  96.7 us (27%)
  other arithmetic  31.5 us (9%)
  local copies, waits for them, and re-layouts  27.8 us (8%)
  between operations  4.46 us (1%)
    pallas_call x15, Pallas kernels, call(): pl.pallas_call(kernel, name=name, out_shape=[jax.ShapeDtypeStruct(shape,...  96.7 us
    ppermute x16, waiting for transfers between devices, deliver(): lax.ppermute(parts[k], 'dp', self.shift(dim, k))  46.1 us
    ppermute x21, waiting for transfers between devices, fetch(): lax.ppermute(array, 'dp', self.shift(dim, -k))  39.1 us
    ppermute x21, starting transfers between devices, fetch(): lax.ppermute(array, 'dp', self.shift(dim, -k))  38.7 us
    ppermute x24, starting transfers between devices, swap(): return lax.ppermute(value, 'mp', swap_pairs)  23.6 us
    ppermute x16, starting transfers between devices, deliver(): lax.ppermute(parts[k], 'dp', self.shift(dim, k))  21.8 us
    ppermute x18, starting transfers between devices, near_swap(): return lax.ppermute(value, 'dp', self.shift(self.near, 1))  18.4 us
    ppermute x18, waiting for transfers between devices, near_swap(): return lax.ppermute(value, 'dp', self.shift(self.near, 1))  9.6 us
  transfers between devices with their start and end apart: 79, of which 23 were waited for; matrix products, arithmetic and copies ran while one was open for 14% of the time, Pallas kernels for 27%

profile of v3, /device:TPU:1, one launch (start us, length us, event | category | flops | bytes accessed | tf_op | source)
XLA Modules:
  0.0 361.4 jit_solution(3591191831416101226)
XLA Ops:
  4.7 2.0 collective-permute-start.5
  13.4 2.2 fusion.spread_ref.refs_6_
  20.5 2.3 collective-permute-start.2
  28.4 10.5 %average_forward.1 = (f32[128,1024]{1,0:T(8,128)}, f32[128,1024]{1,0:T(8,128)}, bf16[128,2048]{1,0:T(8,128)(2,1)}, bf16[128,1024]{1,0:T(8,128)(2,1)}, f32[128,8,128]{2,1,0:T(8,128)}, /*index=5*/f32[1,1024]{1,0:T(1,128)}) custom-call(s32[7]{0:T(128)} %stack.131.place_ref, bf16[128,1024]{1,0:T(8,128)(2,1)} %dynamic-slice_bitcast_fusion.5.x_ref, ...), custom_call_target="tpu_custom_call" | custom-call | flops 1 | bytes 1 | tf_op jit(solution)/shard_map/average_forward/pallas_call | solution.py:236
  38.9 3.7 %collective-permute-done.2 = bf16[2,64,1152]{2,1,0:T(8,128)(2,1)S(1)} collective-permute-done((bf16[2,64,1152]{2,1,0:T(8,128)(2,1)S(1)}, bf16[2,64,1152]{2,1,0:T(8,128)(2,1)S(1)}, u32[]{:S(2)}, u32[]{:S(2)}) %collective-permute-start.2) | collective-permute-done | bytes 294944 | tf_op jit(solution)/shard_map/ppermute | solution.py:73
  44.4 6.6 %collective-permute-start.11 = (bf16[2,64,1024]{2,1,0:T(8,128)(2,1)S(1)}, bf16[2,64,1024]{2,1,0:T(8,128)(2,1)S(1)}, u32[]{:S(2)}, u32[]{:S(2)}) collective-permute-start(bf16[2,64,1024]{2,1,0:T(8,128)(2,1)S(1)} %pad_maximum_fusion.9), channel_id=1, source_target_pairs={{0,8},{2,10},{4,12},{6,14},{8,16},{10,18},{12,20},{14,22},{16,24},... | collective-permute-start | bytes 786440 | tf_op jit(solution)/shard_map/ppermute | solution.py:73
  51.0 2.1 collective-permute-start.9
  55.8 12.5 %collective-permute-done.10 = bf16[2,64,1024]{2,1,0:T(8,128)(2,1)S(1)} collective-permute-done((bf16[2,64,1024]{2,1,0:T(8,128)(2,1)S(1)}, bf16[2,64,1024]{2,1,0:T(8,128)(2,1)S(1)}, u32[]{:S(2)}, u32[]{:S(2)}) %collective-permute-start.10) | collective-permute-done | bytes 262176 | tf_op jit(solution)/shard_map/ppermute | solution.py:73
  73.1 6.6 %collective-permute-start.15 = (bf16[2,64,1024]{2,1,0:T(8,128)(2,1)}, bf16[2,64,1024]{2,1,0:T(8,128)(2,1)}, u32[]{:S(2)}, u32[]{:S(2)}) collective-permute-start(bf16[2,64,1024]{2,1,0:T(8,128)(2,1)} %pad_maximum_fusion.10), channel_id=1, source_target_pairs={{0,8},{2,10},{4,12},{6,14},{8,16},{10,18},{12,20},{14,22},{16,24},... | collective-permute-start | bytes 786440 | tf_op jit(solution)/shard_map/ppermute | solution.py:73
  79.7 2.2 collective-permute-start.13
  84.6 6.2 %attention_forward.1 = (f32[512,512]{1,0:T(8,128)}, bf16[512,512]{1,0:T(8,128)(2,1)}, f32[128,512]{1,0:T(8,128)}, f32[128,512]{1,0:T(8,128)}, bf16[256,512]{1,0:...) custom-call(s32[7]{0:T(128)} %stack.131.place_ref, ...), custom_call_target="tpu_custom_call" | custom-call | flops 1 | bytes 1 | tf_op jit(solution)/shard_map/attention_forward/pallas_call | solution.py:236
  90.9 6.6 %collective-permute-done.14 = bf16[2,64,1024]{2,1,0:T(8,128)(2,1)} collective-permute-done((bf16[2,64,1024]{2,1,0:T(8,128)(2,1)}, bf16[2,64,1024]{2,1,0:T(8,128)(2,1)}, u32[]{:S(2)}, u32[]{:S(2)}) %collective-permute-start.14) | collective-permute-done | bytes 262176 | tf_op jit(solution)/shard_map/ppermute | solution.py:73
  99.1 5.9 %collective-permute-start.20 = (bf16[2,64,1024]{2,1,0:T(8,128)(2,1)S(1)}, bf16[2,64,1024]{2,1,0:T(8,128)(2,1)}, u32[]{:S(2)}, u32[]{:S(2)}) collective-permute-start(bf16[2,64,1024]{2,1,0:T(8,128)(2,1)S(1)} %copy-done.34), channel_id=1, source_target_pairs={{0,8},{2,10},{4,12},{6,14},{8,16},{10,18},{12,20},{14,22},{16,24},... | collective-permute-start | bytes 786440 | tf_op jit(solution)/shard_map/ppermute | solution.py:73
  105.0 2.2 collective-permute-start.19
  109.1 5.0 %reset_and_mix.1 = (f32[512,512]{1,0:T(8,128)}, bf16[512,512]{1,0:T(8,128)(2,1)}, f32[256,1024]{1,0:T(8,128)}, bf16[256,1024]{1,0:T(8,128)(2,1)}) custom-call(bf16[128,2048]{1,0:T(8,128)(2,1)} %get-tuple-element.160.p0.refs_0_, bf16[128,2048]{1,0:T(8,128)(2,1)} %copy-done.7, bf16[128,2048]{1,0:T(8,128)(2,1)} %copy-done.8, bf16[128,2048]{1,0:T(8,128)(2,1)} %copy-done.9, ...), custom_call_target="tpu_custom_call" | custom-call | flops 1 | bytes 1 | tf_op jit(solution)/shard_map/reset_and_mix/pallas_call | solution.py:236
  114.1 11.0 %collective-permute-done.19 = bf16[2,64,1024]{2,1,0:T(8,128)(2,1)} collective-permute-done((bf16[2,64,1024]{2,1,0:T(8,128)(2,1)S(1)}, bf16[2,64,1024]{2,1,0:T(8,128)(2,1)}, u32[]{:S(2)}, u32[]{:S(2)}) %collective-permute-start.19) | collective-permute-done | bytes 262176 | tf_op jit(solution)/shard_map/ppermute | solution.py:73
  133.3 3.5 collective-permute-done.24.near_ref
  137.5 4.9 %hidden_and_norm.1 = (f32[128,1024]{1,0:T(8,128)}, f32[128,1024]{1,0:T(8,128)}, f32[128,1024]{1,0:T(8,128)}, f32[128,1024]{1,0:T(8,128)}, f32[128,1]{1,0:T(8,128)}, /*index=5*/bf16[128,1024]{1,0:T(8,128)(2,1)}) custom-call(s32[7]{0:T(128)} %stack.131.place_ref, bf16[128,1024]{1,0:T(8,128)(2,1)} %dynamic-slice_bitcast_fusion.5.x_ref, ...), custom_call_target="tpu_custom_call" | custom-call | flops 1 | bytes 1 | tf_op jit(solution)/shard_map/hidden_and_norm/pallas_call | solution.py:236
  145.8 3.6 %collective-permute-done.27.refs_1_ = bf16[128,1024]{1,0:T(8,128)(2,1)S(1)} collective-permute-done((bf16[128,1024]{1,0:T(8,128)(2,1)}, bf16[128,1024]{1,0:T(8,128)(2,1)S(1)}, u32[]{:S(2)}, u32[]{:S(2)}) %collective-permute-start.27) | collective-permute-done | bytes 262176 | tf_op jit(solution)/shard_map/ppermute | solution.py:85
  149.4 2.0 collective-permute-start.29
  153.3 6.2 %feed_forward.2 = (bf16[512,512]{1,0:T(8,128)(2,1)}, bf16[512,512]{1,0:T(8,128)(2,1)}, f32[1,512]{1,0:T(1,128)}, f32[512,1024]{1,0:T(8,128)}, f32[512,1024]{1,0:T(8,128)}) custom-call(bf16[128,1024]{1,0:T(8,128)(2,1)} %get-tuple-element.185.refs_0_, bf16[128,1024]{1,0:T(8,128)(2,1)} %copy-done.17, bf16[128,1024]{1,0:T(8,128)(2,1)} %copy-done.20, ...), custom_call_target="tpu_custom_call" | custom-call | flops 1 | bytes 1 | tf_op jit(solution)/shard_map/feed_forward/pallas_call | solution.py:236
  159.5 4.2 %feed_forward_weights.2 = (bf16[512,1024]{1,0:T(8,128)(2,1)}, bf16[512,1024]{1,0:T(8,128)(2,1)}) custom-call(bf16[128,1024]{1,0:T(8,128)(2,1)} %get-tuple-element.185.refs_0_, bf16[128,1024]{1,0:T(8,128)(2,1)} %copy-done.17, bf16[128,1024]{1,0:T(8,128)(2,1)} %copy-done.20, bf16[128,1024]{1,0:T(8,128)(2,1)} %copy-done.21, ...), custom_call_target="tpu_custom_call" | custom-call | flops 1 | bytes 1 | tf_op jit(solution)/shard_map/feed_forward_weights/pallas_call | solution.py:236
  165.1 7.1 %feed_forward.3 = (bf16[512,512]{1,0:T(8,128)(2,1)}, bf16[512,512]{1,0:T(8,128)(2,1)}, f32[1,512]{1,0:T(1,128)}, f32[256,1024]{1,0:T(8,128)}, bf16[256,1024]{1,0...) custom-call(bf16[128,1024]{1,0:T(8,128)(2,1)} %get-tuple-element.185.refs_0_, ...), custom_call_target="tpu_custom_call" | custom-call | flops 1 | bytes 1 | tf_op jit(solution)/shard_map/feed_forward/pallas_call | solution.py:236
  177.2 4.2 %feed_forward_weights.3 = (bf16[512,1024]{1,0:T(8,128)(2,1)}, bf16[512,1024]{1,0:T(8,128)(2,1)}) custom-call(bf16[128,1024]{1,0:T(8,128)(2,1)} %get-tuple-element.185.refs_0_, bf16[128,1024]{1,0:T(8,128)(2,1)} %copy-done.17, bf16[128,1024]{1,0:T(8,128)(2,1)} %copy-done.20, bf16[128,1024]{1,0:T(8,128)(2,1)} %copy-done.21, ...), custom_call_target="tpu_custom_call" | custom-call | flops 1 | bytes 1 | tf_op jit(solution)/shard_map/feed_forward_weights/pallas_call | solution.py:236
  181.4 2.2 collective-permute-done.35.near_ref
  184.3 5.3 %blend_backward.1 = (f32[128,1024]{1,0:T(8,128)}, bf16[128,2048]{1,0:T(8,128)(2,1)}, f32[3,1024]{1,0:T(4,128)}) custom-call(s32[7]{0:T(128)} %stack.131.place_ref, bf16[128,1024]{1,0:T(8,128)(2,1)} %dynamic-slice_bitcast_fusion.5.x_ref, bf16[128,1024]{1,0:T(8,128)(2,1)} %dynamic-slice_bitcast_fusion.4.seed_ref, f32[256,1024]{1,0:T(8,128)} %get-tuple-element.200.kept_ref, ...), custom_call_target="tpu_custom_call" | custom-call | flops 1 | bytes 1 | tf_op jit(solution)/shard_map/blend_backward/pallas_call | solution.py:236
  193.7 5.8 %collective-permute-start.36 = (bf16[2,64,1024]{2,1,0:T(8,128)(2,1)S(1)}, bf16[2,64,1024]{2,1,0:T(8,128)(2,1)S(1)}, u32[]{:S(2)}, u32[]{:S(2)}) collective-permute-start(bf16[2,64,1024]{2,1,0:T(8,128)(2,1)S(1)} %get-tuple-element.296), channel_id=1, source_target_pairs={{0,8},{2,10},{4,12},{6,14},{8,16},{10,18},{12,20},{14,22},{16,24},... | collective-permute-start | bytes 786440 | tf_op jit(solution)/shard_map/ppermute | solution.py:78
  200.6 3.7 %collective-permute-done.36 = bf16[2,64,1024]{2,1,0:T(8,128)(2,1)S(1)} collective-permute-done((bf16[2,64,1024]{2,1,0:T(8,128)(2,1)S(1)}, bf16[2,64,1024]{2,1,0:T(8,128)(2,1)S(1)}, u32[]{:S(2)}, u32[]{:S(2)}) %collective-permute-start.36) | collective-permute-done | bytes 262176 | tf_op jit(solution)/shard_map/ppermute | solution.py:78
  204.4 4.0 %collective-permute-start.49 = (bf16[256,1024]{1,0:T(8,128)(2,1)}, bf16[256,1024]{1,0:T(8,128)(2,1)S(1)}, u32[]{:S(2)}, u32[]{:S(2)}) collective-permute-start(bf16[256,1024]{1,0:T(8,128)(2,1)} %get-tuple-element.242), channel_id=1, source_target_pairs={{0,1},{1,0},{2,3},{3,2},{4,5},{5,4},{6,7},{7,6},{8,9},{9,8},{10,11... | collective-permute-start | bytes 1572872 | tf_op jit(solution)/shard_map/ppermute | solution.py:765
  208.4 3.4 collective-permute-done.38
  213.8 9.2 %collective-permute-done.37 = bf16[2,64,1024]{2,1,0:T(8,128)(2,1)} collective-permute-done((bf16[2,64,1024]{2,1,0:T(8,128)(2,1)}, bf16[2,64,1024]{2,1,0:T(8,128)(2,1)}, u32[]{:S(2)}, u32[]{:S(2)}) %collective-permute-start.37) | collective-permute-done | bytes 262176 | tf_op jit(solution)/shard_map/ppermute | solution.py:78
  225.0 2.0 add_convert_fusion.1
  228.0 3.3 collective-permute-start.48
  232.5 5.6 %attention_backward.1 = (bf16[512,512]{1,0:T(8,128)(2,1)}, bf16[512,512]{1,0:T(8,128)(2,1)}, f32[256,128]{1,0:T(8,128)}, f32[256,128]{1,0:T(8,128)}, f32[2,512]{1,0:T(2,128)}) custom-call(bf16[128,2048]{1,0:T(8,128)(2,1)} %get-tuple-element.211.h0.refs_4_.refs_0_, bf16[128,2048]{1,0:T(8,128)(2,1)} %copy-done.12, bf16[128,2048]{1,0:T(8,128)(2,1)} %copy-done.13, ...), custom_call_target="tpu_custom_call" | custom-call | flops 1 | bytes 1 | tf_op jit(solution)/shard_map/attention_backward/pallas_call | solution.py:236
  239.4 7.3 %input_backward.1 = (bf16[512,512]{1,0:T(8,128)(2,1)}, f32[256,2048]{1,0:T(8,128)}, bf16[256,512]{1,0:T(8,128)(2,1)}, bf16[256,512]{1,0:T(8,128)(2,1)}, bf16[256...) custom-call(s32[7]{0:T(128)} %stack.131.place_ref, bf16[128,2048]{1,0:T(8,128)(2,1)} %get-tuple-element.211.h0.refs_4_.refs_0_, ...), custom_call_target="tpu_custom_call" | custom-call | flops 1 | bytes 1 | tf_op jit(solution)/shard_map/input_backward/pallas_call | solution.py:236
  246.7 4.8 %reset_weights.1 = (bf16[512,1024]{1,0:T(8,128)(2,1)}, bf16[512,1024]{1,0:T(8,128)(2,1)}) custom-call(bf16[128,2048]{1,0:T(8,128)(2,1)} %get-tuple-element.160.p0.refs_0_, bf16[128,2048]{1,0:T(8,128)(2,1)} %copy-done.7, bf16[128,2048]{1,0:T(8,128)(2,1)} %copy-done.8, bf16[128,2048]{1,0:T(8,128)(2,1)} %copy-done.9, ...), custom_call_target="tpu_custom_call" | custom-call | flops 1 | bytes 1 | tf_op jit(solution)/shard_map/reset_weights/pallas_call | solution.py:236
  252.8 2.1 fusion.8
  263.7 4.6 %value_weights.1 = (bf16[512,1152]{1,0:T(8,128)(2,1)}, bf16[512,1152]{1,0:T(8,128)(2,1)}) custom-call(bf16[128,2048]{1,0:T(8,128)(2,1)} %get-tuple-element.160.p0.refs_0_, bf16[128,2048]{1,0:T(8,128)(2,1)} %copy-done.7, bf16[128,2048]{1,0:T(8,128)(2,1)} %copy-done.8, bf16[128,2048]{1,0:T(8,128)(2,1)} %copy-done.9, ...), custom_call_target="tpu_custom_call" | custom-call | flops 1 | bytes 1 | tf_op jit(solution)/shard_map/value_weights/pallas_call | solution.py:236
  268.3 8.4 %collective-permute-done.43 = bf16[4,2,64,1024]{3,2,1,0:T(8,128)(2,1)} collective-permute-done((bf16[4,2,64,1024]{3,2,1,0:T(8,128)(2,1)}, bf16[4,2,64,1024]{3,2,1,0:T(8,128)(2,1)}, u32[]{:S(2)}, u32[]{:S(2)}) %collective-permute-start.43) | collective-permute-done | bytes 1048608 | tf_op jit(solution)/shard_map/ppermute | solution.py:78
  282.9 2.2 collective-permute-start.58
  287.0 18.9 %average_backward.1 = (bf16[128,1024]{1,0:T(8,128)(2,1)}, bf16[128,1024]{1,0:T(8,128)(2,1)}, f32[24,1024]{1,0:T(8,128)}, f32[24,1024]{1,0:T(8,128)}) custom-call(s32[7]{0:T(128)} %stack.131.place_ref, bf16[128,1024]{1,0:T(8,128)(2,1)} %dynamic-slice_bitcast_fusion.5.x_ref, f32[1,1024]{1,0:T(1,128)} %bitcast.235, f32[1,1024]{1,0:T(1,128)} %bitcast.237, ...), custom_call_target="tpu_custom_call" | custom-call | flops 1 | bytes 1 | tf_op jit(solution)/shard_map/average_backward/pallas_call | solution.py:236
  306.9 2.2 collective-permute-done.57
  313.5 3.3 collective-permute-start.72
  320.1 2.9 collective-permute-done.64
  323.7 4.8 %collective-permute-done.72 = bf16[2,64,1152]{2,1,0:T(8,128)(2,1)S(1)} collective-permute-done((bf16[2,64,1152]{2,1,0:T(8,128)(2,1)S(1)}, bf16[2,64,1152]{2,1,0:T(8,128)(2,1)S(1)}, u32[]{:S(2)}, u32[]{:S(2)}) %collective-permute-start.72) | collective-permute-done | bytes 294944 | tf_op jit(solution)/shard_map/ppermute | solution.py:78
  328.5 14.1 %collective-permute-done.71 = bf16[2,64,1152]{2,1,0:T(8,128)(2,1)S(1)} collective-permute-done((bf16[2,64,1152]{2,1,0:T(8,128)(2,1)S(1)}, bf16[2,64,1152]{2,1,0:T(8,128)(2,1)S(1)}, u32[]{:S(2)}, u32[]{:S(2)}) %collective-permute-start.71) | collective-permute-done | bytes 294944 | tf_op jit(solution)/shard_map/ppermute | solution.py:78
  344.5 3.3 collective-permute-start.67
  352.3 2.6 collective-permute-start.69
  (374 shorter events, 107.5 us)
Async XLA Ops:
  4.7 21.2 %collective-permute-start.5 = (s32[2]{0:T(128)S(1)}, s32[2]{0:T(128)S(1)}, u32[]{:S(2)}, u32[]{:S(2)}) collective-permute-start(s32[2]{0:T(128)S(1)} %pad_add_fusion), channel_id=1, source_target_pairs={{0,2},{2,0},{4,6},{6,4},{8,10},{10,8},{12,14},{14,12},{16,18},{18,... | collective-permute-start | bytes 32 | tf_op jit(solution)/shard_map/ppermute | solution.py:85
  19.0 19.9 %collective-permute-start.3 = (bf16[2,64,1152]{2,1,0:T(8,128)(2,1)S(1)}, bf16[2,64,1152]{2,1,0:T(8,128)(2,1)S(1)}, u32[]{:S(2)}, u32[]{:S(2)}) collective-permute-start(bf16[2,64,1152]{2,1,0:T(8,128)(2,1)S(1)} %pad_maximum_fusion.8), channel_id=1, source_target_pairs={{0,8},{2,10},{4,12},{6,14},{8,16},{10,18},{12,20},{14,22},{16,24},... | collective-permute-start | bytes 884744 | tf_op jit(solution)/shard_map/ppermute | solution.py:73
  20.5 22.2 %collective-permute-start.2 = (bf16[2,64,1152]{2,1,0:T(8,128)(2,1)S(1)}, bf16[2,64,1152]{2,1,0:T(8,128)(2,1)S(1)}, u32[]{:S(2)}, u32[]{:S(2)}) collective-permute-start(bf16[2,64,1152]{2,1,0:T(8,128)(2,1)S(1)} %pad_maximum_fusion.8), channel_id=1, source_target_pairs={{0,16},{2,18},{4,20},{6,22},{8,24},{10,26},{12,28},{14,30},{16,0},... | collective-permute-start | bytes 884744 | tf_op jit(solution)/shard_map/ppermute | solution.py:73
  22.8 19.9 %collective-permute-start.1 = (bf16[2,64,1152]{2,1,0:T(8,128)(2,1)S(1)}, bf16[2,64,1152]{2,1,0:T(8,128)(2,1)S(1)}, u32[]{:S(2)}, u32[]{:S(2)}) collective-permute-start(bf16[2,64,1152]{2,1,0:T(8,128)(2,1)S(1)} %pad_maximum_fusion.8), channel_id=1, source_target_pairs={{0,24},{2,26},{4,28},{6,30},{8,0},{10,2},{12,4},{14,6},{16,8},{18,... | collective-permute-start | bytes 884744 | tf_op jit(solution)/shard_map/ppermute | solution.py:73
  23.9 19.0 %collective-permute-start.4 = (bf16[64,3072]{1,0:T(8,128)(2,1)}, bf16[64,3072]{1,0:T(8,128)(2,1)S(1)}, u32[]{:S(2)}, u32[]{:S(2)}) collective-permute-start(bf16[64,3072]{1,0:T(8,128)(2,1)} %bitcast_dynamic-update-slice_fusion), channel_id=1, source_target_pairs={{0,2},{2,0},{4,6},{6,4},{8,10},{10,8},{12,14},{14,12},{16,18},{18,... | collective-permute-start | bytes 1179656 | tf_op jit(solution)/shard_map/ppermute | solution.py:85
  43.1 27.0 %collective-permute-start.12 = (bf16[4,2,64,1152]{3,2,1,0:T(8,128)(2,1)S(1)}, bf16[4,2,64,1152]{3,2,1,0:T(8,128)(2,1)S(1)}, u32[]{:S(2)}, u32[]{:S(2)}) collective-permute-start(bf16[4,2,64,1152]{3,2,1,0:T(8,128)(2,1)S(1)} %pad_maximum_fusion), channel_id=1, source_target_pairs={{0,4},{2,6},{4,0},{6,2},{8,12},{10,14},{12,8},{14,10},{16,20},{18,... | collective-permute-start | bytes 3538952 | tf_op jit(solution)/shard_map/ppermute | solution.py:73
  44.4 11.5 %collective-permute-start.11 = (bf16[2,64,1024]{2,1,0:T(8,128)(2,1)S(1)}, bf16[2,64,1024]{2,1,0:T(8,128)(2,1)S(1)}, u32[]{:S(2)}, u32[]{:S(2)}) collective-permute-start(bf16[2,64,1024]{2,1,0:T(8,128)(2,1)S(1)} %pad_maximum_fusion.9), channel_id=1, source_target_pairs={{0,8},{2,10},{4,12},{6,14},{8,16},{10,18},{12,20},{14,22},{16,24},... | collective-permute-start | bytes 786440 | tf_op jit(solution)/shard_map/ppermute | solution.py:73
  51.0 17.4 %collective-permute-start.10 = (bf16[2,64,1024]{2,1,0:T(8,128)(2,1)S(1)}, bf16[2,64,1024]{2,1,0:T(8,128)(2,1)S(1)}, u32[]{:S(2)}, u32[]{:S(2)}) collective-permute-start(bf16[2,64,1024]{2,1,0:T(8,128)(2,1)S(1)} %pad_maximum_fusion.9), channel_id=1, source_target_pairs={{0,16},{2,18},{4,20},{6,22},{8,24},{10,26},{12,28},{14,30},{16,0},... | collective-permute-start | bytes 786440 | tf_op jit(solution)/shard_map/ppermute | solution.py:73
  51.0 17.4 %collective-permute-start.9 = (bf16[2,64,1024]{2,1,0:T(8,128)(2,1)S(1)}, bf16[2,64,1024]{2,1,0:T(8,128)(2,1)S(1)}, u32[]{:S(2)}, u32[]{:S(2)}) collective-permute-start(bf16[2,64,1024]{2,1,0:T(8,128)(2,1)S(1)} %pad_maximum_fusion.9), channel_id=1, source_target_pairs={{0,24},{2,26},{4,28},{6,30},{8,0},{10,2},{12,4},{14,6},{16,8},{18,... | collective-permute-start | bytes 786440 | tf_op jit(solution)/shard_map/ppermute | solution.py:73
  53.1 20.0 %collective-permute-start.6 = (bf16[128,2048]{1,0:T(8,128)(2,1)S(1)}, bf16[128,2048]{1,0:T(8,128)(2,1)S(1)}, u32[]{:S(2)}, u32[]{:S(2)}) collective-permute-start(bf16[128,2048]{1,0:T(8,128)(2,1)S(1)} %copy-done.6), channel_id=1, source_target_pairs={{0,2},{2,0},{4,6},{6,4},{8,10},{10,8},{12,14},{14,12},{16,18},{18,... | collective-permute-start | bytes 1572872 | tf_op jit(solution)/shard_map/ppermute | solution.py:85
  70.1 28.7 %collective-permute-start.16 = (bf16[4,2,64,1024]{3,2,1,0:T(8,128)(2,1)S(1)}, bf16[4,2,64,1024]{3,2,1,0:T(8,128)(2,1)S(1)}, u32[]{:S(2)}, u32[]{:S(2)}) collective-permute-start(bf16[4,2,64,1024]{3,2,1,0:T(8,128)(2,1)S(1)} %pad_maximum_fusion.1), channel_id=1, source_target_pairs={{0,4},{2,6},{4,0},{6,2},{8,12},{10,14},{12,8},{14,10},{16,20},{18,... | collective-permute-start | bytes 3145736 | tf_op jit(solution)/shard_map/ppermute | solution.py:73
  73.0 8.9 %collective-permute-start.8 = (bf16[128,2048]{1,0:T(8,128)(2,1)S(1)}, bf16[128,2048]{1,0:T(8,128)(2,1)S(1)}, u32[]{:S(2)}, u32[]{:S(2)}) collective-permute-start(bf16[128,2048]{1,0:T(8,128)(2,1)S(1)} %collective-permute-done.6.p1.refs_1_), channel_id=1, source_target_pairs={{0,1},{1,0},{2,3},{3,2},{4,5},{5,4},{6,7},{7,6},{8,9},{9,8},{10,11... | collective-permute-start | bytes 1572872 | tf_op jit(solution)/shard_map/ppermute | solution.py:765
  73.1 17.7 %collective-permute-start.15 = (bf16[2,64,1024]{2,1,0:T(8,128)(2,1)}, bf16[2,64,1024]{2,1,0:T(8,128)(2,1)}, u32[]{:S(2)}, u32[]{:S(2)}) collective-permute-start(bf16[2,64,1024]{2,1,0:T(8,128)(2,1)} %pad_maximum_fusion.10), channel_id=1, source_target_pairs={{0,8},{2,10},{4,12},{6,14},{8,16},{10,18},{12,20},{14,22},{16,24},... | collective-permute-start | bytes 786440 | tf_op jit(solution)/shard_map/ppermute | solution.py:73
  79.7 17.7 %collective-permute-start.14 = (bf16[2,64,1024]{2,1,0:T(8,128)(2,1)}, bf16[2,64,1024]{2,1,0:T(8,128)(2,1)}, u32[]{:S(2)}, u32[]{:S(2)}) collective-permute-start(bf16[2,64,1024]{2,1,0:T(8,128)(2,1)} %pad_maximum_fusion.10), channel_id=1, source_target_pairs={{0,16},{2,18},{4,20},{6,22},{8,24},{10,26},{12,28},{14,30},{16,0},... | collective-permute-start | bytes 786440 | tf_op jit(solution)/shard_map/ppermute | solution.py:73
  79.7 17.7 %collective-permute-start.13 = (bf16[2,64,1024]{2,1,0:T(8,128)(2,1)}, bf16[2,64,1024]{2,1,0:T(8,128)(2,1)}, u32[]{:S(2)}, u32[]{:S(2)}) collective-permute-start(bf16[2,64,1024]{2,1,0:T(8,128)(2,1)} %pad_maximum_fusion.10), channel_id=1, source_target_pairs={{0,24},{2,26},{4,28},{6,30},{8,0},{10,2},{12,4},{14,6},{16,8},{18,... | collective-permute-start | bytes 786440 | tf_op jit(solution)/shard_map/ppermute | solution.py:73
  81.9 16.8 %collective-permute-start.17 = (bf16[128,1024]{1,0:T(8,128)(2,1)}, bf16[128,1024]{1,0:T(8,128)(2,1)}, u32[]{:S(2)}, u32[]{:S(2)}) collective-permute-start(bf16[128,1024]{1,0:T(8,128)(2,1)} %get-tuple-element.171.refs_4_), channel_id=1, source_target_pairs={{0,2},{2,0},{4,6},{6,4},{8,10},{10,8},{12,14},{14,12},{16,18},{18,... | collective-permute-start | bytes 786440 | tf_op jit(solution)/shard_map/ppermute | solution.py:85
  98.8 27.5 %collective-permute-start.21 = (bf16[4,2,64,1024]{3,2,1,0:T(8,128)(2,1)S(1)}, bf16[4,2,64,1024]{3,2,1,0:T(8,128)(2,1)}, u32[]{:S(2)}, u32[]{:S(2)}) collective-permute-start(bf16[4,2,64,1024]{3,2,1,0:T(8,128)(2,1)S(1)} %pad_maximum_fusion.2), channel_id=1, source_target_pairs={{0,4},{2,6},{4,0},{6,2},{8,12},{10,14},{12,8},{14,10},{16,20},{18,... | collective-permute-start | bytes 3145736 | tf_op jit(solution)/shard_map/ppermute | solution.py:73
  99.1 15.0 %collective-permute-start.20 = (bf16[2,64,1024]{2,1,0:T(8,128)(2,1)S(1)}, bf16[2,64,1024]{2,1,0:T(8,128)(2,1)}, u32[]{:S(2)}, u32[]{:S(2)}) collective-permute-start(bf16[2,64,1024]{2,1,0:T(8,128)(2,1)S(1)} %copy-done.34), channel_id=1, source_target_pairs={{0,8},{2,10},{4,12},{6,14},{8,16},{10,18},{12,20},{14,22},{16,24},... | collective-permute-start | bytes 786440 | tf_op jit(solution)/shard_map/ppermute | solution.py:73
  105.0 20.1 %collective-permute-start.19 = (bf16[2,64,1024]{2,1,0:T(8,128)(2,1)S(1)}, bf16[2,64,1024]{2,1,0:T(8,128)(2,1)}, u32[]{:S(2)}, u32[]{:S(2)}) collective-permute-start(bf16[2,64,1024]{2,1,0:T(8,128)(2,1)S(1)} %copy-done.34), channel_id=1, source_target_pairs={{0,16},{2,18},{4,20},{6,22},{8,24},{10,26},{12,28},{14,30},{16,0},... | collective-permute-start | bytes 786440 | tf_op jit(solution)/shard_map/ppermute | solution.py:73
  107.2 17.9 %collective-permute-start.18 = (bf16[2,64,1024]{2,1,0:T(8,128)(2,1)S(1)}, bf16[2,64,1024]{2,1,0:T(8,128)(2,1)}, u32[]{:S(2)}, u32[]{:S(2)}) collective-permute-start(bf16[2,64,1024]{2,1,0:T(8,128)(2,1)S(1)} %copy-done.34), channel_id=1, source_target_pairs={{0,24},{2,26},{4,28},{6,30},{8,0},{10,2},{12,4},{14,6},{16,8},{18,... | collective-permute-start | bytes 786440 | tf_op jit(solution)/shard_map/ppermute | solution.py:73
  107.2 19.1 %collective-permute-start.22 = (bf16[256,512]{1,0:T(8,128)(2,1)}, bf16[256,512]{1,0:T(8,128)(2,1)}, u32[]{:S(2)}, u32[]{:S(2)}) collective-permute-start(bf16[256,512]{1,0:T(8,128)(2,1)} %get-tuple-element.179), channel_id=1, source_target_pairs={{0,2},{2,0},{4,6},{6,4},{8,10},{10,8},{12,14},{14,12},{16,18},{18,... | collective-permute-start | bytes 786440 | tf_op jit(solution)/shard_map/ppermute | solution.py:85
  127.1 38.0 %collective-permute-start.33 = (bf16[4,2,64,1024]{3,2,1,0:T(8,128)(2,1)S(1)}, bf16[4,2,64,1024]{3,2,1,0:T(8,128)(2,1)}, u32[]{:S(2)}, u32[]{:S(2)}) collective-permute-start(bf16[4,2,64,1024]{3,2,1,0:T(8,128)(2,1)S(1)} %pad_maximum_fusion.3), channel_id=1, source_target_pairs={{0,4},{2,6},{4,0},{6,2},{8,12},{10,14},{12,8},{14,10},{16,20},{18,... | collective-permute-start | bytes 3145736 | tf_op jit(solution)/shard_map/ppermute | solution.py:73
  163.7 25.9 %collective-permute-start.32 = (bf16[4,2,64,1024]{3,2,1,0:T(8,128)(2,1)}, bf16[4,2,64,1024]{3,2,1,0:T(8,128)(2,1)}, u32[]{:S(2)}, u32[]{:S(2)}) collective-permute-start(bf16[4,2,64,1024]{3,2,1,0:T(8,128)(2,1)} %bitcast.268), channel_id=1, source_target_pairs={{0,4},{2,6},{4,0},{6,2},{8,12},{10,14},{12,8},{14,10},{16,20},{18,... | collective-permute-start | bytes 3145736 | tf_op jit(solution)/shard_map/ppermute | solution.py:78
  191.3 33.7 %collective-permute-start.39 = (bf16[4,2,64,1024]{3,2,1,0:T(8,128)(2,1)}, bf16[4,2,64,1024]{3,2,1,0:T(8,128)(2,1)}, u32[]{:S(2)}, u32[]{:S(2)}) collective-permute-start(bf16[4,2,64,1024]{3,2,1,0:T(8,128)(2,1)} %bitcast.62), channel_id=1, source_target_pairs={{0,4},{2,6},{4,0},{6,2},{8,12},{10,14},{12,8},{14,10},{16,20},{18,... | collective-permute-start | bytes 3145736 | tf_op jit(solution)/shard_map/ppermute | solution.py:78
  191.5 22.2 %collective-permute-start.40 = (bf16[128,2048]{1,0:T(8,128)(2,1)S(1)}, bf16[128,2048]{1,0:T(8,128)(2,1)S(1)}, u32[]{:S(2)}, u32[]{:S(2)}) collective-permute-start(bf16[128,2048]{1,0:T(8,128)(2,1)S(1)} %copy-done.11), channel_id=1, source_target_pairs={{0,2},{2,0},{4,6},{6,4},{8,10},{10,8},{12,14},{14,12},{16,18},{18,... | collective-permute-start | bytes 1572872 | tf_op jit(solution)/shard_map/ppermute | solution.py:85
  193.7 10.7 %collective-permute-start.36 = (bf16[2,64,1024]{2,1,0:T(8,128)(2,1)S(1)}, bf16[2,64,1024]{2,1,0:T(8,128)(2,1)S(1)}, u32[]{:S(2)}, u32[]{:S(2)}) collective-permute-start(bf16[2,64,1024]{2,1,0:T(8,128)(2,1)S(1)} %get-tuple-element.296), channel_id=1, source_target_pairs={{0,8},{2,10},{4,12},{6,14},{8,16},{10,18},{12,20},{14,22},{16,24},... | collective-permute-start | bytes 786440 | tf_op jit(solution)/shard_map/ppermute | solution.py:78
  199.5 12.3 %collective-permute-start.38 = (bf16[2,64,1024]{2,1,0:T(8,128)(2,1)S(1)}, bf16[2,64,1024]{2,1,0:T(8,128)(2,1)}, u32[]{:S(2)}, u32[]{:S(2)}) collective-permute-start(bf16[2,64,1024]{2,1,0:T(8,128)(2,1)S(1)} %get-tuple-element.297), channel_id=1, source_target_pairs={{0,24},{2,26},{4,28},{6,30},{8,0},{10,2},{12,4},{14,6},{16,8},{18,... | collective-permute-start | bytes 786440 | tf_op jit(solution)/shard_map/ppermute | solution.py:78
  199.5 23.5 %collective-permute-start.37 = (bf16[2,64,1024]{2,1,0:T(8,128)(2,1)}, bf16[2,64,1024]{2,1,0:T(8,128)(2,1)}, u32[]{:S(2)}, u32[]{:S(2)}) collective-permute-start(bf16[2,64,1024]{2,1,0:T(8,128)(2,1)} %get-tuple-element.298), channel_id=1, source_target_pairs={{0,16},{2,18},{4,20},{6,22},{8,24},{10,26},{12,28},{14,30},{16,0},... | collective-permute-start | bytes 786440 | tf_op jit(solution)/shard_map/ppermute | solution.py:78
  204.4 27.0 %collective-permute-start.49 = (bf16[256,1024]{1,0:T(8,128)(2,1)}, bf16[256,1024]{1,0:T(8,128)(2,1)S(1)}, u32[]{:S(2)}, u32[]{:S(2)}) collective-permute-start(bf16[256,1024]{1,0:T(8,128)(2,1)} %get-tuple-element.242), channel_id=1, source_target_pairs={{0,1},{1,0},{2,3},{3,2},{4,5},{5,4},{6,7},{7,6},{8,9},{9,8},{10,11... | collective-permute-start | bytes 1572872 | tf_op jit(solution)/shard_map/ppermute | solution.py:765
  211.8 15.3 %collective-permute-start.41 = (bf16[128,2048]{1,0:T(8,128)(2,1)S(1)}, bf16[128,2048]{1,0:T(8,128)(2,1)S(1)}, u32[]{:S(2)}, u32[]{:S(2)}) collective-permute-start(bf16[128,2048]{1,0:T(8,128)(2,1)S(1)} %copy-done.11), channel_id=1, source_target_pairs={{0,1},{1,0},{2,3},{3,2},{4,5},{5,4},{6,7},{7,6},{8,9},{9,8},{10,11... | collective-permute-start | bytes 1572872 | tf_op jit(solution)/shard_map/ppermute | solution.py:765
  213.7 13.4 %collective-permute-start.42 = (bf16[128,2048]{1,0:T(8,128)(2,1)S(1)}, bf16[128,2048]{1,0:T(8,128)(2,1)S(1)}, u32[]{:S(2)}, u32[]{:S(2)}) collective-permute-start(bf16[128,2048]{1,0:T(8,128)(2,1)S(1)} %collective-permute-done.40.h1.refs_5_.refs_1_), channel_id=1, source_target_pairs={{0,1},{1,0},{2,3},{3,2},{4,5},{5,4},{6,7},{7,6},{8,9},{9,8},{10,11... | collective-permute-start | bytes 1572872 | tf_op jit(solution)/shard_map/ppermute | solution.py:765
  228.0 23.5 %collective-permute-start.46 = (bf16[2,64,1024]{2,1,0:T(8,128)(2,1)}, bf16[2,64,1024]{2,1,0:T(8,128)(2,1)}, u32[]{:S(2)}, u32[]{:S(2)}) collective-permute-start(bf16[2,64,1024]{2,1,0:T(8,128)(2,1)} %get-tuple-element.293), channel_id=1, source_target_pairs={{0,8},{2,10},{4,12},{6,14},{8,16},{10,18},{12,20},{14,22},{16,24},... | collective-permute-start | bytes 786440 | tf_op jit(solution)/shard_map/ppermute | solution.py:78
  228.0 24.7 %collective-permute-start.48 = (bf16[2,64,1024]{2,1,0:T(8,128)(2,1)}, bf16[2,64,1024]{2,1,0:T(8,128)(2,1)}, u32[]{:S(2)}, u32[]{:S(2)}) collective-permute-start(bf16[2,64,1024]{2,1,0:T(8,128)(2,1)} %get-tuple-element.294), channel_id=1, source_target_pairs={{0,24},{2,26},{4,28},{6,30},{8,0},{10,2},{12,4},{14,6},{16,8},{18,... | collective-permute-start | bytes 786440 | tf_op jit(solution)/shard_map/ppermute | solution.py:78
  231.3 21.5 %collective-permute-start.47 = (bf16[2,64,1024]{2,1,0:T(8,128)(2,1)}, bf16[2,64,1024]{2,1,0:T(8,128)(2,1)}, u32[]{:S(2)}, u32[]{:S(2)}) collective-permute-start(bf16[2,64,1024]{2,1,0:T(8,128)(2,1)} %get-tuple-element.295), channel_id=1, source_target_pairs={{0,16},{2,18},{4,20},{6,22},{8,24},{10,26},{12,28},{14,30},{16,0},... | collective-permute-start | bytes 786440 | tf_op jit(solution)/shard_map/ppermute | solution.py:78
  232.2 22.6 %collective-permute-start.50 = (bf16[128,1024]{1,0:T(8,128)(2,1)}, bf16[128,1024]{1,0:T(8,128)(2,1)S(1)}, u32[]{:S(2)}, u32[]{:S(2)}) collective-permute-start(bf16[128,1024]{1,0:T(8,128)(2,1)} %add_convert_fusion.3), channel_id=1, source_target_pairs={{0,2},{2,0},{4,6},{6,4},{8,10},{10,8},{12,14},{14,12},{16,18},{18,... | collective-permute-start | bytes 786440 | tf_op jit(solution)/shard_map/ppermute | solution.py:85
  238.1 18.6 %collective-permute-start.44 = (f32[256,128]{1,0:T(8,128)}, f32[256,128]{1,0:T(8,128)}, u32[]{:S(2)}, u32[]{:S(2)}) collective-permute-start(f32[256,128]{1,0:T(8,128)} %get-tuple-element.226), channel_id=1, source_target_pairs={{0,1},{1,0},{2,3},{3,2},{4,5},{5,4},{6,7},{7,6},{8,9},{9,8},{10,11... | collective-permute-start | bytes 393224 | tf_op jit(solution)/shard_map/ppermute | solution.py:765
  251.6 25.2 %collective-permute-start.43 = (bf16[4,2,64,1024]{3,2,1,0:T(8,128)(2,1)}, bf16[4,2,64,1024]{3,2,1,0:T(8,128)(2,1)}, u32[]{:S(2)}, u32[]{:S(2)}) collective-permute-start(bf16[4,2,64,1024]{3,2,1,0:T(8,128)(2,1)} %bitcast.267), channel_id=1, source_target_pairs={{0,4},{2,6},{4,0},{6,2},{8,12},{10,14},{12,8},{14,10},{16,20},{18,... | collective-permute-start | bytes 3145736 | tf_op jit(solution)/shard_map/ppermute | solution.py:78
  260.5 17.9 %collective-permute-start.55 = (bf16[128,2048]{1,0:T(8,128)(2,1)}, bf16[128,2048]{1,0:T(8,128)(2,1)}, u32[]{:S(2)}, u32[]{:S(2)}) collective-permute-start(bf16[128,2048]{1,0:T(8,128)(2,1)} %add_convert_fusion.2), channel_id=1, source_target_pairs={{0,2},{2,0},{4,6},{6,4},{8,10},{10,8},{12,14},{14,12},{16,18},{18,... | collective-permute-start | bytes 1572872 | tf_op jit(solution)/shard_map/ppermute | solution.py:85
  278.4 31.9 %collective-permute-start.59 = (bf16[4,2,64,1152]{3,2,1,0:T(8,128)(2,1)}, bf16[4,2,64,1152]{3,2,1,0:T(8,128)(2,1)S(1)}, u32[]{:S(2)}, u32[]{:S(2)}) collective-permute-start(bf16[4,2,64,1152]{3,2,1,0:T(8,128)(2,1)} %bitcast.70), channel_id=1, source_target_pairs={{0,4},{2,6},{4,0},{6,2},{8,12},{10,14},{12,8},{14,10},{16,20},{18,... | collective-permute-start | bytes 3538952 | tf_op jit(solution)/shard_map/ppermute | solution.py:78
  281.9 25.0 %collective-permute-start.56 = (bf16[2,64,1024]{2,1,0:T(8,128)(2,1)}, bf16[2,64,1024]{2,1,0:T(8,128)(2,1)S(1)}, u32[]{:S(2)}, u32[]{:S(2)}) collective-permute-start(bf16[2,64,1024]{2,1,0:T(8,128)(2,1)} %get-tuple-element.290), channel_id=1, source_target_pairs={{0,8},{2,10},{4,12},{6,14},{8,16},{10,18},{12,20},{14,22},{16,24},... | collective-permute-start | bytes 786440 | tf_op jit(solution)/shard_map/ppermute | solution.py:78
  282.9 24.0 %collective-permute-start.58 = (bf16[2,64,1024]{2,1,0:T(8,128)(2,1)}, bf16[2,64,1024]{2,1,0:T(8,128)(2,1)}, u32[]{:S(2)}, u32[]{:S(2)}) collective-permute-start(bf16[2,64,1024]{2,1,0:T(8,128)(2,1)} %get-tuple-element.291), channel_id=1, source_target_pairs={{0,24},{2,26},{4,28},{6,30},{8,0},{10,2},{12,4},{14,6},{16,8},{18,... | collective-permute-start | bytes 786440 | tf_op jit(solution)/shard_map/ppermute | solution.py:78
  285.1 23.9 %collective-permute-start.57 = (bf16[2,64,1024]{2,1,0:T(8,128)(2,1)}, bf16[2,64,1024]{2,1,0:T(8,128)(2,1)}, u32[]{:S(2)}, u32[]{:S(2)}) collective-permute-start(bf16[2,64,1024]{2,1,0:T(8,128)(2,1)} %get-tuple-element.292), channel_id=1, source_target_pairs={{0,16},{2,18},{4,20},{6,22},{8,24},{10,26},{12,28},{14,30},{16,0},... | collective-permute-start | bytes 786440 | tf_op jit(solution)/shard_map/ppermute | solution.py:78
  286.7 19.2 %collective-permute-start.60 = (bf16[64,1024]{1,0:T(8,128)(2,1)}, bf16[64,1024]{1,0:T(8,128)(2,1)}, u32[]{:S(2)}, u32[]{:S(2)}) collective-permute-start(bf16[64,1024]{1,0:T(8,128)(2,1)} %fusion.16), channel_id=1, source_target_pairs={{0,2},{2,0},{4,6},{6,4},{8,10},{10,8},{12,14},{14,12},{16,18},{18,... | collective-permute-start | bytes 393224 | tf_op jit(solution)/shard_map/ppermute | solution.py:85
  313.0 47.3 %collective-permute-start.62 = (bf16[2,128,1024]{2,1,0:T(8,128)(2,1)S(1)}, bf16[2,128,1024]{2,1,0:T(8,128)(2,1)S(1)}, u32[]{:S(2)}, u32[]{:S(2)}) collective-permute-start(bf16[2,128,1024]{2,1,0:T(8,128)(2,1)S(1)} %pad_maximum_fusion.4), channel_id=1, source_target_pairs={{0,1},{1,0},{2,3},{3,2},{4,5},{5,4},{6,7},{7,6},{8,9},{9,8},{10,11... | collective-permute-start | bytes 1572872 | tf_op jit(solution)/shard_map/ppermute | solution.py:765
  313.4 10.3 %collective-permute-start.70 = (bf16[2,64,1152]{2,1,0:T(8,128)(2,1)S(1)}, bf16[2,64,1152]{2,1,0:T(8,128)(2,1)S(1)}, u32[]{:S(2)}, u32[]{:S(2)}) collective-permute-start(bf16[2,64,1152]{2,1,0:T(8,128)(2,1)S(1)} %get-tuple-element.287), channel_id=1, source_target_pairs={{0,8},{2,10},{4,12},{6,14},{8,16},{10,18},{12,20},{14,22},{16,24},... | collective-permute-start | bytes 884744 | tf_op jit(solution)/shard_map/ppermute | solution.py:78
  313.5 15.0 %collective-permute-start.72 = (bf16[2,64,1152]{2,1,0:T(8,128)(2,1)S(1)}, bf16[2,64,1152]{2,1,0:T(8,128)(2,1)S(1)}, u32[]{:S(2)}, u32[]{:S(2)}) collective-permute-start(bf16[2,64,1152]{2,1,0:T(8,128)(2,1)S(1)} %get-tuple-element.288), channel_id=1, source_target_pairs={{0,24},{2,26},{4,28},{6,30},{8,0},{10,2},{12,4},{14,6},{16,8},{18,... | collective-permute-start | bytes 884744 | tf_op jit(solution)/shard_map/ppermute | solution.py:78
  318.5 24.1 %collective-permute-start.71 = (bf16[2,64,1152]{2,1,0:T(8,128)(2,1)S(1)}, bf16[2,64,1152]{2,1,0:T(8,128)(2,1)S(1)}, u32[]{:S(2)}, u32[]{:S(2)}) collective-permute-start(bf16[2,64,1152]{2,1,0:T(8,128)(2,1)S(1)} %get-tuple-element.289), channel_id=1, source_target_pairs={{0,16},{2,18},{4,20},{6,22},{8,24},{10,26},{12,28},{14,30},{16,0},... | collective-permute-start | bytes 884744 | tf_op jit(solution)/shard_map/ppermute | solution.py:78
  323.0 21.4 %collective-permute-start.65 = (f32[28,1024]{1,0:T(8,128)S(1)}, f32[28,1024]{1,0:T(8,128)S(1)}, u32[]{:S(2)}, u32[]{:S(2)}) collective-permute-start(f32[28,1024]{1,0:T(8,128)S(1)} %fusion.50), channel_id=1, source_target_pairs={{0,4},{2,6},{4,0},{6,2},{8,12},{10,14},{12,8},{14,10},{16,20},{18,... | collective-permute-start | bytes 344072 | tf_op jit(solution)/shard_map/ppermute | solution.py:73
  (100 other events, 765.5 us)

commit v4 on v3

--- a/solution.py
+++ b/solution.py
@@ -129,7 +129,7 @@
 
 
 class Gather:
-    def __init__(self, grid, mine, theirs):
+    def __init__(self, grid, mine, theirs, held):
         self.grid = grid
         near = grid.near_index()
         pack = functools.partial(jnp.concatenate, axis=1)
@@ -141,7 +141,7 @@
 
         first = beside(kept[0], grid.near_swap(sent[0]))
         rest = pack(sent[1:])
-        first, rest = tie((first, rest))
+        first, rest, self.held = tie((first, rest, held))
         rest = grid.near_swap(rest)
         self.state, at = [first], 0
         for own in kept[1:]:
@@ -804,7 +804,9 @@
             for at in hidden
         ]
 
-    gather = Gather(grid, chunks_of(near), chunks_of(1 - near))
+    held = (layer_entries, loss_sensitivity, occupied_counts)
+    gather = Gather(grid, chunks_of(near), chunks_of(1 - near), held)
+    layer_entries, loss_sensitivity, occupied_counts = gather.held
     gather.advance()
 
     row_in = lax.dynamic_index_in_dim(layer_entries, core, 0, keepdims=False)

time: 362 us -> 358 us (0.989)
  starting transfers between devices: 102 us -> 96.8 us
    ppermute x18, starting transfers between devices: 18.4 us -> 11.9 us  [near_swap(): return lax.ppermute(value, 'dp', self.shift(self.near, 1))]
    unnamed x142 -> x140, local copies, waits for them, and re-layouts: 8.97 us -> 8.08 us
  transfers between devices with their start and end apart: 79 -> 79, of which waited for: 23 -> 26; matrix products, arithmetic and copies ran while one was open for 14% -> 12% of each run, Pallas kernels for 27% -> 27%
where the time goes in v4:
time: 358 us; the launch traced here: 357 us
  waiting for transfers between devices  101 us (28%)
  starting transfers between devices  96.8 us (27%)
  Pallas kernels  96.8 us (27%)
  other arithmetic  31.5 us (9%)
  local copies, waits for them, and re-layouts  26.1 us (7%)
  between operations  4.5 us (1%)
    pallas_call x15, Pallas kernels, call(): pl.pallas_call(kernel, name=name, out_shape=[jax.ShapeDtypeStruct(shape,...  96.8 us
    ppermute x16, waiting for transfers between devices, deliver(): lax.ppermute(parts[k], 'dp', self.shift(dim, k))  45.5 us
    ppermute x21, waiting for transfers between devices, fetch(): lax.ppermute(array, 'dp', self.shift(dim, -k))  39.1 us
    ppermute x21, starting transfers between devices, fetch(): lax.ppermute(array, 'dp', self.shift(dim, -k))  39.1 us
    ppermute x24, starting transfers between devices, swap(): return lax.ppermute(value, 'mp', swap_pairs)  24.1 us
    ppermute x16, starting transfers between devices, deliver(): lax.ppermute(parts[k], 'dp', self.shift(dim, k))  21.8 us
    ppermute x18, waiting for transfers between devices, near_swap(): return lax.ppermute(value, 'dp', self.shift(self.near, 1))  12.7 us
    ppermute x18, starting transfers between devices, near_swap(): return lax.ppermute(value, 'dp', self.shift(self.near, 1))  11.9 us
  transfers between devices with their start and end apart: 79, of which 26 were waited for; matrix products, arithmetic and copies ran while one was open for 12% of the time, Pallas kernels for 27%

profile of v4, /device:TPU:1, one launch (start us, length us, event | category | flops | bytes accessed | tf_op | source)
XLA Modules:
  0.0 357.0 jit_solution(7510365377446622838)
XLA Ops:
  4.1 2.1 collective-permute-start
  8.8 2.2 fusion.spread_ref.refs_6_
  16.6 2.3 collective-permute-start.2
  26.4 10.5 %average_forward.1 = (f32[128,1024]{1,0:T(8,128)}, f32[128,1024]{1,0:T(8,128)}, bf16[128,2048]{1,0:T(8,128)(2,1)}, bf16[128,1024]{1,0:T(8,128)(2,1)}, f32[128,8,128]{2,1,0:T(8,128)}, /*index=5*/f32[1,1024]{1,0:T(1,128)}) custom-call(s32[7]{0:T(128)} %stack.131.place_ref, bf16[128,1024]{1,0:T(8,128)(2,1)} %dynamic-slice_bitcast_fusion.5.x_ref, ...), custom_call_target="tpu_custom_call" | custom-call | flops 1 | bytes 1 | tf_op jit(solution)/shard_map/average_forward/pallas_call | solution.py:236
  40.5 6.6 %collective-permute-start.11 = (bf16[2,64,1024]{2,1,0:T(8,128)(2,1)S(1)}, bf16[2,64,1024]{2,1,0:T(8,128)(2,1)S(1)}, u32[]{:S(2)}, u32[]{:S(2)}) collective-permute-start(bf16[2,64,1024]{2,1,0:T(8,128)(2,1)S(1)} %pad_maximum_fusion.9), channel_id=1, source_target_pairs={{0,8},{2,10},{4,12},{6,14},{8,16},{10,18},{12,20},{14,22},{16,24},... | collective-permute-start | bytes 786440 | tf_op jit(solution)/shard_map/ppermute | solution.py:73
  47.1 2.1 collective-permute-start.9
  52.0 12.8 %collective-permute-done.10 = bf16[2,64,1024]{2,1,0:T(8,128)(2,1)S(1)} collective-permute-done((bf16[2,64,1024]{2,1,0:T(8,128)(2,1)S(1)}, bf16[2,64,1024]{2,1,0:T(8,128)(2,1)S(1)}, u32[]{:S(2)}, u32[]{:S(2)}) %collective-permute-start.10) | collective-permute-done | bytes 262176 | tf_op jit(solution)/shard_map/ppermute | solution.py:73
  69.3 6.6 %collective-permute-start.15 = (bf16[2,64,1024]{2,1,0:T(8,128)(2,1)}, bf16[2,64,1024]{2,1,0:T(8,128)(2,1)}, u32[]{:S(2)}, u32[]{:S(2)}) collective-permute-start(bf16[2,64,1024]{2,1,0:T(8,128)(2,1)} %pad_maximum_fusion.10), channel_id=1, source_target_pairs={{0,8},{2,10},{4,12},{6,14},{8,16},{10,18},{12,20},{14,22},{16,24},... | collective-permute-start | bytes 786440 | tf_op jit(solution)/shard_map/ppermute | solution.py:73
  75.9 2.2 collective-permute-start.13
  80.3 6.2 %attention_forward.1 = (f32[512,512]{1,0:T(8,128)}, bf16[512,512]{1,0:T(8,128)(2,1)}, f32[128,512]{1,0:T(8,128)}, f32[128,512]{1,0:T(8,128)}, bf16[256,512]{1,0:...) custom-call(s32[7]{0:T(128)} %stack.131.place_ref, ...), custom_call_target="tpu_custom_call" | custom-call | flops 1 | bytes 1 | tf_op jit(solution)/shard_map/attention_forward/pallas_call | solution.py:236
  86.6 7.3 %collective-permute-done.14 = bf16[2,64,1024]{2,1,0:T(8,128)(2,1)} collective-permute-done((bf16[2,64,1024]{2,1,0:T(8,128)(2,1)}, bf16[2,64,1024]{2,1,0:T(8,128)(2,1)}, u32[]{:S(2)}, u32[]{:S(2)}) %collective-permute-start.14) | collective-permute-done | bytes 262176 | tf_op jit(solution)/shard_map/ppermute | solution.py:73
  95.5 5.9 %collective-permute-start.20 = (bf16[2,64,1024]{2,1,0:T(8,128)(2,1)S(1)}, bf16[2,64,1024]{2,1,0:T(8,128)(2,1)}, u32[]{:S(2)}, u32[]{:S(2)}) collective-permute-start(bf16[2,64,1024]{2,1,0:T(8,128)(2,1)S(1)} %copy-done.34), channel_id=1, source_target_pairs={{0,8},{2,10},{4,12},{6,14},{8,16},{10,18},{12,20},{14,22},{16,24},... | collective-permute-start | bytes 786440 | tf_op jit(solution)/shard_map/ppermute | solution.py:73
  104.4 5.0 %reset_and_mix.1 = (f32[512,512]{1,0:T(8,128)}, bf16[512,512]{1,0:T(8,128)(2,1)}, f32[256,1024]{1,0:T(8,128)}, bf16[256,1024]{1,0:T(8,128)(2,1)}) custom-call(bf16[128,2048]{1,0:T(8,128)(2,1)} %get-tuple-element.166.p0.refs_0_, bf16[128,2048]{1,0:T(8,128)(2,1)} %copy-done.7, bf16[128,2048]{1,0:T(8,128)(2,1)} %copy-done.8, bf16[128,2048]{1,0:T(8,128)(2,1)} %copy-done.9, ...), custom_call_target="tpu_custom_call" | custom-call | flops 1 | bytes 1 | tf_op jit(solution)/shard_map/reset_and_mix/pallas_call | solution.py:236
  109.4 11.8 %collective-permute-done.19 = bf16[2,64,1024]{2,1,0:T(8,128)(2,1)} collective-permute-done((bf16[2,64,1024]{2,1,0:T(8,128)(2,1)S(1)}, bf16[2,64,1024]{2,1,0:T(8,128)(2,1)}, u32[]{:S(2)}, u32[]{:S(2)}) %collective-permute-start.19) | collective-permute-done | bytes 262176 | tf_op jit(solution)/shard_map/ppermute | solution.py:73
  128.5 4.5 %collective-permute-done.24.near_ref = bf16[128,1024]{1,0:T(8,128)(2,1)S(1)} collective-permute-done((bf16[128,1024]{1,0:T(8,128)(2,1)S(1)}, bf16[128,1024]{1,0:T(8,128)(2,1)S(1)}, u32[]{:S(2)}, u32[]{:S(2)}) %collective-permute-start.24) | collective-permute-done | bytes 262176 | tf_op jit(solution)/shard_map/ppermute | solution.py:85
  133.7 4.9 %hidden_and_norm.1 = (f32[128,1024]{1,0:T(8,128)}, f32[128,1024]{1,0:T(8,128)}, f32[128,1024]{1,0:T(8,128)}, f32[128,1024]{1,0:T(8,128)}, f32[128,1]{1,0:T(8,128)}, /*index=5*/bf16[128,1024]{1,0:T(8,128)(2,1)}) custom-call(s32[7]{0:T(128)} %stack.131.place_ref, bf16[128,1024]{1,0:T(8,128)(2,1)} %dynamic-slice_bitcast_fusion.5.x_ref, ...), custom_call_target="tpu_custom_call" | custom-call | flops 1 | bytes 1 | tf_op jit(solution)/shard_map/hidden_and_norm/pallas_call | solution.py:236
  141.0 4.6 %collective-permute-done.27.refs_1_ = bf16[128,1024]{1,0:T(8,128)(2,1)S(1)} collective-permute-done((bf16[128,1024]{1,0:T(8,128)(2,1)}, bf16[128,1024]{1,0:T(8,128)(2,1)S(1)}, u32[]{:S(2)}, u32[]{:S(2)}) %collective-permute-start.27) | collective-permute-done | bytes 262176 | tf_op jit(solution)/shard_map/ppermute | solution.py:85
  145.6 2.1 collective-permute-start.29
  149.5 6.2 %feed_forward.2 = (bf16[512,512]{1,0:T(8,128)(2,1)}, bf16[512,512]{1,0:T(8,128)(2,1)}, f32[1,512]{1,0:T(1,128)}, f32[512,1024]{1,0:T(8,128)}, f32[512,1024]{1,0:T(8,128)}) custom-call(bf16[128,1024]{1,0:T(8,128)(2,1)} %get-tuple-element.191.refs_0_, bf16[128,1024]{1,0:T(8,128)(2,1)} %copy-done.17, bf16[128,1024]{1,0:T(8,128)(2,1)} %copy-done.20, ...), custom_call_target="tpu_custom_call" | custom-call | flops 1 | bytes 1 | tf_op jit(solution)/shard_map/feed_forward/pallas_call | solution.py:236
  155.7 4.2 %feed_forward_weights.2 = (bf16[512,1024]{1,0:T(8,128)(2,1)}, bf16[512,1024]{1,0:T(8,128)(2,1)}) custom-call(bf16[128,1024]{1,0:T(8,128)(2,1)} %get-tuple-element.191.refs_0_, bf16[128,1024]{1,0:T(8,128)(2,1)} %copy-done.17, bf16[128,1024]{1,0:T(8,128)(2,1)} %copy-done.20, bf16[128,1024]{1,0:T(8,128)(2,1)} %copy-done.21, ...), custom_call_target="tpu_custom_call" | custom-call | flops 1 | bytes 1 | tf_op jit(solution)/shard_map/feed_forward_weights/pallas_call | solution.py:236
  161.2 7.1 %feed_forward.3 = (bf16[512,512]{1,0:T(8,128)(2,1)}, bf16[512,512]{1,0:T(8,128)(2,1)}, f32[1,512]{1,0:T(1,128)}, f32[256,1024]{1,0:T(8,128)}, bf16[256,1024]{1,0...) custom-call(bf16[128,1024]{1,0:T(8,128)(2,1)} %get-tuple-element.191.refs_0_, ...), custom_call_target="tpu_custom_call" | custom-call | flops 1 | bytes 1 | tf_op jit(solution)/shard_map/feed_forward/pallas_call | solution.py:236
  172.4 4.2 %feed_forward_weights.3 = (bf16[512,1024]{1,0:T(8,128)(2,1)}, bf16[512,1024]{1,0:T(8,128)(2,1)}) custom-call(bf16[128,1024]{1,0:T(8,128)(2,1)} %get-tuple-element.191.refs_0_, bf16[128,1024]{1,0:T(8,128)(2,1)} %copy-done.17, bf16[128,1024]{1,0:T(8,128)(2,1)} %copy-done.20, bf16[128,1024]{1,0:T(8,128)(2,1)} %copy-done.21, ...), custom_call_target="tpu_custom_call" | custom-call | flops 1 | bytes 1 | tf_op jit(solution)/shard_map/feed_forward_weights/pallas_call | solution.py:236
  176.6 3.2 collective-permute-done.35.near_ref
  180.5 5.3 %blend_backward.1 = (f32[128,1024]{1,0:T(8,128)}, bf16[128,2048]{1,0:T(8,128)(2,1)}, f32[3,1024]{1,0:T(4,128)}) custom-call(s32[7]{0:T(128)} %stack.131.place_ref, bf16[128,1024]{1,0:T(8,128)(2,1)} %dynamic-slice_bitcast_fusion.5.x_ref, bf16[128,1024]{1,0:T(8,128)(2,1)} %dynamic-slice_bitcast_fusion.4.seed_ref, f32[256,1024]{1,0:T(8,128)} %get-tuple-element.206.kept_ref, ...), custom_call_target="tpu_custom_call" | custom-call | flops 1 | bytes 1 | tf_op jit(solution)/shard_map/blend_backward/pallas_call | solution.py:236
  188.9 5.8 %collective-permute-start.36 = (bf16[2,64,1024]{2,1,0:T(8,128)(2,1)S(1)}, bf16[2,64,1024]{2,1,0:T(8,128)(2,1)S(1)}, u32[]{:S(2)}, u32[]{:S(2)}) collective-permute-start(bf16[2,64,1024]{2,1,0:T(8,128)(2,1)S(1)} %get-tuple-element.302), channel_id=1, source_target_pairs={{0,8},{2,10},{4,12},{6,14},{8,16},{10,18},{12,20},{14,22},{16,24},... | collective-permute-start | bytes 786440 | tf_op jit(solution)/shard_map/ppermute | solution.py:78
  195.9 4.1 %collective-permute-done.36 = bf16[2,64,1024]{2,1,0:T(8,128)(2,1)S(1)} collective-permute-done((bf16[2,64,1024]{2,1,0:T(8,128)(2,1)S(1)}, bf16[2,64,1024]{2,1,0:T(8,128)(2,1)S(1)}, u32[]{:S(2)}, u32[]{:S(2)}) %collective-permute-start.36) | collective-permute-done | bytes 262176 | tf_op jit(solution)/shard_map/ppermute | solution.py:78
  199.9 4.0 %collective-permute-start.49 = (bf16[256,1024]{1,0:T(8,128)(2,1)}, bf16[256,1024]{1,0:T(8,128)(2,1)S(1)}, u32[]{:S(2)}, u32[]{:S(2)}) collective-permute-start(bf16[256,1024]{1,0:T(8,128)(2,1)} %get-tuple-element.248), channel_id=1, source_target_pairs={{0,1},{1,0},{2,3},{3,2},{4,5},{5,4},{6,7},{7,6},{8,9},{9,8},{10,11... | collective-permute-start | bytes 1572872 | tf_op jit(solution)/shard_map/ppermute | solution.py:765
  203.9 3.4 collective-permute-done.38
  209.0 9.5 %collective-permute-done.37 = bf16[2,64,1024]{2,1,0:T(8,128)(2,1)} collective-permute-done((bf16[2,64,1024]{2,1,0:T(8,128)(2,1)}, bf16[2,64,1024]{2,1,0:T(8,128)(2,1)}, u32[]{:S(2)}, u32[]{:S(2)}) %collective-permute-start.37) | collective-permute-done | bytes 262176 | tf_op jit(solution)/shard_map/ppermute | solution.py:78
  218.5 2.0 fusion.10
  220.5 2.0 add_convert_fusion.1
  223.6 3.3 collective-permute-start.48
  229.0 5.6 %attention_backward.1 = (bf16[512,512]{1,0:T(8,128)(2,1)}, bf16[512,512]{1,0:T(8,128)(2,1)}, f32[256,128]{1,0:T(8,128)}, f32[256,128]{1,0:T(8,128)}, f32[2,512]{1,0:T(2,128)}) custom-call(bf16[128,2048]{1,0:T(8,128)(2,1)} %get-tuple-element.217.h0.refs_4_.refs_0_, bf16[128,2048]{1,0:T(8,128)(2,1)} %copy-done.12, bf16[128,2048]{1,0:T(8,128)(2,1)} %copy-done.13, ...), custom_call_target="tpu_custom_call" | custom-call | flops 1 | bytes 1 | tf_op jit(solution)/shard_map/attention_backward/pallas_call | solution.py:236
  235.9 7.3 %input_backward.1 = (bf16[512,512]{1,0:T(8,128)(2,1)}, f32[256,2048]{1,0:T(8,128)}, bf16[256,512]{1,0:T(8,128)(2,1)}, bf16[256,512]{1,0:T(8,128)(2,1)}, bf16[256...) custom-call(s32[7]{0:T(128)} %stack.131.place_ref, bf16[128,2048]{1,0:T(8,128)(2,1)} %get-tuple-element.217.h0.refs_4_.refs_0_, ...), custom_call_target="tpu_custom_call" | custom-call | flops 1 | bytes 1 | tf_op jit(solution)/shard_map/input_backward/pallas_call | solution.py:236
  243.2 4.8 %reset_weights.1 = (bf16[512,1024]{1,0:T(8,128)(2,1)}, bf16[512,1024]{1,0:T(8,128)(2,1)}) custom-call(bf16[128,2048]{1,0:T(8,128)(2,1)} %get-tuple-element.166.p0.refs_0_, bf16[128,2048]{1,0:T(8,128)(2,1)} %copy-done.7, bf16[128,2048]{1,0:T(8,128)(2,1)} %copy-done.8, bf16[128,2048]{1,0:T(8,128)(2,1)} %copy-done.9, ...), custom_call_target="tpu_custom_call" | custom-call | flops 1 | bytes 1 | tf_op jit(solution)/shard_map/reset_weights/pallas_call | solution.py:236
  249.3 2.1 fusion.8
  258.2 2.0 scores_backward.1
  260.2 4.6 %value_weights.1 = (bf16[512,1152]{1,0:T(8,128)(2,1)}, bf16[512,1152]{1,0:T(8,128)(2,1)}) custom-call(bf16[128,2048]{1,0:T(8,128)(2,1)} %get-tuple-element.166.p0.refs_0_, bf16[128,2048]{1,0:T(8,128)(2,1)} %copy-done.7, bf16[128,2048]{1,0:T(8,128)(2,1)} %copy-done.8, bf16[128,2048]{1,0:T(8,128)(2,1)} %copy-done.9, ...), custom_call_target="tpu_custom_call" | custom-call | flops 1 | bytes 1 | tf_op jit(solution)/shard_map/value_weights/pallas_call | solution.py:236
  264.8 8.4 %collective-permute-done.43 = bf16[4,2,64,1024]{3,2,1,0:T(8,128)(2,1)} collective-permute-done((bf16[4,2,64,1024]{3,2,1,0:T(8,128)(2,1)}, bf16[4,2,64,1024]{3,2,1,0:T(8,128)(2,1)}, u32[]{:S(2)}, u32[]{:S(2)}) %collective-permute-start.43) | collective-permute-done | bytes 1048608 | tf_op jit(solution)/shard_map/ppermute | solution.py:78
  278.2 2.6 collective-permute-start.58
  283.5 18.9 %average_backward.1 = (bf16[128,1024]{1,0:T(8,128)(2,1)}, bf16[128,1024]{1,0:T(8,128)(2,1)}, f32[24,1024]{1,0:T(8,128)}, f32[24,1024]{1,0:T(8,128)}) custom-call(s32[7]{0:T(128)} %stack.131.place_ref, bf16[128,1024]{1,0:T(8,128)(2,1)} %dynamic-slice_bitcast_fusion.5.x_ref, f32[1,1024]{1,0:T(1,128)} %bitcast.235, f32[1,1024]{1,0:T(1,128)} %bitcast.237, ...), custom_call_target="tpu_custom_call" | custom-call | flops 1 | bytes 1 | tf_op jit(solution)/shard_map/average_backward/pallas_call | solution.py:236
  309.2 3.3 collective-permute-start.72
  316.4 2.3 collective-permute-done.64
  319.4 4.7 %collective-permute-done.72 = bf16[2,64,1152]{2,1,0:T(8,128)(2,1)S(1)} collective-permute-done((bf16[2,64,1152]{2,1,0:T(8,128)(2,1)S(1)}, bf16[2,64,1152]{2,1,0:T(8,128)(2,1)S(1)}, u32[]{:S(2)}, u32[]{:S(2)}) %collective-permute-start.72) | collective-permute-done | bytes 294944 | tf_op jit(solution)/shard_map/ppermute | solution.py:78
  324.1 14.0 %collective-permute-done.71 = bf16[2,64,1152]{2,1,0:T(8,128)(2,1)S(1)} collective-permute-done((bf16[2,64,1152]{2,1,0:T(8,128)(2,1)S(1)}, bf16[2,64,1152]{2,1,0:T(8,128)(2,1)S(1)}, u32[]{:S(2)}, u32[]{:S(2)}) %collective-permute-start.71) | collective-permute-done | bytes 294944 | tf_op jit(solution)/shard_map/ppermute | solution.py:78
  340.0 3.3 collective-permute-start.67
  344.1 2.0 collective-permute-start.75
  347.8 2.7 collective-permute-start.69
  (372 shorter events, 100.3 us)
Async XLA Ops:
  15.3 21.7 %collective-permute-start.3 = (bf16[2,64,1152]{2,1,0:T(8,128)(2,1)S(1)}, bf16[2,64,1152]{2,1,0:T(8,128)(2,1)S(1)}, u32[]{:S(2)}, u32[]{:S(2)}) collective-permute-start(bf16[2,64,1152]{2,1,0:T(8,128)(2,1)S(1)} %pad_maximum_fusion.8), channel_id=1, source_target_pairs={{0,8},{2,10},{4,12},{6,14},{8,16},{10,18},{12,20},{14,22},{16,24},... | collective-permute-start | bytes 884744 | tf_op jit(solution)/shard_map/ppermute | solution.py:73
  16.6 22.2 %collective-permute-start.2 = (bf16[2,64,1152]{2,1,0:T(8,128)(2,1)S(1)}, bf16[2,64,1152]{2,1,0:T(8,128)(2,1)S(1)}, u32[]{:S(2)}, u32[]{:S(2)}) collective-permute-start(bf16[2,64,1152]{2,1,0:T(8,128)(2,1)S(1)} %pad_maximum_fusion.8), channel_id=1, source_target_pairs={{0,16},{2,18},{4,20},{6,22},{8,24},{10,26},{12,28},{14,30},{16,0},... | collective-permute-start | bytes 884744 | tf_op jit(solution)/shard_map/ppermute | solution.py:73
  18.9 19.9 %collective-permute-start.1 = (bf16[2,64,1152]{2,1,0:T(8,128)(2,1)S(1)}, bf16[2,64,1152]{2,1,0:T(8,128)(2,1)S(1)}, u32[]{:S(2)}, u32[]{:S(2)}) collective-permute-start(bf16[2,64,1152]{2,1,0:T(8,128)(2,1)S(1)} %pad_maximum_fusion.8), channel_id=1, source_target_pairs={{0,24},{2,26},{4,28},{6,30},{8,0},{10,2},{12,4},{14,6},{16,8},{18,... | collective-permute-start | bytes 884744 | tf_op jit(solution)/shard_map/ppermute | solution.py:73
  20.3 18.7 %collective-permute-start.4 = (bf16[64,3072]{1,0:T(8,128)(2,1)S(1)}, bf16[64,3072]{1,0:T(8,128)(2,1)S(1)}, u32[]{:S(2)}, u32[]{:S(2)}) collective-permute-start(bf16[64,3072]{1,0:T(8,128)(2,1)S(1)} %bitcast_dynamic-update-slice_fusion), channel_id=1, source_target_pairs={{0,2},{2,0},{4,6},{6,4},{8,10},{10,8},{12,14},{14,12},{16,18},{18,... | collective-permute-start | bytes 1179656 | tf_op jit(solution)/shard_map/ppermute | solution.py:85
  39.2 27.0 %collective-permute-start.12 = (bf16[4,2,64,1152]{3,2,1,0:T(8,128)(2,1)S(1)}, bf16[4,2,64,1152]{3,2,1,0:T(8,128)(2,1)S(1)}, u32[]{:S(2)}, u32[]{:S(2)}) collective-permute-start(bf16[4,2,64,1152]{3,2,1,0:T(8,128)(2,1)S(1)} %pad_maximum_fusion), channel_id=1, source_target_pairs={{0,4},{2,6},{4,0},{6,2},{8,12},{10,14},{12,8},{14,10},{16,20},{18,... | collective-permute-start | bytes 3538952 | tf_op jit(solution)/shard_map/ppermute | solution.py:73
  40.5 11.5 %collective-permute-start.11 = (bf16[2,64,1024]{2,1,0:T(8,128)(2,1)S(1)}, bf16[2,64,1024]{2,1,0:T(8,128)(2,1)S(1)}, u32[]{:S(2)}, u32[]{:S(2)}) collective-permute-start(bf16[2,64,1024]{2,1,0:T(8,128)(2,1)S(1)} %pad_maximum_fusion.9), channel_id=1, source_target_pairs={{0,8},{2,10},{4,12},{6,14},{8,16},{10,18},{12,20},{14,22},{16,24},... | collective-permute-start | bytes 786440 | tf_op jit(solution)/shard_map/ppermute | solution.py:73
  47.1 17.7 %collective-permute-start.10 = (bf16[2,64,1024]{2,1,0:T(8,128)(2,1)S(1)}, bf16[2,64,1024]{2,1,0:T(8,128)(2,1)S(1)}, u32[]{:S(2)}, u32[]{:S(2)}) collective-permute-start(bf16[2,64,1024]{2,1,0:T(8,128)(2,1)S(1)} %pad_maximum_fusion.9), channel_id=1, source_target_pairs={{0,16},{2,18},{4,20},{6,22},{8,24},{10,26},{12,28},{14,30},{16,0},... | collective-permute-start | bytes 786440 | tf_op jit(solution)/shard_map/ppermute | solution.py:73
  47.1 17.7 %collective-permute-start.9 = (bf16[2,64,1024]{2,1,0:T(8,128)(2,1)S(1)}, bf16[2,64,1024]{2,1,0:T(8,128)(2,1)S(1)}, u32[]{:S(2)}, u32[]{:S(2)}) collective-permute-start(bf16[2,64,1024]{2,1,0:T(8,128)(2,1)S(1)} %pad_maximum_fusion.9), channel_id=1, source_target_pairs={{0,24},{2,26},{4,28},{6,30},{8,0},{10,2},{12,4},{14,6},{16,8},{18,... | collective-permute-start | bytes 786440 | tf_op jit(solution)/shard_map/ppermute | solution.py:73
  49.2 20.0 %collective-permute-start.6 = (bf16[128,2048]{1,0:T(8,128)(2,1)S(1)}, bf16[128,2048]{1,0:T(8,128)(2,1)S(1)}, u32[]{:S(2)}, u32[]{:S(2)}) collective-permute-start(bf16[128,2048]{1,0:T(8,128)(2,1)S(1)} %copy-done.6), channel_id=1, source_target_pairs={{0,2},{2,0},{4,6},{6,4},{8,10},{10,8},{12,14},{14,12},{16,18},{18,... | collective-permute-start | bytes 1572872 | tf_op jit(solution)/shard_map/ppermute | solution.py:85
  66.2 29.0 %collective-permute-start.16 = (bf16[4,2,64,1024]{3,2,1,0:T(8,128)(2,1)S(1)}, bf16[4,2,64,1024]{3,2,1,0:T(8,128)(2,1)S(1)}, u32[]{:S(2)}, u32[]{:S(2)}) collective-permute-start(bf16[4,2,64,1024]{3,2,1,0:T(8,128)(2,1)S(1)} %pad_maximum_fusion.1), channel_id=1, source_target_pairs={{0,4},{2,6},{4,0},{6,2},{8,12},{10,14},{12,8},{14,10},{16,20},{18,... | collective-permute-start | bytes 3145736 | tf_op jit(solution)/shard_map/ppermute | solution.py:73
  69.2 8.9 %collective-permute-start.8 = (bf16[128,2048]{1,0:T(8,128)(2,1)S(1)}, bf16[128,2048]{1,0:T(8,128)(2,1)S(1)}, u32[]{:S(2)}, u32[]{:S(2)}) collective-permute-start(bf16[128,2048]{1,0:T(8,128)(2,1)S(1)} %collective-permute-done.6.p1.refs_1_), channel_id=1, source_target_pairs={{0,1},{1,0},{2,3},{3,2},{4,5},{5,4},{6,7},{7,6},{8,9},{9,8},{10,11... | collective-permute-start | bytes 1572872 | tf_op jit(solution)/shard_map/ppermute | solution.py:765
  69.3 17.3 %collective-permute-start.15 = (bf16[2,64,1024]{2,1,0:T(8,128)(2,1)}, bf16[2,64,1024]{2,1,0:T(8,128)(2,1)}, u32[]{:S(2)}, u32[]{:S(2)}) collective-permute-start(bf16[2,64,1024]{2,1,0:T(8,128)(2,1)} %pad_maximum_fusion.10), channel_id=1, source_target_pairs={{0,8},{2,10},{4,12},{6,14},{8,16},{10,18},{12,20},{14,22},{16,24},... | collective-permute-start | bytes 786440 | tf_op jit(solution)/shard_map/ppermute | solution.py:73
  75.9 18.0 %collective-permute-start.14 = (bf16[2,64,1024]{2,1,0:T(8,128)(2,1)}, bf16[2,64,1024]{2,1,0:T(8,128)(2,1)}, u32[]{:S(2)}, u32[]{:S(2)}) collective-permute-start(bf16[2,64,1024]{2,1,0:T(8,128)(2,1)} %pad_maximum_fusion.10), channel_id=1, source_target_pairs={{0,16},{2,18},{4,20},{6,22},{8,24},{10,26},{12,28},{14,30},{16,0},... | collective-permute-start | bytes 786440 | tf_op jit(solution)/shard_map/ppermute | solution.py:73
  75.9 18.0 %collective-permute-start.13 = (bf16[2,64,1024]{2,1,0:T(8,128)(2,1)}, bf16[2,64,1024]{2,1,0:T(8,128)(2,1)}, u32[]{:S(2)}, u32[]{:S(2)}) collective-permute-start(bf16[2,64,1024]{2,1,0:T(8,128)(2,1)} %pad_maximum_fusion.10), channel_id=1, source_target_pairs={{0,24},{2,26},{4,28},{6,30},{8,0},{10,2},{12,4},{14,6},{16,8},{18,... | collective-permute-start | bytes 786440 | tf_op jit(solution)/shard_map/ppermute | solution.py:73
  78.1 17.1 %collective-permute-start.17 = (bf16[128,1024]{1,0:T(8,128)(2,1)}, bf16[128,1024]{1,0:T(8,128)(2,1)}, u32[]{:S(2)}, u32[]{:S(2)}) collective-permute-start(bf16[128,1024]{1,0:T(8,128)(2,1)} %get-tuple-element.177.refs_4_), channel_id=1, source_target_pairs={{0,2},{2,0},{4,6},{6,4},{8,10},{10,8},{12,14},{14,12},{16,18},{18,... | collective-permute-start | bytes 786440 | tf_op jit(solution)/shard_map/ppermute | solution.py:85
  95.2 27.2 %collective-permute-start.21 = (bf16[4,2,64,1024]{3,2,1,0:T(8,128)(2,1)S(1)}, bf16[4,2,64,1024]{3,2,1,0:T(8,128)(2,1)}, u32[]{:S(2)}, u32[]{:S(2)}) collective-permute-start(bf16[4,2,64,1024]{3,2,1,0:T(8,128)(2,1)S(1)} %pad_maximum_fusion.2), channel_id=1, source_target_pairs={{0,4},{2,6},{4,0},{6,2},{8,12},{10,14},{12,8},{14,10},{16,20},{18,... | collective-permute-start | bytes 3145736 | tf_op jit(solution)/shard_map/ppermute | solution.py:73
  95.5 13.9 %collective-permute-start.20 = (bf16[2,64,1024]{2,1,0:T(8,128)(2,1)S(1)}, bf16[2,64,1024]{2,1,0:T(8,128)(2,1)}, u32[]{:S(2)}, u32[]{:S(2)}) collective-permute-start(bf16[2,64,1024]{2,1,0:T(8,128)(2,1)S(1)} %copy-done.34), channel_id=1, source_target_pairs={{0,8},{2,10},{4,12},{6,14},{8,16},{10,18},{12,20},{14,22},{16,24},... | collective-permute-start | bytes 786440 | tf_op jit(solution)/shard_map/ppermute | solution.py:73
  101.4 19.8 %collective-permute-start.19 = (bf16[2,64,1024]{2,1,0:T(8,128)(2,1)S(1)}, bf16[2,64,1024]{2,1,0:T(8,128)(2,1)}, u32[]{:S(2)}, u32[]{:S(2)}) collective-permute-start(bf16[2,64,1024]{2,1,0:T(8,128)(2,1)S(1)} %copy-done.34), channel_id=1, source_target_pairs={{0,16},{2,18},{4,20},{6,22},{8,24},{10,26},{12,28},{14,30},{16,0},... | collective-permute-start | bytes 786440 | tf_op jit(solution)/shard_map/ppermute | solution.py:73
  103.4 17.9 %collective-permute-start.18 = (bf16[2,64,1024]{2,1,0:T(8,128)(2,1)S(1)}, bf16[2,64,1024]{2,1,0:T(8,128)(2,1)}, u32[]{:S(2)}, u32[]{:S(2)}) collective-permute-start(bf16[2,64,1024]{2,1,0:T(8,128)(2,1)S(1)} %copy-done.34), channel_id=1, source_target_pairs={{0,24},{2,26},{4,28},{6,30},{8,0},{10,2},{12,4},{14,6},{16,8},{18,... | collective-permute-start | bytes 786440 | tf_op jit(solution)/shard_map/ppermute | solution.py:73
  103.5 19.0 %collective-permute-start.22 = (bf16[256,512]{1,0:T(8,128)(2,1)}, bf16[256,512]{1,0:T(8,128)(2,1)}, u32[]{:S(2)}, u32[]{:S(2)}) collective-permute-start(bf16[256,512]{1,0:T(8,128)(2,1)} %get-tuple-element.185), channel_id=1, source_target_pairs={{0,2},{2,0},{4,6},{6,4},{8,10},{10,8},{12,14},{14,12},{16,18},{18,... | collective-permute-start | bytes 786440 | tf_op jit(solution)/shard_map/ppermute | solution.py:85
  123.2 38.0 %collective-permute-start.33 = (bf16[4,2,64,1024]{3,2,1,0:T(8,128)(2,1)S(1)}, bf16[4,2,64,1024]{3,2,1,0:T(8,128)(2,1)}, u32[]{:S(2)}, u32[]{:S(2)}) collective-permute-start(bf16[4,2,64,1024]{3,2,1,0:T(8,128)(2,1)S(1)} %pad_maximum_fusion.3), channel_id=1, source_target_pairs={{0,4},{2,6},{4,0},{6,2},{8,12},{10,14},{12,8},{14,10},{16,20},{18,... | collective-permute-start | bytes 3145736 | tf_op jit(solution)/shard_map/ppermute | solution.py:73
  138.9 9.3 %collective-permute-start.30 = (bf16[128,1024]{1,0:T(8,128)(2,1)}, bf16[128,1024]{1,0:T(8,128)(2,1)S(1)}, u32[]{:S(2)}, u32[]{:S(2)}) collective-permute-start(bf16[128,1024]{1,0:T(8,128)(2,1)} %get-tuple-element.177.refs_4_), channel_id=1, source_target_pairs={{0,1},{1,0},{2,3},{3,2},{4,5},{5,4},{6,7},{7,6},{8,9},{9,8},{10,11... | collective-permute-start | bytes 786440 | tf_op jit(solution)/shard_map/ppermute | solution.py:765
  159.9 25.9 %collective-permute-start.32 = (bf16[4,2,64,1024]{3,2,1,0:T(8,128)(2,1)}, bf16[4,2,64,1024]{3,2,1,0:T(8,128)(2,1)}, u32[]{:S(2)}, u32[]{:S(2)}) collective-permute-start(bf16[4,2,64,1024]{3,2,1,0:T(8,128)(2,1)} %bitcast.268), channel_id=1, source_target_pairs={{0,4},{2,6},{4,0},{6,2},{8,12},{10,14},{12,8},{14,10},{16,20},{18,... | collective-permute-start | bytes 3145736 | tf_op jit(solution)/shard_map/ppermute | solution.py:78
  187.5 33.1 %collective-permute-start.39 = (bf16[4,2,64,1024]{3,2,1,0:T(8,128)(2,1)}, bf16[4,2,64,1024]{3,2,1,0:T(8,128)(2,1)}, u32[]{:S(2)}, u32[]{:S(2)}) collective-permute-start(bf16[4,2,64,1024]{3,2,1,0:T(8,128)(2,1)} %bitcast.62), channel_id=1, source_target_pairs={{0,4},{2,6},{4,0},{6,2},{8,12},{10,14},{12,8},{14,10},{16,20},{18,... | collective-permute-start | bytes 3145736 | tf_op jit(solution)/shard_map/ppermute | solution.py:78
  187.7 21.3 %collective-permute-start.40 = (bf16[128,2048]{1,0:T(8,128)(2,1)S(1)}, bf16[128,2048]{1,0:T(8,128)(2,1)S(1)}, u32[]{:S(2)}, u32[]{:S(2)}) collective-permute-start(bf16[128,2048]{1,0:T(8,128)(2,1)S(1)} %copy-done.11), channel_id=1, source_target_pairs={{0,2},{2,0},{4,6},{6,4},{8,10},{10,8},{12,14},{14,12},{16,18},{18,... | collective-permute-start | bytes 1572872 | tf_op jit(solution)/shard_map/ppermute | solution.py:85
  188.9 11.0 %collective-permute-start.36 = (bf16[2,64,1024]{2,1,0:T(8,128)(2,1)S(1)}, bf16[2,64,1024]{2,1,0:T(8,128)(2,1)S(1)}, u32[]{:S(2)}, u32[]{:S(2)}) collective-permute-start(bf16[2,64,1024]{2,1,0:T(8,128)(2,1)S(1)} %get-tuple-element.302), channel_id=1, source_target_pairs={{0,8},{2,10},{4,12},{6,14},{8,16},{10,18},{12,20},{14,22},{16,24},... | collective-permute-start | bytes 786440 | tf_op jit(solution)/shard_map/ppermute | solution.py:78
  194.7 12.6 %collective-permute-start.38 = (bf16[2,64,1024]{2,1,0:T(8,128)(2,1)S(1)}, bf16[2,64,1024]{2,1,0:T(8,128)(2,1)}, u32[]{:S(2)}, u32[]{:S(2)}) collective-permute-start(bf16[2,64,1024]{2,1,0:T(8,128)(2,1)S(1)} %get-tuple-element.303), channel_id=1, source_target_pairs={{0,24},{2,26},{4,28},{6,30},{8,0},{10,2},{12,4},{14,6},{16,8},{18,... | collective-permute-start | bytes 786440 | tf_op jit(solution)/shard_map/ppermute | solution.py:78
  194.8 23.7 %collective-permute-start.37 = (bf16[2,64,1024]{2,1,0:T(8,128)(2,1)}, bf16[2,64,1024]{2,1,0:T(8,128)(2,1)}, u32[]{:S(2)}, u32[]{:S(2)}) collective-permute-start(bf16[2,64,1024]{2,1,0:T(8,128)(2,1)} %get-tuple-element.304), channel_id=1, source_target_pairs={{0,16},{2,18},{4,20},{6,22},{8,24},{10,26},{12,28},{14,30},{16,0},... | collective-permute-start | bytes 786440 | tf_op jit(solution)/shard_map/ppermute | solution.py:78
  199.9 27.0 %collective-permute-start.49 = (bf16[256,1024]{1,0:T(8,128)(2,1)}, bf16[256,1024]{1,0:T(8,128)(2,1)S(1)}, u32[]{:S(2)}, u32[]{:S(2)}) collective-permute-start(bf16[256,1024]{1,0:T(8,128)(2,1)} %get-tuple-element.248), channel_id=1, source_target_pairs={{0,1},{1,0},{2,3},{3,2},{4,5},{5,4},{6,7},{7,6},{8,9},{9,8},{10,11... | collective-permute-start | bytes 1572872 | tf_op jit(solution)/shard_map/ppermute | solution.py:765
  207.3 15.3 %collective-permute-start.41 = (bf16[128,2048]{1,0:T(8,128)(2,1)S(1)}, bf16[128,2048]{1,0:T(8,128)(2,1)S(1)}, u32[]{:S(2)}, u32[]{:S(2)}) collective-permute-start(bf16[128,2048]{1,0:T(8,128)(2,1)S(1)} %copy-done.11), channel_id=1, source_target_pairs={{0,1},{1,0},{2,3},{3,2},{4,5},{5,4},{6,7},{7,6},{8,9},{9,8},{10,11... | collective-permute-start | bytes 1572872 | tf_op jit(solution)/shard_map/ppermute | solution.py:765
  209.0 13.7 %collective-permute-start.42 = (bf16[128,2048]{1,0:T(8,128)(2,1)S(1)}, bf16[128,2048]{1,0:T(8,128)(2,1)S(1)}, u32[]{:S(2)}, u32[]{:S(2)}) collective-permute-start(bf16[128,2048]{1,0:T(8,128)(2,1)S(1)} %collective-permute-done.40.h1.refs_5_.refs_1_), channel_id=1, source_target_pairs={{0,1},{1,0},{2,3},{3,2},{4,5},{5,4},{6,7},{7,6},{8,9},{9,8},{10,11... | collective-permute-start | bytes 1572872 | tf_op jit(solution)/shard_map/ppermute | solution.py:765
  223.6 24.5 %collective-permute-start.46 = (bf16[2,64,1024]{2,1,0:T(8,128)(2,1)}, bf16[2,64,1024]{2,1,0:T(8,128)(2,1)}, u32[]{:S(2)}, u32[]{:S(2)}) collective-permute-start(bf16[2,64,1024]{2,1,0:T(8,128)(2,1)} %get-tuple-element.299), channel_id=1, source_target_pairs={{0,8},{2,10},{4,12},{6,14},{8,16},{10,18},{12,20},{14,22},{16,24},... | collective-permute-start | bytes 786440 | tf_op jit(solution)/shard_map/ppermute | solution.py:78
  223.6 25.7 %collective-permute-start.48 = (bf16[2,64,1024]{2,1,0:T(8,128)(2,1)}, bf16[2,64,1024]{2,1,0:T(8,128)(2,1)}, u32[]{:S(2)}, u32[]{:S(2)}) collective-permute-start(bf16[2,64,1024]{2,1,0:T(8,128)(2,1)} %get-tuple-element.300), channel_id=1, source_target_pairs={{0,24},{2,26},{4,28},{6,30},{8,0},{10,2},{12,4},{14,6},{16,8},{18,... | collective-permute-start | bytes 786440 | tf_op jit(solution)/shard_map/ppermute | solution.py:78
  226.9 22.4 %collective-permute-start.47 = (bf16[2,64,1024]{2,1,0:T(8,128)(2,1)}, bf16[2,64,1024]{2,1,0:T(8,128)(2,1)}, u32[]{:S(2)}, u32[]{:S(2)}) collective-permute-start(bf16[2,64,1024]{2,1,0:T(8,128)(2,1)} %get-tuple-element.301), channel_id=1, source_target_pairs={{0,16},{2,18},{4,20},{6,22},{8,24},{10,26},{12,28},{14,30},{16,0},... | collective-permute-start | bytes 786440 | tf_op jit(solution)/shard_map/ppermute | solution.py:78
  227.8 23.6 %collective-permute-start.50 = (bf16[128,1024]{1,0:T(8,128)(2,1)}, bf16[128,1024]{1,0:T(8,128)(2,1)S(1)}, u32[]{:S(2)}, u32[]{:S(2)}) collective-permute-start(bf16[128,1024]{1,0:T(8,128)(2,1)} %add_convert_fusion.3), channel_id=1, source_target_pairs={{0,2},{2,0},{4,6},{6,4},{8,10},{10,8},{12,14},{14,12},{16,18},{18,... | collective-permute-start | bytes 786440 | tf_op jit(solution)/shard_map/ppermute | solution.py:85
  234.6 18.3 %collective-permute-start.44 = (f32[256,128]{1,0:T(8,128)}, f32[256,128]{1,0:T(8,128)}, u32[]{:S(2)}, u32[]{:S(2)}) collective-permute-start(f32[256,128]{1,0:T(8,128)} %get-tuple-element.232), channel_id=1, source_target_pairs={{0,1},{1,0},{2,3},{3,2},{4,5},{5,4},{6,7},{7,6},{8,9},{9,8},{10,11... | collective-permute-start | bytes 393224 | tf_op jit(solution)/shard_map/ppermute | solution.py:765
  248.1 25.2 %collective-permute-start.43 = (bf16[4,2,64,1024]{3,2,1,0:T(8,128)(2,1)}, bf16[4,2,64,1024]{3,2,1,0:T(8,128)(2,1)}, u32[]{:S(2)}, u32[]{:S(2)}) collective-permute-start(bf16[4,2,64,1024]{3,2,1,0:T(8,128)(2,1)} %bitcast.267), channel_id=1, source_target_pairs={{0,4},{2,6},{4,0},{6,2},{8,12},{10,14},{12,8},{14,10},{16,20},{18,... | collective-permute-start | bytes 3145736 | tf_op jit(solution)/shard_map/ppermute | solution.py:78
  256.2 18.7 %collective-permute-start.55 = (bf16[128,2048]{1,0:T(8,128)(2,1)}, bf16[128,2048]{1,0:T(8,128)(2,1)}, u32[]{:S(2)}, u32[]{:S(2)}) collective-permute-start(bf16[128,2048]{1,0:T(8,128)(2,1)} %add_convert_fusion.2), channel_id=1, source_target_pairs={{0,2},{2,0},{4,6},{6,4},{8,10},{10,8},{12,14},{14,12},{16,18},{18,... | collective-permute-start | bytes 1572872 | tf_op jit(solution)/shard_map/ppermute | solution.py:85
  274.9 31.0 %collective-permute-start.59 = (bf16[4,2,64,1152]{3,2,1,0:T(8,128)(2,1)}, bf16[4,2,64,1152]{3,2,1,0:T(8,128)(2,1)S(1)}, u32[]{:S(2)}, u32[]{:S(2)}) collective-permute-start(bf16[4,2,64,1152]{3,2,1,0:T(8,128)(2,1)} %bitcast.70), channel_id=1, source_target_pairs={{0,4},{2,6},{4,0},{6,2},{8,12},{10,14},{12,8},{14,10},{16,20},{18,... | collective-permute-start | bytes 3538952 | tf_op jit(solution)/shard_map/ppermute | solution.py:78
  277.5 26.0 %collective-permute-start.56 = (bf16[2,64,1024]{2,1,0:T(8,128)(2,1)}, bf16[2,64,1024]{2,1,0:T(8,128)(2,1)S(1)}, u32[]{:S(2)}, u32[]{:S(2)}) collective-permute-start(bf16[2,64,1024]{2,1,0:T(8,128)(2,1)} %get-tuple-element.296), channel_id=1, source_target_pairs={{0,8},{2,10},{4,12},{6,14},{8,16},{10,18},{12,20},{14,22},{16,24},... | collective-permute-start | bytes 786440 | tf_op jit(solution)/shard_map/ppermute | solution.py:78
  278.2 25.3 %collective-permute-start.58 = (bf16[2,64,1024]{2,1,0:T(8,128)(2,1)}, bf16[2,64,1024]{2,1,0:T(8,128)(2,1)}, u32[]{:S(2)}, u32[]{:S(2)}) collective-permute-start(bf16[2,64,1024]{2,1,0:T(8,128)(2,1)} %get-tuple-element.297), channel_id=1, source_target_pairs={{0,24},{2,26},{4,28},{6,30},{8,0},{10,2},{12,4},{14,6},{16,8},{18,... | collective-permute-start | bytes 786440 | tf_op jit(solution)/shard_map/ppermute | solution.py:78
  280.7 23.9 %collective-permute-start.57 = (bf16[2,64,1024]{2,1,0:T(8,128)(2,1)}, bf16[2,64,1024]{2,1,0:T(8,128)(2,1)}, u32[]{:S(2)}, u32[]{:S(2)}) collective-permute-start(bf16[2,64,1024]{2,1,0:T(8,128)(2,1)} %get-tuple-element.298), channel_id=1, source_target_pairs={{0,16},{2,18},{4,20},{6,22},{8,24},{10,26},{12,28},{14,30},{16,0},... | collective-permute-start | bytes 786440 | tf_op jit(solution)/shard_map/ppermute | solution.py:78
  282.3 20.2 %collective-permute-start.60 = (bf16[64,1024]{1,0:T(8,128)(2,1)}, bf16[64,1024]{1,0:T(8,128)(2,1)}, u32[]{:S(2)}, u32[]{:S(2)}) collective-permute-start(bf16[64,1024]{1,0:T(8,128)(2,1)} %fusion.16), channel_id=1, source_target_pairs={{0,2},{2,0},{4,6},{6,4},{8,10},{10,8},{12,14},{14,12},{16,18},{18,... | collective-permute-start | bytes 393224 | tf_op jit(solution)/shard_map/ppermute | solution.py:85
  308.7 47.1 %collective-permute-start.62 = (bf16[2,128,1024]{2,1,0:T(8,128)(2,1)S(1)}, bf16[2,128,1024]{2,1,0:T(8,128)(2,1)S(1)}, u32[]{:S(2)}, u32[]{:S(2)}) collective-permute-start(bf16[2,128,1024]{2,1,0:T(8,128)(2,1)S(1)} %pad_maximum_fusion.4), channel_id=1, source_target_pairs={{0,1},{1,0},{2,3},{3,2},{4,5},{5,4},{6,7},{7,6},{8,9},{9,8},{10,11... | collective-permute-start | bytes 1572872 | tf_op jit(solution)/shard_map/ppermute | solution.py:765
  309.1 10.3 %collective-permute-start.70 = (bf16[2,64,1152]{2,1,0:T(8,128)(2,1)S(1)}, bf16[2,64,1152]{2,1,0:T(8,128)(2,1)S(1)}, u32[]{:S(2)}, u32[]{:S(2)}) collective-permute-start(bf16[2,64,1152]{2,1,0:T(8,128)(2,1)S(1)} %get-tuple-element.293), channel_id=1, source_target_pairs={{0,8},{2,10},{4,12},{6,14},{8,16},{10,18},{12,20},{14,22},{16,24},... | collective-permute-start | bytes 884744 | tf_op jit(solution)/shard_map/ppermute | solution.py:78
  309.2 14.9 %collective-permute-start.72 = (bf16[2,64,1152]{2,1,0:T(8,128)(2,1)S(1)}, bf16[2,64,1152]{2,1,0:T(8,128)(2,1)S(1)}, u32[]{:S(2)}, u32[]{:S(2)}) collective-permute-start(bf16[2,64,1152]{2,1,0:T(8,128)(2,1)S(1)} %get-tuple-element.294), channel_id=1, source_target_pairs={{0,24},{2,26},{4,28},{6,30},{8,0},{10,2},{12,4},{14,6},{16,8},{18,... | collective-permute-start | bytes 884744 | tf_op jit(solution)/shard_map/ppermute | solution.py:78
  314.3 23.8 %collective-permute-start.71 = (bf16[2,64,1152]{2,1,0:T(8,128)(2,1)S(1)}, bf16[2,64,1152]{2,1,0:T(8,128)(2,1)S(1)}, u32[]{:S(2)}, u32[]{:S(2)}) collective-permute-start(bf16[2,64,1152]{2,1,0:T(8,128)(2,1)S(1)} %get-tuple-element.295), channel_id=1, source_target_pairs={{0,16},{2,18},{4,20},{6,22},{8,24},{10,26},{12,28},{14,30},{16,0},... | collective-permute-start | bytes 884744 | tf_op jit(solution)/shard_map/ppermute | solution.py:78
  318.8 21.1 %collective-permute-start.65 = (f32[28,1024]{1,0:T(8,128)S(1)}, f32[28,1024]{1,0:T(8,128)S(1)}, u32[]{:S(2)}, u32[]{:S(2)}) collective-permute-start(f32[28,1024]{1,0:T(8,128)S(1)} %fusion.50), channel_id=1, source_target_pairs={{0,4},{2,6},{4,0},{6,2},{8,12},{10,14},{12,8},{14,10},{16,20},{18,... | collective-permute-start | bytes 344072 | tf_op jit(solution)/shard_map/ppermute | solution.py:73
  (99 other events, 759.1 us)
